TPU v7x, 32 devices: a whole 2x2x4 slice. The times are simulated.
32 devices in a mesh: samp: 8 (over y, x, core), ctr: 4 (over z).
Axes of the slice: x: 2, y: 2, z: 4, core: 2. Of those that a mesh axis runs over, the one named last changes fastest.
Arguments:
- samples: bfloat16 [16384, 512], P('samp'), may hold values from -6 to 6
- centers: bfloat16 [4096, 512], P('ctr'), may hold values from -6 to 6
Outputs:
- gram_panel: float32 [4, 1024, 512], P('ctr', 'samp')
- chol_panel: float32 [4, 1024, 512], P('ctr', 'samp')
- precond_factor: float32 [512, 512], replicated
All inputs are finite; a program needn't handle non-finite values.
Results may differ from a plain program's by a relative error of at most 0.0003.
Values may be sent and summed in bfloat16 or wider, within the bound.
No kernel may reach another device: no remote copies, remote signals or barrier semaphores. Data moves between devices by JAX's collectives and lax.ppermute only.
A program may use at most 64 MiB of HBM per device.

v0:
```python
import functools
import jax, jax.numpy as jnp
from jax import lax
from jax.experimental import pallas as pl
from jax.experimental.pallas import tpu as pltpu
JITTER=0.01; SHIFT=0.5
B=128
VB=64
HI=lax.Precision.HIGHEST
def mmul(a,b): return jnp.dot(a,b,preferred_element_type=jnp.float32,precision=HI)
def mmul_nt(a,b): return lax.dot_general(a,b,(((1,),(1,)),((),())),preferred_element_type=jnp.float32,precision=HI)
def lanebc(x,c): return jnp.broadcast_to(x[:,c:c+1],(8,B))
def subbc(x,j): return jnp.broadcast_to(x[j:j+1,:],(8,B))

def factor128(r_ref,w_ref,u_ref,m_ref):
    row=lax.broadcasted_iota(jnp.int32,(B,B),0)
    lane=lax.broadcasted_iota(jnp.int32,(B,B),1)
    w_ref[...]=jnp.where(lane==row,1.0,0.0)
    n=VB//8
    for b in range(B//VB):
        base=b*VB
        X=[r_ref[base+8*k:base+8*k+8,:] for k in range(n)]
        Y=[w_ref[base+8*k:base+8*k+8,:] for k in range(n)]
        for i in range(n):
            a=X[i]; w=Y[i]
            g=[];c={m:[] for m in range(i+1,n)}
            for j in range(8):
                g.append(lanebc(a,base+8*i+j))
                for m in range(i+1,n): c[m].append(lanebc(X[m],base+8*i+j))
            for j in range(8):
                rs=lax.rsqrt(subbc(g[j],j))
                q=[None]*8
                lj=g[j]*rs
                for m in range(j+1,8):
                    q[m]=subbc(g[m],j)*rs
                    g[m]=g[m]-lj*q[m]
                ur=subbc(a,j)*rs; wr=subbc(w,j)*rs
                if j<7:
                    a=a-lj*ur; w=w-lj*wr
                k=base+8*i+j
                u_ref[k:k+1,:]=ur[0:1]; m_ref[k:k+1,:]=wr[0:1]
                for m in range(i+1,n):
                    cj=c[m][j]*rs
                    for t in range(j+1,8): c[m][t]=c[m][t]-cj*q[t]
                    X[m]=X[m]-cj*ur; Y[m]=Y[m]-cj*wr
        e=base+VB
        if e<B:
            ub=u_ref[base:e,:]; mb=m_ref[base:e,:]
            ut=ub.T[e:,:]
            z=mmul(ut,jnp.concatenate([ub,mb],axis=1))
            r_ref[e:,:]=r_ref[e:,:]-z[:,:B]
            w_ref[e:,:]=w_ref[e:,:]-z[:,B:]
    u_ref[...]=jnp.where(lane>=row,u_ref[...],0.0)

def kern_init(off_ref,panel_ref,own_ref,a_ref,nb,no):
    pan=panel_ref[...]; ow=own_ref[...]
    def bdot(a,b): return lax.dot_general(a,b,(((1,),(1,)),((),())),preferred_element_type=jnp.float32)
    c=-(2.0/panel_ref.shape[1])
    eye=lax.broadcasted_iota(jnp.int32,(B,B),0)==lax.broadcasted_iota(jnp.int32,(B,B),1)
    def diagrow(x):
        d=jnp.where(eye,x,0.0)
        return jnp.sum(d,axis=0,keepdims=True), jnp.sum(d,axis=1,keepdims=True)
    rows=[];cols=[]
    for i in range(nb):
        pi=pan[i*B:(i+1)*B]
        r,cc=diagrow(bdot(pi,pi)); rows.append(r); cols.append(cc)
    for i in range(no):
        oi=ow[i*B:(i+1)*B]
        r,_=diagrow(bdot(oi,oi)); rows.append(r)
    for i in range(nb):
        for j in range(i,nb+no):
            rhs=pan[j*B:(j+1)*B] if j<nb else ow[(j-nb)*B:(j-nb+1)*B]
            x=bdot(pan[i*B:(i+1)*B],rhs)
            k=jnp.exp(c*jnp.maximum(cols[i]+rows[j]-2.0*x,0.0))
            if j<nb:
                if i==j: k=k+jnp.where(eye,JITTER,0.0)
            else:
                gid=lax.broadcasted_iota(jnp.int32,(B,B),1)+(off_ref[0]+(j-nb)*B)
                k=k+jnp.where(gid==lax.broadcasted_iota(jnp.int32,(B,B),0)+i*B,JITTER,0.0)
            a_ref[i,j]=k

def body(off_ref,panel_ref,own_ref,chol_ref,prec_ref,a_ref,u_ref,l_ref,r_ref,w_ref,uk_ref,m_ref,*,own):
    nb=panel_ref.shape[0]//B; no=own//B; nj=nb+no
    eye=lax.broadcasted_iota(jnp.int32,(B,B),0)==lax.broadcasted_iota(jnp.int32,(B,B),1)
    kern_init(off_ref,panel_ref,own_ref,a_ref,nb,no)
    r_ref[...]=a_ref[0,0]
    u_ref[...]=jnp.zeros_like(u_ref); l_ref[...]=jnp.zeros_like(l_ref)
    def step(s,carry):
        ph=s//nb; K=s-ph*nb
        factor128(r_ref,w_ref,uk_ref,m_ref)
        lrow=jnp.concatenate([l_ref[K,t] for t in range(nb)],axis=1)
        M=m_ref[...]
        ua=u_ref[...]
        upd=mmul(lrow,ua)
        ar=jnp.concatenate([a_ref[K,j] for j in range(nj)],axis=1)-upd
        un=mmul(M,ar)
        for j in range(nj):
            v=un[:,j*B:(j+1)*B]
            if j<nb:
                v=jnp.where(j>K,v,0.0); v=jnp.where(j==K,uk_ref[...],v)
            u_ref[pl.ds(pl.multiple_of(K*B,B),B),j*B:(j+1)*B]=v
            l_ref[j,K]=v.T
        K1=jnp.minimum(K+1,nb-1)
        @pl.when(K<nb-1)
        def _():
            z=a_ref[K1,K1]
            lr=jnp.concatenate([l_ref[K1,t] for t in range(nb)],axis=1)
            r_ref[...]=z-mmul_nt(lr,lr)
        @pl.when(s==nb-1)
        def _():
            for i in range(no):
                for t in range(nb):
                    chol_ref[i*B:(i+1)*B,t*B:(t+1)*B]=l_ref[nb+i,t]
            for J in range(nb):
                for C in range(J,nb):
                    x=u_ref[J*B:(J+1)*B,C*B:nb*B]; y=u_ref[C*B:(C+1)*B,C*B:nb*B]
                    acc=mmul_nt(x,y)
                    if J==C: acc=acc+jnp.where(eye,SHIFT,0.0)
                    a_ref[J,C]=acc
            r_ref[...]=a_ref[0,0]
            u_ref[...]=jnp.zeros_like(u_ref); l_ref[...]=jnp.zeros_like(l_ref)
        return carry
    lax.fori_loop(0,2*nb,step,0)
    for J in range(nb):
        for C in range(nb):
            prec_ref[J*B:(J+1)*B,C*B:(C+1)*B]=l_ref[J,C]

def chol_kernel(off,panel,own):
    n=panel.shape[0]; ro=own.shape[0]; nb=n//B; no=ro//B
    vm=pl.BlockSpec(memory_space=pltpu.VMEM)
    f32=jnp.float32
    return pl.pallas_call(functools.partial(body,own=ro),
        out_shape=(jax.ShapeDtypeStruct((ro,n),f32),jax.ShapeDtypeStruct((n,n),f32)),
        in_specs=[pl.BlockSpec(memory_space=pltpu.SMEM),vm,vm],out_specs=(vm,vm),
        scratch_shapes=[pltpu.VMEM((nb,nb+no,B,B),f32),pltpu.VMEM((n,n+ro),f32),pltpu.VMEM((nb+no,nb,B,B),f32)]+[pltpu.VMEM((B,B),f32)]*4,
        name='chol')(off,panel,own)


from jax.sharding import PartitionSpec as P

PANEL = 512
GRAM_SCALE = 64.0


def swap(x, axis, d):
    n = lax.axis_size(axis)
    return lax.ppermute(x, axis, [(i, i ^ d) for i in range(n)])


def panel_everywhere(panel):
    ctrs = lax.axis_size("ctr")
    samps = lax.axis_size("samp")
    me = lax.axis_index("samp")
    rows = panel.shape[0] // samps
    chunk = lax.dynamic_slice_in_dim(panel, me * rows, rows, 0)
    got = [lax.ppermute(chunk, "ctr", [(0, d)]) for d in range(1, ctrs)]
    total = got[0]
    for piece in got[1:]:
        total = total + piece
    chunk = jnp.where(lax.axis_index("ctr") == 0, chunk, total)
    parts = jnp.stack([chunk] + [swap(chunk, "samp", d) for d in range(1, samps)])
    return jnp.take(parts, jnp.arange(samps) ^ me, axis=0).reshape(panel.shape)


def sample_scatter(part):
    samps = lax.axis_size("samp")
    me = lax.axis_index("samp")
    rows = part.shape[0] // samps
    blocks = part.reshape(samps // 2, 2, rows, part.shape[1])
    side = me & 1
    mine = lax.dynamic_index_in_dim(blocks, side, 1, False)
    other = lax.dynamic_index_in_dim(blocks, 1 - side, 1, False)
    half = mine + swap(other, "samp", 1)
    k = me >> 1
    total = lax.dynamic_index_in_dim(half, k, 0, False)
    for d in range(1, samps // 2):
        total = total + swap(lax.dynamic_index_in_dim(half, k ^ d, 0, False), "samp", 2 * d)
    return total


def kernel_block(first_set, second_set):
    cross_dot = lax.dot_general(
        first_set, second_set, (((1,), (1,)), ((), ())), preferred_element_type=jnp.float32
    )
    first_sq = jnp.sum(jnp.square(first_set.astype(jnp.float32)), axis=1)
    second_sq = jnp.sum(jnp.square(second_set.astype(jnp.float32)), axis=1)
    sq_dist = jnp.maximum(first_sq[:, None] + second_sq[None, :] - 2.0 * cross_dot, 0.0)
    return jnp.exp(-(2.0 / first_set.shape[1]) * sq_dist)


def local(samples, centers):
    samp_count = lax.axis_size("samp")
    samp_index = lax.axis_index("samp")
    ctr_index = lax.axis_index("ctr")
    mc_dev = centers.shape[0]
    row_dev = mc_dev // samp_count
    panel = panel_everywhere(centers[:PANEL])
    kern_own = kernel_block(centers, samples).astype(jnp.bfloat16)
    kern_panel = kernel_block(samples, panel).astype(jnp.bfloat16)
    part = jnp.dot(kern_own, kern_panel, preferred_element_type=jnp.float32)
    gram = sample_scatter(part) * (GRAM_SCALE / (samples.shape[0] * samp_count))
    own = lax.dynamic_slice_in_dim(centers, samp_index * row_dev, row_dev, 0)
    pad = -row_dev % B
    own = jnp.pad(own, ((0, pad), (0, 0)))
    off = (ctr_index * mc_dev + samp_index * row_dev).astype(jnp.int32).reshape(1)
    chol, precond = chol_kernel(off, panel, own)
    return (gram[None], chol[None, :row_dev], precond)


def solution(mesh):
    placed = (P("samp", None), P("ctr", None))
    return jax.shard_map(
        local,
        mesh=mesh,
        in_specs=placed,
        out_specs=(P("ctr", "samp", None), P("ctr", "samp", None), P()),
        check_vma=False,
    )
```

profile of v0, /device:TPU:0, one launch (start us, length us, event | category | flops | bytes accessed | tf_op | source)
XLA Modules:
  0.0 90.1 jit_solution(1474168330150760363)
XLA Ops:
  0.6 0.0 copy-start.2
  0.6 1.2 %slice.3 = bf16[512,512]{1,0:T(8,128)(2,1)S(1)} slice(bf16[1024,512]{1,0:T(8,128)(2,1)} %param.3), slice={[0:512], [0:512]} | slice | bytes 1048576 | tf_op jit(solution)/shard_map/slice | solution.py:197
  1.9 5.0 %collective-permute-start = (bf16[64,512]{1,0:T(8,128)(2,1)S(1)}, bf16[64,512]{1,0:T(8,128)(2,1)S(1)}, u32[]{:S(2)}, u32[]{:S(2)}) collective-permute-start(bf16[64,512]{1,0:T(8,128)(2,1)S(1)} %constant_dynamic-slice_fusion.1), channel_id=1, source_target_pairs={{0,1},{4,5},{8,9},{12,13},{16,17},{20,21},{24,25},{28,29}} | collective-permute-start | bytes 196616 | tf_op jit(solution)/shard_map/ppermute | solution.py:156
  6.9 1.7 %collective-permute-start.1 = (bf16[64,512]{1,0:T(8,128)(2,1)S(1)}, bf16[64,512]{1,0:T(8,128)(2,1)S(1)}, u32[]{:S(2)}, u32[]{:S(2)}) collective-permute-start(bf16[64,512]{1,0:T(8,128)(2,1)S(1)} %constant_dynamic-slice_fusion.1), channel_id=1, source_target_pairs={{0,2},{4,6},{8,10},{12,14},{16,18},{20,22},{24,26},{28,30}} | collective-permute-start | bytes 196616 | tf_op jit(solution)/shard_map/ppermute | solution.py:156
  8.6 1.7 %collective-permute-start.2 = (bf16[64,512]{1,0:T(8,128)(2,1)S(1)}, bf16[64,512]{1,0:T(8,128)(2,1)S(1)}, u32[]{:S(2)}, u32[]{:S(2)}) collective-permute-start(bf16[64,512]{1,0:T(8,128)(2,1)S(1)} %constant_dynamic-slice_fusion.1), channel_id=1, source_target_pairs={{0,3},{4,7},{8,11},{12,15},{16,19},{20,23},{24,27},{28,31}} | collective-permute-start | bytes 196616 | tf_op jit(solution)/shard_map/ppermute | solution.py:156
  10.3 1.5 %multiply_reduce_fusion.1 = f32[1024]{0:T(1024)S(1)} fusion(bf16[1024,512]{1,0:T(8,128)(2,1)} %param.3), kind=kLoop, calls=%fused_computation.8 | loop fusion | flops 1571840 | bytes 1052672 | tf_op jit(solution)/shard_map/reduce_sum | solution.py:185
  11.8 0.1 broadcast_in_dim.30
  11.8 0.1 broadcast_in_dim.31
  11.9 0.0 copy-done.2
  11.9 0.5 multiply_reduce_fusion
  12.4 0.0 collective-permute-done
  12.4 0.0 collective-permute-done.1
  12.4 0.0 collective-permute-done.2
  12.5 0.1 collective-permute-start.3
  12.6 1.6 %collective-permute-start.4 = (bf16[64,512]{1,0:T(8,128)(2,1)S(1)}, bf16[64,512]{1,0:T(8,128)(2,1)S(1)}, u32[]{:S(2)}, u32[]{:S(2)}) collective-permute-start(bf16[64,512]{1,0:T(8,128)(2,1)S(1)} %get-tuple-element.8), channel_id=1, source_target_pairs={{0,8},{4,12},{8,0},{12,4},{16,24},{20,28},{24,16},{28,20},{1,9},{5... | collective-permute-start | bytes 196616 | tf_op jit(solution)/shard_map/ppermute | solution.py:147
  14.2 0.3 collective-permute-start.5
  14.4 1.5 %collective-permute-start.6 = (bf16[64,512]{1,0:T(8,128)(2,1)S(1)}, bf16[64,512]{1,0:T(8,128)(2,1)S(1)}, u32[]{:S(2)}, u32[]{:S(2)}) collective-permute-start(bf16[64,512]{1,0:T(8,128)(2,1)S(1)} %get-tuple-element.8), channel_id=1, source_target_pairs={{0,16},{4,20},{8,24},{12,28},{16,0},{20,4},{24,8},{28,12},{1,17},{... | collective-permute-start | bytes 196616 | tf_op jit(solution)/shard_map/ppermute | solution.py:147
  16.0 0.2 collective-permute-start.7
  16.2 0.0 collective-permute-done.3
  16.2 2.4 %collective-permute-start.8 = (bf16[64,512]{1,0:T(8,128)(2,1)S(1)}, bf16[64,512]{1,0:T(8,128)(2,1)S(1)}, u32[]{:S(2)}, u32[]{:S(2)}) collective-permute-start(bf16[64,512]{1,0:T(8,128)(2,1)S(1)} %get-tuple-element.8), channel_id=1, source_target_pairs={{0,24},{4,28},{8,16},{12,20},{16,8},{20,12},{24,0},{28,4},{1,25},{... | collective-permute-start | bytes 196616 | tf_op jit(solution)/shard_map/ppermute | solution.py:147
  18.6 0.0 collective-permute-done.4
  18.6 0.3 collective-permute-start.9
  18.9 0.0 collective-permute-done.5
  18.9 0.0 collective-permute-done.6
  19.0 1.1 %collective-permute-done.7 = bf16[64,512]{1,0:T(8,128)(2,1)S(1)} collective-permute-done((bf16[64,512]{1,0:T(8,128)(2,1)S(1)}, bf16[64,512]{1,0:T(8,128)(2,1)S(1)}, u32[]{:S(2)}, u32[]{:S(2)}) %collective-permute-start.7) | collective-permute-done | bytes 65568 | tf_op jit(solution)/shard_map/ppermute | solution.py:147
  20.1 1.5 %collective-permute-done.8 = bf16[64,512]{1,0:T(8,128)(2,1)S(1)} collective-permute-done((bf16[64,512]{1,0:T(8,128)(2,1)S(1)}, bf16[64,512]{1,0:T(8,128)(2,1)S(1)}, u32[]{:S(2)}, u32[]{:S(2)}) %collective-permute-start.8) | collective-permute-done | bytes 65568 | tf_op jit(solution)/shard_map/ppermute | solution.py:147
  21.6 2.1 %collective-permute-done.9 = bf16[64,512]{1,0:T(8,128)(2,1)S(1)} collective-permute-done((bf16[64,512]{1,0:T(8,128)(2,1)S(1)}, bf16[64,512]{1,0:T(8,128)(2,1)S(1)}, u32[]{:S(2)}, u32[]{:S(2)}) %collective-permute-start.9) | collective-permute-done | bytes 65568 | tf_op jit(solution)/shard_map/ppermute | solution.py:147
  23.7 0.6 gather_fusion
  24.2 0.3 multiply_reduce_fusion.2
  24.5 1.0 %bitcast_select_fusion.panel_ref = bf16[512,512]{1,0:T(8,128)(2,1)} fusion(bf16[8,64,512]{2,1,0:T(8,128)(2,1)S(1)} %gather_fusion, pred[512]{0:T(512)(128)(4,1)S(1)} %broadcast_in_dim.31), kind=kLoop, calls=%fused_computation.13 | loop fusion | flops 262144 | bytes 1049088 | tf_op jit(solution)/shard_map/jit(_take)/select_n | solution.py:162
  25.5 0.1 add.100
  25.6 4.3 %fusion.3 = bf16[2048,512]{1,0:T(8,128)(2,1)} fusion(bf16[512,512]{1,0:T(8,128)(2,1)} %bitcast_select_fusion.panel_ref, bf16[2048,512]{1,0:T(8,128)(2,1)S(1)} %copy-done.2, f32[512]{0:T(512)S(1)} %add.100, f32[2048]{0:T(1024)S(1)} %multiply_reduce_fusion), kind=kOutput, calls=%fused_computation.6 | convolution fusion | flops 1080033280 | bytes 4728832 | tf_op jit(solution)/shard_map/dot_general | solution.py:182
  29.9 6.9 %fusion.4 = f32[1024,512]{1,0:T(8,128)S(1)} fusion(bf16[2048,512]{1,0:T(8,128)(2,1)} %fusion.3, bf16[1024,512]{1,0:T(8,128)(2,1)S(1)} %copy-done, bf16[2048,512]{1,0:T(8,128)(2,1)} %param.2, f32[2048]{0:T(1024)S(1)} %multiply_reduce_fusion, f32[1024]{0:T(1024)S(1)} %multiply_reduce_fusion.1), kind=kOutput, calls=%fused_computation.9 | convolution fusion | flops 4307550208 | bytes 7352320 | tf_op jit(solution)/shard_map/dot_general | solution.py:200
  36.8 1.1 %dynamic-slice_bitcast_fusion = f32[4,128,512]{2,1,0:T(8,128)} fusion(f32[4,2,128,512]{3,2,1,0:T(8,128)S(1)} %bitcast.60, s32[]{:T(128)S(6)} %select_n.66), kind=kLoop, calls=%fused_computation.11 | loop fusion | bytes 2097156 | tf_op jit(solution)/shard_map/jit(dynamic_index_in_dim)/squeeze | solution.py:172
  37.9 0.1 collective-permute-start.10
  38.0 0.5 copy-done.1
  38.5 2.4 %collective-permute-done.10 = f32[4,128,512]{2,1,0:T(8,128)} collective-permute-done((f32[4,128,512]{2,1,0:T(8,128)}, f32[4,128,512]{2,1,0:T(8,128)}, u32[]{:S(2)}, u32[]{:S(2)}) %collective-permute-start.10) | collective-permute-done | bytes 1048608 | tf_op jit(solution)/shard_map/ppermute | solution.py:147
  40.9 1.7 %bitcast_add_fusion = f32[4,128,512]{2,1,0:T(8,128)S(1)} fusion(f32[4,128,512]{2,1,0:T(8,128)} %collective-permute-done.10, f32[4,2,128,512]{3,2,1,0:T(8,128)} %bitcast.61, s32[]{:T(128)S(6)} %select_n.65), kind=kLoop, calls=%fused_computation.10 | loop fusion | flops 262144 | bytes 3145732 | tf_op jit(solution)/shard_map/add | solution.py:173
  42.6 0.1 dynamic-slice_bitcast_fusion.3
  42.7 0.6 collective-permute-start.11
  43.3 1.8 %collective-permute-start.12 = (f32[128,512]{1,0:T(8,128)S(1)}, f32[128,512]{1,0:T(8,128)S(1)}, u32[]{:S(2)}, u32[]{:S(2)}) collective-permute-start(f32[128,512]{1,0:T(8,128)S(1)} %get-tuple-element.11), channel_id=1, source_target_pairs={{0,16},{4,20},{8,24},{12,28},{16,0},{20,4},{24,8},{28,12},{1,17},{... | collective-permute-start | bytes 786440 | tf_op jit(solution)/shard_map/ppermute | solution.py:147
  45.1 1.2 %collective-permute-start.13 = (f32[128,512]{1,0:T(8,128)S(1)}, f32[128,512]{1,0:T(8,128)}, u32[]{:S(2)}, u32[]{:S(2)}) collective-permute-start(f32[128,512]{1,0:T(8,128)S(1)} %get-tuple-element.10), channel_id=1, source_target_pairs={{0,24},{4,28},{8,16},{12,20},{16,8},{20,12},{24,0},{28,4},{1,25},{... | collective-permute-start | bytes 786440 | tf_op jit(solution)/shard_map/ppermute | solution.py:147
  46.3 0.7 constant_dynamic-slice_fusion.own_ref
  46.9 41.4 %chol.1 = (f32[128,512]{1,0:T(8,128)}, f32[512,512]{1,0:T(8,128)}) custom-call(s32[1]{0:T(128)} %bitcast.19.off_ref, bf16[512,512]{1,0:T(8,128)(2,1)} %bitcast_select_fusion.panel_ref, bf16[128,512]{1,0:T(8,128)(2,1)} %constant_dynamic-slice_fusion.own_ref), custom_call_target="tpu_custom_call" | custom-call | tf_op jit(solution)/shard_map/chol/pallas_call | solution.py:132
  88.4 0.0 collective-permute-done.11
  88.4 0.0 collective-permute-done.12
  88.4 0.0 collective-permute-done.13
  88.4 1.7 %fusion.8 = f32[1,128,512]{2,1,0:T(8,128)} fusion(f32[128,512]{1,0:T(8,128)} %collective-permute-done.13, f32[128,512]{1,0:T(8,128)S(1)} %collective-permute-done.12, f32[128,512]{1,0:T(8,128)S(1)} %collective-permute-done.11, f32[4,128,512]{2,1,0:T(8,128)S(1)} %bitcast_add_fusion, s32[]{:T(128)S(6)} %select_n.67), kind=kLoop, calls=%fused_computation.18 | loop fusion | flops 262144 | bytes 1310724 | tf_op jit(solution)/shard_map/broadcast_in_dim | solution.py:207
  (15 shorter events, 0.1 us)
Async XLA Ops:
  0.6 11.3 %copy-start.2 = (bf16[2048,512]{1,0:T(8,128)(2,1)S(1)}, bf16[2048,512]{1,0:T(8,128)(2,1)}, u32[]{:S(2)}) copy-start(bf16[2048,512]{1,0:T(8,128)(2,1)} %param.2) | copy-start | bytes 6291460
  1.9 10.5 %collective-permute-start = (bf16[64,512]{1,0:T(8,128)(2,1)S(1)}, bf16[64,512]{1,0:T(8,128)(2,1)S(1)}, u32[]{:S(2)}, u32[]{:S(2)}) collective-permute-start(bf16[64,512]{1,0:T(8,128)(2,1)S(1)} %constant_dynamic-slice_fusion.1), channel_id=1, source_target_pairs={{0,1},{4,5},{8,9},{12,13},{16,17},{20,21},{24,25},{28,29}} | collective-permute-start | bytes 196616 | tf_op jit(solution)/shard_map/ppermute | solution.py:156
  6.9 5.6 %collective-permute-start.1 = (bf16[64,512]{1,0:T(8,128)(2,1)S(1)}, bf16[64,512]{1,0:T(8,128)(2,1)S(1)}, u32[]{:S(2)}, u32[]{:S(2)}) collective-permute-start(bf16[64,512]{1,0:T(8,128)(2,1)S(1)} %constant_dynamic-slice_fusion.1), channel_id=1, source_target_pairs={{0,2},{4,6},{8,10},{12,14},{16,18},{20,22},{24,26},{28,30}} | collective-permute-start | bytes 196616 | tf_op jit(solution)/shard_map/ppermute | solution.py:156
  8.6 3.9 %collective-permute-start.2 = (bf16[64,512]{1,0:T(8,128)(2,1)S(1)}, bf16[64,512]{1,0:T(8,128)(2,1)S(1)}, u32[]{:S(2)}, u32[]{:S(2)}) collective-permute-start(bf16[64,512]{1,0:T(8,128)(2,1)S(1)} %constant_dynamic-slice_fusion.1), channel_id=1, source_target_pairs={{0,3},{4,7},{8,11},{12,15},{16,19},{20,23},{24,27},{28,31}} | collective-permute-start | bytes 196616 | tf_op jit(solution)/shard_map/ppermute | solution.py:156
  12.5 3.7 %collective-permute-start.3 = (bf16[64,512]{1,0:T(8,128)(2,1)S(1)}, bf16[64,512]{1,0:T(8,128)(2,1)S(1)}, u32[]{:S(2)}, u32[]{:S(2)}) collective-permute-start(bf16[64,512]{1,0:T(8,128)(2,1)S(1)} %get-tuple-element.8), channel_id=1, source_target_pairs={{0,4},{4,0},{8,12},{12,8},{16,20},{20,16},{24,28},{28,24},{1,5},{5... | collective-permute-start | bytes 196616 | tf_op jit(solution)/shard_map/ppermute | solution.py:147
  12.6 6.0 %collective-permute-start.4 = (bf16[64,512]{1,0:T(8,128)(2,1)S(1)}, bf16[64,512]{1,0:T(8,128)(2,1)S(1)}, u32[]{:S(2)}, u32[]{:S(2)}) collective-permute-start(bf16[64,512]{1,0:T(8,128)(2,1)S(1)} %get-tuple-element.8), channel_id=1, source_target_pairs={{0,8},{4,12},{8,0},{12,4},{16,24},{20,28},{24,16},{28,20},{1,9},{5... | collective-permute-start | bytes 196616 | tf_op jit(solution)/shard_map/ppermute | solution.py:147
  14.2 4.8 %collective-permute-start.5 = (bf16[64,512]{1,0:T(8,128)(2,1)S(1)}, bf16[64,512]{1,0:T(8,128)(2,1)S(1)}, u32[]{:S(2)}, u32[]{:S(2)}) collective-permute-start(bf16[64,512]{1,0:T(8,128)(2,1)S(1)} %get-tuple-element.8), channel_id=1, source_target_pairs={{0,12},{4,8},{8,4},{12,0},{16,28},{20,24},{24,20},{28,16},{1,13},{... | collective-permute-start | bytes 196616 | tf_op jit(solution)/shard_map/ppermute | solution.py:147
  14.4 4.5 %collective-permute-start.6 = (bf16[64,512]{1,0:T(8,128)(2,1)S(1)}, bf16[64,512]{1,0:T(8,128)(2,1)S(1)}, u32[]{:S(2)}, u32[]{:S(2)}) collective-permute-start(bf16[64,512]{1,0:T(8,128)(2,1)S(1)} %get-tuple-element.8), channel_id=1, source_target_pairs={{0,16},{4,20},{8,24},{12,28},{16,0},{20,4},{24,8},{28,12},{1,17},{... | collective-permute-start | bytes 196616 | tf_op jit(solution)/shard_map/ppermute | solution.py:147
  16.0 4.1 %collective-permute-start.7 = (bf16[64,512]{1,0:T(8,128)(2,1)S(1)}, bf16[64,512]{1,0:T(8,128)(2,1)S(1)}, u32[]{:S(2)}, u32[]{:S(2)}) collective-permute-start(bf16[64,512]{1,0:T(8,128)(2,1)S(1)} %get-tuple-element.8), channel_id=1, source_target_pairs={{0,20},{4,16},{8,28},{12,24},{16,4},{20,0},{24,12},{28,8},{1,21},{... | collective-permute-start | bytes 196616 | tf_op jit(solution)/shard_map/ppermute | solution.py:147
  16.2 5.4 %collective-permute-start.8 = (bf16[64,512]{1,0:T(8,128)(2,1)S(1)}, bf16[64,512]{1,0:T(8,128)(2,1)S(1)}, u32[]{:S(2)}, u32[]{:S(2)}) collective-permute-start(bf16[64,512]{1,0:T(8,128)(2,1)S(1)} %get-tuple-element.8), channel_id=1, source_target_pairs={{0,24},{4,28},{8,16},{12,20},{16,8},{20,12},{24,0},{28,4},{1,25},{... | collective-permute-start | bytes 196616 | tf_op jit(solution)/shard_map/ppermute | solution.py:147
  18.6 5.0 %collective-permute-start.9 = (bf16[64,512]{1,0:T(8,128)(2,1)S(1)}, bf16[64,512]{1,0:T(8,128)(2,1)S(1)}, u32[]{:S(2)}, u32[]{:S(2)}) collective-permute-start(bf16[64,512]{1,0:T(8,128)(2,1)S(1)} %get-tuple-element.8), channel_id=1, source_target_pairs={{0,28},{4,24},{8,20},{12,16},{16,12},{20,8},{24,4},{28,0},{1,29},{... | collective-permute-start | bytes 196616 | tf_op jit(solution)/shard_map/ppermute | solution.py:147
  25.6 4.3 %copy-start = (bf16[1024,512]{1,0:T(8,128)(2,1)S(1)}, bf16[1024,512]{1,0:T(8,128)(2,1)}, u32[]{:S(2)}) copy-start(bf16[1024,512]{1,0:T(8,128)(2,1)} %param.3) | copy-start | bytes 3145732
  36.8 1.8 %copy-start.1 = (f32[1024,512]{1,0:T(8,128)}, f32[1024,512]{1,0:T(8,128)S(1)}, u32[]{:S(2)}) copy-start(f32[1024,512]{1,0:T(8,128)S(1)} %fusion.4) | copy-start | bytes 6291460
  37.9 3.0 %collective-permute-start.10 = (f32[4,128,512]{2,1,0:T(8,128)}, f32[4,128,512]{2,1,0:T(8,128)}, u32[]{:S(2)}, u32[]{:S(2)}) collective-permute-start(f32[4,128,512]{2,1,0:T(8,128)} %dynamic-slice_bitcast_fusion), channel_id=1, source_target_pairs={{0,4},{4,0},{8,12},{12,8},{16,20},{20,16},{24,28},{28,24},{1,5},{5... | collective-permute-start | bytes 3145736 | tf_op jit(solution)/shard_map/ppermute | solution.py:147
  42.7 45.7 %collective-permute-start.11 = (f32[128,512]{1,0:T(8,128)S(1)}, f32[128,512]{1,0:T(8,128)S(1)}, u32[]{:S(2)}, u32[]{:S(2)}) collective-permute-start(f32[128,512]{1,0:T(8,128)S(1)} %get-tuple-element.9), channel_id=1, source_target_pairs={{0,8},{4,12},{8,0},{12,4},{16,24},{20,28},{24,16},{28,20},{1,9},{5... | collective-permute-start | bytes 786440 | tf_op jit(solution)/shard_map/ppermute | solution.py:147
  43.3 45.1 %collective-permute-start.12 = (f32[128,512]{1,0:T(8,128)S(1)}, f32[128,512]{1,0:T(8,128)S(1)}, u32[]{:S(2)}, u32[]{:S(2)}) collective-permute-start(f32[128,512]{1,0:T(8,128)S(1)} %get-tuple-element.11), channel_id=1, source_target_pairs={{0,16},{4,20},{8,24},{12,28},{16,0},{20,4},{24,8},{28,12},{1,17},{... | collective-permute-start | bytes 786440 | tf_op jit(solution)/shard_map/ppermute | solution.py:147
  45.1 43.3 %collective-permute-start.13 = (f32[128,512]{1,0:T(8,128)S(1)}, f32[128,512]{1,0:T(8,128)}, u32[]{:S(2)}, u32[]{:S(2)}) collective-permute-start(f32[128,512]{1,0:T(8,128)S(1)} %get-tuple-element.10), channel_id=1, source_target_pairs={{0,24},{4,28},{8,16},{12,20},{16,8},{20,12},{24,0},{28,4},{1,25},{... | collective-permute-start | bytes 786440 | tf_op jit(solution)/shard_map/ppermute | solution.py:147
where the time goes:
time: 90.5 us; the launch traced here: 90.1 us
  Pallas kernels  41.4 us (46%)
  starting transfers between devices  18.4 us (20%)
  matrix products  11.2 us (12%)
  waiting for transfers between devices  7.08 us (8%)
  other arithmetic  6.77 us (7%)
  local copies, waits for them, and re-layouts  4.44 us (5%)
    pallas_call x1, Pallas kernels, chol_kernel(): pl.pallas_call(functools.partial(body, own=ro), out_shape=(jax.ShapeDtype...  41.4 us
    ppermute x11, starting transfers between devices, swap(): return lax.ppermute(x, axis, [(i, i ^ d) for i in range(n)])  10.1 us
    ppermute x3, starting transfers between devices, panel_everywhere(): got = [lax.ppermute(chunk, 'ctr', [(0, d)]) for d in range(1, ctrs)]  8.31 us
    ppermute x11, waiting for transfers between devices, swap(): return lax.ppermute(x, axis, [(i, i ^ d) for i in range(n)])  7.07 us
    dot_general x1, matrix products, local(): part = jnp.dot(kern_own, kern_panel, preferred_element_type=jnp.float32)  6.88 us
    dot_general x1, matrix products, kernel_block(): lax.dot_general(first_set, second_set, (((1,), (1,)), ((), ())), preferre...  4.29 us
  transfers between devices with their start and end apart: 14, of which 4 were waited for; matrix products, arithmetic and copies ran while one was open for 3% of the time, Pallas kernels for 46%

commit v1 on v0

v1 whole, which is shorter than its diff:
```python
import functools
import jax, jax.numpy as jnp
from jax import lax
from jax.experimental import pallas as pl
from jax.experimental.pallas import tpu as pltpu
JITTER=0.01; SHIFT=0.5
RATIO=1.0/64
B=128
VB=32
HI=lax.Precision.HIGHEST
def mmul(a,b): return jnp.dot(a,b,preferred_element_type=jnp.float32,precision=HI)
def mmul_nt(a,b): return lax.dot_general(a,b,(((1,),(1,)),((),())),preferred_element_type=jnp.float32,precision=HI)
def lanebc(x,c): return jnp.broadcast_to(x[:,c:c+1],(8,B))
def subbc(x,j): return jnp.broadcast_to(x[j:j+1,:],(8,B))

def factor128(probs):
    row=lax.broadcasted_iota(jnp.int32,(B,B),0)
    lane=lax.broadcasted_iota(jnp.int32,(B,B),1)
    n=VB//8
    for r,w,u,m in probs: w[...]=jnp.where(lane==row,1.0,0.0)
    for b in range(B//VB):
        base=b*VB
        st=[]
        for r,w,u,m in probs:
            st.append(([r[base+8*k:base+8*k+8,:] for k in range(n)],[w[base+8*k:base+8*k+8,:] for k in range(n)]))
        for i in range(n):
            loc=[]
            for X,Y in st:
                g=[lanebc(X[i],base+8*i+j) for j in range(8)]
                c={k:[lanebc(X[k],base+8*i+j) for j in range(8)] for k in range(i+1,n)}
                loc.append([g,c,X[i],Y[i]])
            for j in range(8):
                k=base+8*i+j
                for (r,w,u,m),(X,Y),L in zip(probs,st,loc):
                    g,c,a,y=L
                    rs=lax.rsqrt(subbc(g[j],j))
                    q=[None]*8
                    lj=g[j]*rs
                    for t in range(j+1,8):
                        q[t]=subbc(g[t],j)*rs
                        g[t]=g[t]-lj*q[t]
                    ur=subbc(a,j)*rs; wr=subbc(y,j)*rs
                    if j<7:
                        L[2]=a-lj*ur; L[3]=y-lj*wr
                    u[k:k+1,:]=ur[0:1]; m[k:k+1,:]=wr[0:1]
                    for z in range(i+1,n):
                        cj=c[z][j]*rs
                        for t in range(j+1,8): c[z][t]=c[z][t]-cj*q[t]
                        X[z]=X[z]-cj*ur; Y[z]=Y[z]-cj*wr
        e=base+VB
        if e<B:
            for r,w,u,m in probs:
                ub=u[base:e,:]; mb=m[base:e,:]
                z=mmul(ub.T[e:,:],jnp.concatenate([ub,mb],axis=1))
                r[e:,:]=r[e:,:]-z[:,:B]
                w[e:,:]=w[e:,:]-z[:,B:]
    for r,w,u,m in probs: u[...]=jnp.where(lane>=row,u[...],0.0)

def kern_init(off_ref,panel_ref,own_ref,a_ref,nb,no):
    pan=panel_ref[...]; ow=own_ref[...]
    def bdot(a,b): return lax.dot_general(a,b,(((1,),(1,)),((),())),preferred_element_type=jnp.float32)
    c=-(2.0/panel_ref.shape[1])
    eye=lax.broadcasted_iota(jnp.int32,(B,B),0)==lax.broadcasted_iota(jnp.int32,(B,B),1)
    def diagrow(x):
        d=jnp.where(eye,x,0.0)
        return jnp.sum(d,axis=0,keepdims=True), jnp.sum(d,axis=1,keepdims=True)
    rows=[];cols=[]
    for i in range(nb):
        pi=pan[i*B:(i+1)*B]
        r,cc=diagrow(bdot(pi,pi)); rows.append(r); cols.append(cc)
    for i in range(no):
        oi=ow[i*B:(i+1)*B]
        r,_=diagrow(bdot(oi,oi)); rows.append(r)
    for i in range(nb):
        for j in range(nb+no):
            rhs=pan[j*B:(j+1)*B] if j<nb else ow[(j-nb)*B:(j-nb+1)*B]
            x=bdot(pan[i*B:(i+1)*B],rhs)
            k=jnp.exp(c*jnp.maximum(cols[i]+rows[j]-2.0*x,0.0))
            if j<nb:
                if i==j: k=k+jnp.where(eye,JITTER,0.0)
            else:
                gid=lax.broadcasted_iota(jnp.int32,(B,B),1)+(off_ref[0]+(j-nb)*B)
                k=k+jnp.where(gid==lax.broadcasted_iota(jnp.int32,(B,B),0)+i*B,JITTER,0.0)
            a_ref[i,j]=k

def put(M,uk,row,K,nb,u_ref,l_ref):
    un=mmul(M,jnp.concatenate(row,axis=1))
    for j in range(len(row)):
        v=un[:,j*B:(j+1)*B]
        if j<nb:
            v=jnp.where(j>K,v,0.0); v=jnp.where(j==K,uk,v)
        u_ref[K,j]=v
        l_ref[j,K]=v.T

def trail(a_ref,u_ref,l_ref,Kp,nb,nj):
    for i in range(1,nb):
        z=mmul(l_ref[i,Kp],jnp.concatenate([u_ref[Kp,j] for j in range(i,nj)],axis=1))
        for j in range(i,nj):
            a_ref[i,j]=a_ref[i,j]-z[:,(j-i)*B:(j-i+1)*B]

def body(off_ref,panel_ref,own_ref,chol_ref,prec_ref,a_ref,u_ref,l_ref,s_ref,v_ref,h_ref,ms_ref,r0,w0,k0,m0,r1,w1,k1,m1,*,own):
    nb=panel_ref.shape[0]//B; no=own//B; nj=nb+no
    eye=lax.broadcasted_iota(jnp.int32,(B,B),0)==lax.broadcasted_iota(jnp.int32,(B,B),1)
    kern_init(off_ref,panel_ref,own_ref,a_ref,nb,no)
    zero=jnp.zeros((B,B),jnp.float32)
    for j in range(nj):
        u_ref[nb,j]=zero; l_ref[j,nb]=zero
    for j in range(nb):
        v_ref[nb,j]=zero; h_ref[j,nb]=zero
    kr=[jnp.concatenate([a_ref[i,j] for j in range(nb)],axis=1) for i in range(nb)]
    kc=jnp.concatenate(kr,axis=0)
    top=None
    for i in range(nb):
        z=mmul(kr[i],kc[:,i*B:])+SHIFT*kr[i][:,i*B:]
        for j in range(i,nb):
            s_ref[i,j]=z[:,(j-i)*B:(j-i+1)*B]
        d=jnp.where(eye,s_ref[i,i],0.0)
        top=d if top is None else jnp.maximum(top,d)
    r0[...]=a_ref[0,0]; r1[...]=s_ref[0,0]
    def step(K,low):
        Kp=jnp.where(K==0,nb,K-1)
        factor128([(r0,w0,k0,m0),(r1,w1,k1,m1)])
        trail(a_ref,u_ref,l_ref,Kp,nb,nj)
        trail(s_ref,v_ref,h_ref,Kp,nb,nb)
        ms_ref[K]=m0[...]
        put(m0[...],k0[...],[a_ref[K,j] for j in range(nj)],K,nb,u_ref,l_ref)
        put(m1[...],k1[...],[s_ref[K,j] for j in range(nb)],K,nb,v_ref,h_ref)
        K1=jnp.minimum(K+1,nb-1)
        r0[...]=a_ref[K1,K1]-mmul(l_ref[K1,K],u_ref[K,K1])
        r1[...]=s_ref[K1,K1]-mmul(h_ref[K1,K],v_ref[K,K1])
        x=k1[...]
        return jnp.minimum(low,jnp.where(eye,x*x,1e30))
    low=lax.fori_loop(0,nb,step,jnp.full((B,B),1e30,jnp.float32))
    for i in range(no):
        for t in range(nb):
            chol_ref[i*B:(i+1)*B,t*B:(t+1)*B]=l_ref[nb+i,t]
    good=jnp.min(low)>=RATIO*jnp.max(top)
    @pl.when(good)
    def _():
        g=[]
        for K in range(nb):
            c=jnp.concatenate([h_ref[K,J] for J in range(K+1)],axis=1)
            for t in range(K):
                z=mmul(l_ref[K,t],g[t])
                c=jnp.concatenate([c[:,:(t+1)*B]-z,c[:,(t+1)*B:]],axis=1)
            g.append(mmul(ms_ref[K],c))
        for K in range(nb):
            for J in range(nb):
                prec_ref[K*B:(K+1)*B,J*B:(J+1)*B]=g[K][:,J*B:(J+1)*B] if J<=K else zero
    @pl.when(jnp.logical_not(good))
    def _():
        for C in range(nb):
            rows=[jnp.concatenate([u_ref[J,I] for I in range(C,nb)],axis=1) for J in range(C+1)]
            acc=mmul_nt(jnp.concatenate(rows,axis=0),rows[C])
            for J in range(C+1):
                v=acc[J*B:(J+1)*B]
                if J==C: v=v+jnp.where(eye,SHIFT,0.0)
                s_ref[J,C]=v
        for j in range(nb):
            v_ref[nb,j]=zero; h_ref[j,nb]=zero
        r1[...]=s_ref[0,0]
        def again(K,carry):
            Kp=jnp.where(K==0,nb,K-1)
            factor128([(r1,w1,k1,m1)])
            trail(s_ref,v_ref,h_ref,Kp,nb,nb)
            put(m1[...],k1[...],[s_ref[K,j] for j in range(nb)],K,nb,v_ref,h_ref)
            K1=jnp.minimum(K+1,nb-1)
            r1[...]=s_ref[K1,K1]-mmul(h_ref[K1,K],v_ref[K,K1])
            return carry
        lax.fori_loop(0,nb,again,0)
        for J in range(nb):
            for C in range(nb):
                prec_ref[J*B:(J+1)*B,C*B:(C+1)*B]=h_ref[J,C]

def chol_kernel(off,panel,own):
    n=panel.shape[0]; ro=own.shape[0]; nb=n//B; no=ro//B; nj=nb+no
    vm=pl.BlockSpec(memory_space=pltpu.VMEM)
    f32=jnp.float32
    V=lambda *s: pltpu.VMEM(s+(B,B),f32)
    return pl.pallas_call(functools.partial(body,own=ro),
        out_shape=(jax.ShapeDtypeStruct((ro,n),f32),jax.ShapeDtypeStruct((n,n),f32)),
        in_specs=[pl.BlockSpec(memory_space=pltpu.SMEM),vm,vm],out_specs=(vm,vm),
        scratch_shapes=[V(nb,nj),V(nb+1,nj),V(nj,nb+1),V(nb,nb),V(nb+1,nb),V(nb,nb+1),V(nb)]+[V()]*8,
        name='chol')(off,panel,own)


LOG2E = 1.4426950408889634


def row_norms(x, scale):
    sq = jnp.square(x.astype(jnp.float32))
    hi = sq.astype(jnp.bfloat16)
    lo = (sq - hi.astype(jnp.float32)).astype(jnp.bfloat16)
    one = jnp.ones((8, x.shape[1]), jnp.bfloat16)
    dims = (((1,), (1,)), ((), ()))
    out = lax.dot_general(one, hi, dims, preferred_element_type=jnp.float32)
    out = out + lax.dot_general(one, lo, dims, preferred_element_type=jnp.float32)
    return out[0:1] * scale


def col_norms(x, scale):
    return jnp.sum(jnp.square(x.astype(jnp.float32)), axis=1, keepdims=True) * scale


def kern_tile(x, y, xcol, yrow):
    dot = lax.dot_general(x, y, (((1,), (1,)), ((), ())), preferred_element_type=jnp.float32)
    arg = jnp.minimum(dot * (4.0 * LOG2E / x.shape[1]) + (xcol + yrow), 0.0)
    return jnp.exp2(arg).astype(jnp.bfloat16)


def own_body(c_ref, s_ref, o_ref):
    scale = -2.0 * LOG2E / c_ref.shape[1]
    s = s_ref[...]
    yrow = row_norms(s, scale)
    for r in range(c_ref.shape[0] // B):
        c = c_ref[r * B : (r + 1) * B, :]
        o_ref[r * B : (r + 1) * B, :] = kern_tile(c, s, col_norms(c, scale), yrow)


def own_kernel(centers, samples, tile=512):
    mc, d = centers.shape
    ns = samples.shape[0]
    return pl.pallas_call(
        own_body,
        grid=(ns // tile,),
        in_specs=[pl.BlockSpec((mc, d), lambda t: (0, 0)), pl.BlockSpec((tile, d), lambda t: (t, 0))],
        out_specs=pl.BlockSpec((mc, tile), lambda t: (0, t)),
        out_shape=jax.ShapeDtypeStruct((mc, ns), jnp.bfloat16),
        name="kern_own",
    )(centers, samples)


def gram_body(me_ref, *refs, tiles):
    pieces, (k_ref, s_ref, other_ref, mine_ref, panel_ref, acc_ref, row_ref) = refs[:-7], refs[-7:]
    samps = len(pieces)
    t = pl.program_id(0)
    me = me_ref[0]
    scale = -2.0 * LOG2E / s_ref.shape[1]

    @pl.when(t == 0)
    def _():
        rows = pieces[0].shape[0]
        for d in range(samps):
            at = pl.multiple_of((me ^ d) * rows, rows)
            panel_ref[pl.ds(at, rows), :] = pieces[d][...]
        row_ref[...] = row_norms(panel_ref[...], scale)
        acc_ref[...] = jnp.zeros_like(acc_ref)

    panel = panel_ref[...]
    yrow = row_ref[...]
    kp = []
    for r in range(s_ref.shape[0] // B):
        s = s_ref[r * B : (r + 1) * B, :]
        kp.append(kern_tile(s, panel, col_norms(s, scale), yrow))
    acc_ref[...] += jnp.dot(k_ref[...], jnp.concatenate(kp, axis=0), preferred_element_type=jnp.float32)

    @pl.when(t == tiles - 1)
    def _():
        side = me & 1
        k = me >> 1
        rows = other_ref.shape[1]
        for d in range(samps // 2):
            at = (k ^ d) * 2
            mine_ref[d] = acc_ref[pl.ds(pl.multiple_of((at + side) * rows, rows), rows), :]
            other_ref[d] = acc_ref[pl.ds(pl.multiple_of((at + 1 - side) * rows, rows), rows), :]


def gram_kernel(me, pieces, kern_own, samples, tile=512):
    samps = len(pieces)
    mc, ns = kern_own.shape
    d = samples.shape[1]
    width = samps * pieces[0].shape[0]
    rows = mc // samps
    inside = pl.BlockSpec(memory_space=pltpu.VMEM)
    half = jax.ShapeDtypeStruct((samps // 2, rows, width), jnp.float32)
    return pl.pallas_call(
        functools.partial(gram_body, tiles=ns // tile),
        grid=(ns // tile,),
        in_specs=[pl.BlockSpec(memory_space=pltpu.SMEM)]
        + [inside] * samps
        + [pl.BlockSpec((mc, tile), lambda t: (0, t)), pl.BlockSpec((tile, d), lambda t: (t, 0))],
        out_specs=(inside, inside, inside),
        out_shape=(half, half, jax.ShapeDtypeStruct((width, d), jnp.bfloat16)),
        scratch_shapes=[pltpu.VMEM((mc, width), jnp.float32), pltpu.VMEM((1, width), jnp.float32)],
        name="gram",
    )(me, *pieces, kern_own, samples)


from jax.sharding import PartitionSpec as P

PANEL = 512
GRAM_SCALE = 64.0


def swap(x, axis, d):
    n = lax.axis_size(axis)
    return lax.ppermute(x, axis, [(i, i ^ d) for i in range(n)])


def panel_pieces(centers):
    ctrs = lax.axis_size("ctr")
    samps = lax.axis_size("samp")
    rows = PANEL // samps
    chunk = lax.dynamic_slice_in_dim(centers, lax.axis_index("samp") * rows, rows, 0)
    got = [lax.ppermute(chunk, "ctr", [(0, d)]) for d in range(1, ctrs)]
    total = got[0]
    for piece in got[1:]:
        total = total + piece
    chunk = jnp.where(lax.axis_index("ctr") == 0, chunk, total)
    return [chunk] + [swap(chunk, "samp", d) for d in range(1, samps)]


def local(samples, centers):
    samp_count = lax.axis_size("samp")
    samp_index = lax.axis_index("samp").astype(jnp.int32)
    ctr_index = lax.axis_index("ctr").astype(jnp.int32)
    mc_dev = centers.shape[0]
    row_dev = mc_dev // samp_count
    own = lax.dynamic_slice_in_dim(centers, samp_index * row_dev, row_dev, 0)
    own = jnp.pad(own, ((0, -row_dev % B), (0, 0)))
    pieces = panel_pieces(centers)
    kern_own = own_kernel(centers, samples)
    other, mine, panel = gram_kernel(samp_index.reshape(1), pieces, kern_own, samples)
    half = mine + swap(other, "samp", 1)
    total = half[0]
    for d in range(1, samp_count // 2):
        total = total + swap(half[d], "samp", 2 * d)
    gram = total * (GRAM_SCALE / (samples.shape[0] * samp_count))
    off = (ctr_index * mc_dev + samp_index * row_dev).reshape(1)
    chol, precond = chol_kernel(off, panel, own)
    return (gram[None], chol[None, :row_dev], precond)


def solution(mesh):
    placed = (P("samp", None), P("ctr", None))
    return jax.shard_map(
        local,
        mesh=mesh,
        in_specs=placed,
        out_specs=(P("ctr", "samp", None), P("ctr", "samp", None), P()),
        check_vma=False,
    )
```

time: 90.5 us -> 79.6 us (0.88)
  matrix products: 11.2 us -> 0 us
  Pallas kernels: 41.4 us -> 48.3 us
  other arithmetic: 6.77 us -> 3.1 us
  waiting for transfers between devices: 7.08 us -> 4.39 us
  local copies, waits for them, and re-layouts: 4.44 us -> 3.12 us
  starting transfers between devices: 18.4 us -> 19.5 us
    pallas_call x0 -> x2, Pallas kernels: none -> 19.1 us  [the longest x1 9.9 us: own_kernel(): pl.pallas_call(own_body, grid=(ns // tile,), in_specs=[pl.BlockSpec((mc,...]
    pallas_call x1, Pallas kernels: 41.4 us -> 29.2 us  [chol_kernel(): pl.pallas_call(functools.partial(body, own=ro), out_shape=(jax.ShapeDtype...]
    dot_general x2 -> x0, matrix products: 11.2 us -> none  [the longest x1 6.88 us: local(): part = jnp.dot(kern_own, kern_panel, preferred_element_type=jnp.float32)]
    ppermute x11, waiting for transfers between devices: 7.07 us -> 2.52 us  [swap(): return lax.ppermute(x, axis, [(i, i ^ d) for i in range(n)])]
    reduce_sum x3 -> x0, other arithmetic: 2.25 us -> none  [the longest x1 1.5 us: kernel_block(): first_sq = jnp.sum(jnp.square(first_set.astype(jnp.float32)), axis=1)]
    ppermute x3, waiting for transfers between devices: 0.01 us -> 1.87 us  [panel_pieces(): got = [lax.ppermute(chunk, 'ctr', [(0, d)]) for d in range(1, ctrs)]]
    slice x1 -> x0, local copies, waits for them, and re-layouts: 1.22 us -> none  [local(): panel = panel_everywhere(centers[:PANEL])]
    ppermute x11, starting transfers between devices: 10.1 us -> 11.2 us  [swap(): return lax.ppermute(x, axis, [(i, i ^ d) for i in range(n)])]
  transfers between devices with their start and end apart: 14 -> 14, of which waited for: 4 -> 3; matrix products, arithmetic and copies ran while one was open for 3% -> 2% of each run, Pallas kernels for 46% -> 49%
where the time goes in v1:
time: 79.6 us; the launch traced here: 79.2 us
  Pallas kernels  48.3 us (61%)
  starting transfers between devices  19.5 us (24%)
  waiting for transfers between devices  4.39 us (6%)
  local copies, waits for them, and re-layouts  3.12 us (4%)
  other arithmetic  3.1 us (4%)
  between operations  0.8 us (1%)
    pallas_call x1, Pallas kernels, chol_kernel(): pl.pallas_call(functools.partial(body, own=ro), out_shape=(jax.ShapeDtype...  29.2 us
    ppermute x11, starting transfers between devices, swap(): return lax.ppermute(x, axis, [(i, i ^ d) for i in range(n)])  11.2 us
    pallas_call x1, Pallas kernels, own_kernel(): pl.pallas_call(own_body, grid=(ns // tile,), in_specs=[pl.BlockSpec((mc,...  9.9 us
    pallas_call x1, Pallas kernels, gram_kernel(): pl.pallas_call(functools.partial(gram_body, tiles=ns // tile), grid=(ns /...  9.22 us
    ppermute x3, starting transfers between devices, panel_pieces(): got = [lax.ppermute(chunk, 'ctr', [(0, d)]) for d in range(1, ctrs)]  8.3 us
    ppermute x11, waiting for transfers between devices, swap(): return lax.ppermute(x, axis, [(i, i ^ d) for i in range(n)])  2.52 us
    ppermute x3, waiting for transfers between devices, panel_pieces(): got = [lax.ppermute(chunk, 'ctr', [(0, d)]) for d in range(1, ctrs)]  1.87 us
  transfers between devices with their start and end apart: 14, of which 3 were waited for; matrix products, arithmetic and copies ran while one was open for 2% of the time, Pallas kernels for 49%

profile of v1, /device:TPU:0, one launch (start us, length us, event | category | flops | bytes accessed | tf_op | source)
XLA Modules:
  0.0 79.2 jit_solution(12164771293178728634)
XLA Ops:
  0.6 0.8 %constant_dynamic-slice_fusion.1 = bf16[64,512]{1,0:T(8,128)(2,1)S(1)} fusion(bf16[1024,512]{1,0:T(8,128)(2,1)} %c_ref.1, s32[]{:T(128)S(6)} %select_n.15), kind=kLoop, calls=%fused_computation.11 | loop fusion | bytes 131076 | tf_op jit(solution)/shard_map/dynamic_slice | solution.py:304
  1.5 4.9 %collective-permute-start = (bf16[64,512]{1,0:T(8,128)(2,1)S(1)}, bf16[64,512]{1,0:T(8,128)(2,1)S(1)}, u32[]{:S(2)}, u32[]{:S(2)}) collective-permute-start(bf16[64,512]{1,0:T(8,128)(2,1)S(1)} %constant_dynamic-slice_fusion.1), channel_id=1, source_target_pairs={{0,1},{4,5},{8,9},{12,13},{16,17},{20,21},{24,25},{28,29}} | collective-permute-start | bytes 196616 | tf_op jit(solution)/shard_map/ppermute | solution.py:305
  6.4 1.7 %collective-permute-start.1 = (bf16[64,512]{1,0:T(8,128)(2,1)S(1)}, bf16[64,512]{1,0:T(8,128)(2,1)S(1)}, u32[]{:S(2)}, u32[]{:S(2)}) collective-permute-start(bf16[64,512]{1,0:T(8,128)(2,1)S(1)} %constant_dynamic-slice_fusion.1), channel_id=1, source_target_pairs={{0,2},{4,6},{8,10},{12,14},{16,18},{20,22},{24,26},{28,30}} | collective-permute-start | bytes 196616 | tf_op jit(solution)/shard_map/ppermute | solution.py:305
  8.1 1.7 %collective-permute-start.2 = (bf16[64,512]{1,0:T(8,128)(2,1)S(1)}, bf16[64,512]{1,0:T(8,128)(2,1)S(1)}, u32[]{:S(2)}, u32[]{:S(2)}) collective-permute-start(bf16[64,512]{1,0:T(8,128)(2,1)S(1)} %constant_dynamic-slice_fusion.1), channel_id=1, source_target_pairs={{0,3},{4,7},{8,11},{12,15},{16,19},{20,23},{24,27},{28,31}} | collective-permute-start | bytes 196616 | tf_op jit(solution)/shard_map/ppermute | solution.py:305
  9.8 0.0 collective-permute-done
  9.8 0.2 collective-permute-done.1
  10.0 1.7 %collective-permute-done.2 = bf16[64,512]{1,0:T(8,128)(2,1)S(1)} collective-permute-done((bf16[64,512]{1,0:T(8,128)(2,1)S(1)}, bf16[64,512]{1,0:T(8,128)(2,1)S(1)}, u32[]{:S(2)}, u32[]{:S(2)}) %collective-permute-start.2) | collective-permute-done | bytes 65568 | tf_op jit(solution)/shard_map/ppermute | solution.py:305
  11.7 0.9 %add_select_fusion.refs_0_ = bf16[64,512]{1,0:T(8,128)(2,1)S(1)} fusion(bf16[64,512]{1,0:T(8,128)(2,1)S(1)} %collective-permute-done.2, bf16[64,512]{1,0:T(8,128)(2,1)S(1)} %collective-permute-done, bf16[64,512]{1,0:T(8,128)(2,1)S(1)} %collective-permute-done.1, pred[]{:T(512)S(6)} %eq.3, bf16[1024,512]{1,0:T(8,128)(2,1)} %c_ref.1, s32[]{:T(128)S(6)} %select_n.15), kind=kLoop, calls=%fused_computation.9 | loop fusion | flops 229376 | bytes 327685 | tf_op jit(solution)/shard_map/jit(_where)/select_n | solution.py:309
  12.6 0.0 copy-start
  12.6 0.1 collective-permute-start.3
  12.7 1.6 %collective-permute-start.4 = (bf16[64,512]{1,0:T(8,128)(2,1)S(1)}, bf16[64,512]{1,0:T(8,128)(2,1)S(1)}, u32[]{:S(2)}, u32[]{:S(2)}) collective-permute-start(bf16[64,512]{1,0:T(8,128)(2,1)S(1)} %add_select_fusion.refs_0_), channel_id=1, source_target_pairs={{0,8},{4,12},{8,0},{12,4},{16,24},{20,28},{24,16},{28,20},{1,9},{5... | collective-permute-start | bytes 196616 | tf_op jit(solution)/shard_map/ppermute | solution.py:297
  14.2 0.3 collective-permute-start.5
  14.5 1.5 %collective-permute-start.6 = (bf16[64,512]{1,0:T(8,128)(2,1)S(1)}, bf16[64,512]{1,0:T(8,128)(2,1)S(1)}, u32[]{:S(2)}, u32[]{:S(2)}) collective-permute-start(bf16[64,512]{1,0:T(8,128)(2,1)S(1)} %add_select_fusion.refs_0_), channel_id=1, source_target_pairs={{0,16},{4,20},{8,24},{12,28},{16,0},{20,4},{24,8},{28,12},{1,17},{... | collective-permute-start | bytes 196616 | tf_op jit(solution)/shard_map/ppermute | solution.py:297
  16.0 0.2 collective-permute-start.7
  16.2 0.0 collective-permute-done.3.refs_1_
  16.2 2.4 %collective-permute-start.8 = (bf16[64,512]{1,0:T(8,128)(2,1)S(1)}, bf16[64,512]{1,0:T(8,128)(2,1)S(1)}, u32[]{:S(2)}, u32[]{:S(2)}) collective-permute-start(bf16[64,512]{1,0:T(8,128)(2,1)S(1)} %add_select_fusion.refs_0_), channel_id=1, source_target_pairs={{0,24},{4,28},{8,16},{12,20},{16,8},{20,12},{24,0},{28,4},{1,25},{... | collective-permute-start | bytes 196616 | tf_op jit(solution)/shard_map/ppermute | solution.py:297
  18.7 0.0 collective-permute-done.4.refs_2_
  18.7 0.2 collective-permute-start.9
  18.9 9.9 %kern_own.1.refs_8_ = bf16[1024,2048]{1,0:T(8,128)(2,1)} custom-call(bf16[1024,512]{1,0:T(8,128)(2,1)} %c_ref.1, bf16[2048,512]{1,0:T(8,128)(2,1)} %refs_9_.1), custom_call_target="tpu_custom_call" | custom-call | tf_op jit(solution)/shard_map/kern_own/pallas_call | solution.py:223
  28.8 0.0 collective-permute-done.5.refs_3_
  28.8 0.0 collective-permute-done.6.refs_4_
  28.8 0.0 copy-start.4
  28.8 0.0 collective-permute-done.7.refs_5_
  28.9 0.0 copy-start.5
  28.9 0.0 collective-permute-done.8.refs_6_
  28.9 0.0 copy-start.6
  28.9 0.0 collective-permute-done.9.refs_7_
  28.9 0.0 copy-start.7
  28.9 0.0 copy-done
  28.9 0.5 copy-done.3
  29.5 0.0 copy-done.4
  29.5 0.0 copy-done.5
  29.5 0.0 copy-done.6
  29.5 0.0 copy-done.7
  29.6 9.2 %gram.1 = (f32[4,128,512]{2,1,0:T(8,128)}, f32[4,128,512]{2,1,0:T(8,128)}, bf16[512,512]{1,0:T(8,128)(2,1)}) custom-call(s32[1]{0:T(128)} %bitcast.me_ref, bf16[64,512]{1,0:T(8,128)(2,1)} %copy-done, bf16[64,512]{1,0:T(8,128)(2,1)} %copy-done.1, bf16[64,512]{1,0:T(8,128)(2,1)} %copy-done.2, bf16[64,512]{1,0:T(8,128)(2,1)} %copy-done.3, ...), custom_call_target="tpu_custom_call" | custom-call | tf_op jit(solution)/shard_map/gram/pallas_call | solution.py:276
  38.8 1.3 %collective-permute-start.10 = (f32[4,128,512]{2,1,0:T(8,128)}, f32[4,128,512]{2,1,0:T(8,128)S(1)}, u32[]{:S(2)}, u32[]{:S(2)}) collective-permute-start(f32[4,128,512]{2,1,0:T(8,128)} %get-tuple-element.9), channel_id=1, source_target_pairs={{0,4},{4,0},{8,12},{12,8},{16,20},{20,16},{24,28},{28,24},{1,5},{5... | collective-permute-start | bytes 3145736 | tf_op jit(solution)/shard_map/ppermute | solution.py:297
  40.1 2.5 %collective-permute-done.10 = f32[4,128,512]{2,1,0:T(8,128)S(1)} collective-permute-done((f32[4,128,512]{2,1,0:T(8,128)}, f32[4,128,512]{2,1,0:T(8,128)S(1)}, u32[]{:S(2)}, u32[]{:S(2)}) %collective-permute-start.10) | collective-permute-done | bytes 1048608 | tf_op jit(solution)/shard_map/ppermute | solution.py:297
  42.6 1.4 %add.30 = f32[4,128,512]{2,1,0:T(8,128)S(1)} add(f32[4,128,512]{2,1,0:T(8,128)} %get-tuple-element.8, f32[4,128,512]{2,1,0:T(8,128)S(1)} %collective-permute-done.10) | non-fusion elementwise | flops 262144 | bytes 3145728 | tf_op jit(solution)/shard_map/add | solution.py:324
  44.1 0.1 slice_bitcast_fusion.2
  44.1 0.6 collective-permute-start.11
  44.7 1.5 %collective-permute-start.12 = (f32[128,512]{1,0:T(8,128)S(1)}, f32[128,512]{1,0:T(8,128)S(1)}, u32[]{:S(2)}, u32[]{:S(2)}) collective-permute-start(f32[128,512]{1,0:T(8,128)S(1)} %get-tuple-element.15), channel_id=1, source_target_pairs={{0,16},{4,20},{8,24},{12,28},{16,0},{20,4},{24,8},{28,12},{1,17},{... | collective-permute-start | bytes 786440 | tf_op jit(solution)/shard_map/ppermute | solution.py:297
  46.2 1.5 %collective-permute-start.13 = (f32[128,512]{1,0:T(8,128)S(1)}, f32[128,512]{1,0:T(8,128)S(1)}, u32[]{:S(2)}, u32[]{:S(2)}) collective-permute-start(f32[128,512]{1,0:T(8,128)S(1)} %get-tuple-element.14), channel_id=1, source_target_pairs={{0,24},{4,28},{8,16},{12,20},{16,8},{20,12},{24,0},{28,4},{1,25},{... | collective-permute-start | bytes 786440 | tf_op jit(solution)/shard_map/ppermute | solution.py:297
  47.7 1.6 %constant_dynamic-slice_fusion.own_ref = bf16[128,512]{1,0:T(8,128)(2,1)} fusion(bf16[1024,512]{1,0:T(8,128)(2,1)} %c_ref.1, s32[]{:T(128)S(6)} %select_n.17), kind=kLoop, calls=%fused_computation.10 | loop fusion | bytes 262148 | tf_op jit(solution)/shard_map/dynamic_slice | solution.py:319
  49.2 29.2 %chol.1 = (f32[128,512]{1,0:T(8,128)}, f32[512,512]{1,0:T(8,128)}) custom-call(s32[1]{0:T(128)} %bitcast.6.off_ref, bf16[512,512]{1,0:T(8,128)(2,1)} %get-tuple-element.10.panel_ref, bf16[128,512]{1,0:T(8,128)(2,1)} %constant_dynamic-slice_fusion.own_ref), custom_call_target="tpu_custom_call" | custom-call | tf_op jit(solution)/shard_map/chol/pallas_call | solution.py:180
  78.4 0.0 collective-permute-done.11
  78.4 0.0 collective-permute-done.12
  78.4 0.0 collective-permute-done.13
  78.4 0.8 fusion.4
  (5 shorter events, 0.0 us)
Async XLA Ops:
  1.5 8.3 %collective-permute-start = (bf16[64,512]{1,0:T(8,128)(2,1)S(1)}, bf16[64,512]{1,0:T(8,128)(2,1)S(1)}, u32[]{:S(2)}, u32[]{:S(2)}) collective-permute-start(bf16[64,512]{1,0:T(8,128)(2,1)S(1)} %constant_dynamic-slice_fusion.1), channel_id=1, source_target_pairs={{0,1},{4,5},{8,9},{12,13},{16,17},{20,21},{24,25},{28,29}} | collective-permute-start | bytes 196616 | tf_op jit(solution)/shard_map/ppermute | solution.py:305
  6.4 3.6 %collective-permute-start.1 = (bf16[64,512]{1,0:T(8,128)(2,1)S(1)}, bf16[64,512]{1,0:T(8,128)(2,1)S(1)}, u32[]{:S(2)}, u32[]{:S(2)}) collective-permute-start(bf16[64,512]{1,0:T(8,128)(2,1)S(1)} %constant_dynamic-slice_fusion.1), channel_id=1, source_target_pairs={{0,2},{4,6},{8,10},{12,14},{16,18},{20,22},{24,26},{28,30}} | collective-permute-start | bytes 196616 | tf_op jit(solution)/shard_map/ppermute | solution.py:305
  8.1 3.6 %collective-permute-start.2 = (bf16[64,512]{1,0:T(8,128)(2,1)S(1)}, bf16[64,512]{1,0:T(8,128)(2,1)S(1)}, u32[]{:S(2)}, u32[]{:S(2)}) collective-permute-start(bf16[64,512]{1,0:T(8,128)(2,1)S(1)} %constant_dynamic-slice_fusion.1), channel_id=1, source_target_pairs={{0,3},{4,7},{8,11},{12,15},{16,19},{20,23},{24,27},{28,31}} | collective-permute-start | bytes 196616 | tf_op jit(solution)/shard_map/ppermute | solution.py:305
  12.6 16.3 %copy-start = (bf16[64,512]{1,0:T(8,128)(2,1)}, bf16[64,512]{1,0:T(8,128)(2,1)S(1)}, u32[]{:S(2)}) copy-start(bf16[64,512]{1,0:T(8,128)(2,1)S(1)} %add_select_fusion.refs_0_) | copy-start | bytes 196612
  12.6 3.6 %collective-permute-start.3 = (bf16[64,512]{1,0:T(8,128)(2,1)S(1)}, bf16[64,512]{1,0:T(8,128)(2,1)S(1)}, u32[]{:S(2)}, u32[]{:S(2)}) collective-permute-start(bf16[64,512]{1,0:T(8,128)(2,1)S(1)} %add_select_fusion.refs_0_), channel_id=1, source_target_pairs={{0,4},{4,0},{8,12},{12,8},{16,20},{20,16},{24,28},{28,24},{1,5},{5... | collective-permute-start | bytes 196616 | tf_op jit(solution)/shard_map/ppermute | solution.py:297
  12.7 6.0 %collective-permute-start.4 = (bf16[64,512]{1,0:T(8,128)(2,1)S(1)}, bf16[64,512]{1,0:T(8,128)(2,1)S(1)}, u32[]{:S(2)}, u32[]{:S(2)}) collective-permute-start(bf16[64,512]{1,0:T(8,128)(2,1)S(1)} %add_select_fusion.refs_0_), channel_id=1, source_target_pairs={{0,8},{4,12},{8,0},{12,4},{16,24},{20,28},{24,16},{28,20},{1,9},{5... | collective-permute-start | bytes 196616 | tf_op jit(solution)/shard_map/ppermute | solution.py:297
  14.2 14.6 %collective-permute-start.5 = (bf16[64,512]{1,0:T(8,128)(2,1)S(1)}, bf16[64,512]{1,0:T(8,128)(2,1)S(1)}, u32[]{:S(2)}, u32[]{:S(2)}) collective-permute-start(bf16[64,512]{1,0:T(8,128)(2,1)S(1)} %add_select_fusion.refs_0_), channel_id=1, source_target_pairs={{0,12},{4,8},{8,4},{12,0},{16,28},{20,24},{24,20},{28,16},{1,13},{... | collective-permute-start | bytes 196616 | tf_op jit(solution)/shard_map/ppermute | solution.py:297
  14.5 14.3 %collective-permute-start.6 = (bf16[64,512]{1,0:T(8,128)(2,1)S(1)}, bf16[64,512]{1,0:T(8,128)(2,1)S(1)}, u32[]{:S(2)}, u32[]{:S(2)}) collective-permute-start(bf16[64,512]{1,0:T(8,128)(2,1)S(1)} %add_select_fusion.refs_0_), channel_id=1, source_target_pairs={{0,16},{4,20},{8,24},{12,28},{16,0},{20,4},{24,8},{28,12},{1,17},{... | collective-permute-start | bytes 196616 | tf_op jit(solution)/shard_map/ppermute | solution.py:297
  16.0 12.8 %collective-permute-start.7 = (bf16[64,512]{1,0:T(8,128)(2,1)S(1)}, bf16[64,512]{1,0:T(8,128)(2,1)S(1)}, u32[]{:S(2)}, u32[]{:S(2)}) collective-permute-start(bf16[64,512]{1,0:T(8,128)(2,1)S(1)} %add_select_fusion.refs_0_), channel_id=1, source_target_pairs={{0,20},{4,16},{8,28},{12,24},{16,4},{20,0},{24,12},{28,8},{1,21},{... | collective-permute-start | bytes 196616 | tf_op jit(solution)/shard_map/ppermute | solution.py:297
  16.2 12.7 %copy-start.1 = (bf16[64,512]{1,0:T(8,128)(2,1)}, bf16[64,512]{1,0:T(8,128)(2,1)S(1)}, u32[]{:S(2)}) copy-start(bf16[64,512]{1,0:T(8,128)(2,1)S(1)} %collective-permute-done.3.refs_1_) | copy-start | bytes 196612
  16.2 12.6 %collective-permute-start.8 = (bf16[64,512]{1,0:T(8,128)(2,1)S(1)}, bf16[64,512]{1,0:T(8,128)(2,1)S(1)}, u32[]{:S(2)}, u32[]{:S(2)}) collective-permute-start(bf16[64,512]{1,0:T(8,128)(2,1)S(1)} %add_select_fusion.refs_0_), channel_id=1, source_target_pairs={{0,24},{4,28},{8,16},{12,20},{16,8},{20,12},{24,0},{28,4},{1,25},{... | collective-permute-start | bytes 196616 | tf_op jit(solution)/shard_map/ppermute | solution.py:297
  18.7 10.2 %copy-start.2 = (bf16[64,512]{1,0:T(8,128)(2,1)}, bf16[64,512]{1,0:T(8,128)(2,1)S(1)}, u32[]{:S(2)}) copy-start(bf16[64,512]{1,0:T(8,128)(2,1)S(1)} %collective-permute-done.4.refs_2_) | copy-start | bytes 196612
  18.7 10.2 %collective-permute-start.9 = (bf16[64,512]{1,0:T(8,128)(2,1)S(1)}, bf16[64,512]{1,0:T(8,128)(2,1)S(1)}, u32[]{:S(2)}, u32[]{:S(2)}) collective-permute-start(bf16[64,512]{1,0:T(8,128)(2,1)S(1)} %add_select_fusion.refs_0_), channel_id=1, source_target_pairs={{0,28},{4,24},{8,20},{12,16},{16,12},{20,8},{24,4},{28,0},{1,29},{... | collective-permute-start | bytes 196616 | tf_op jit(solution)/shard_map/ppermute | solution.py:297
  28.8 0.6 copy-start.3
  28.8 0.7 copy-start.4
  28.9 0.6 copy-start.5
  28.9 0.6 copy-start.6
  28.9 0.7 copy-start.7
  38.8 3.8 %collective-permute-start.10 = (f32[4,128,512]{2,1,0:T(8,128)}, f32[4,128,512]{2,1,0:T(8,128)S(1)}, u32[]{:S(2)}, u32[]{:S(2)}) collective-permute-start(f32[4,128,512]{2,1,0:T(8,128)} %get-tuple-element.9), channel_id=1, source_target_pairs={{0,4},{4,0},{8,12},{12,8},{16,20},{20,16},{24,28},{28,24},{1,5},{5... | collective-permute-start | bytes 3145736 | tf_op jit(solution)/shard_map/ppermute | solution.py:297
  44.1 34.3 %collective-permute-start.11 = (f32[128,512]{1,0:T(8,128)S(1)}, f32[128,512]{1,0:T(8,128)S(1)}, u32[]{:S(2)}, u32[]{:S(2)}) collective-permute-start(f32[128,512]{1,0:T(8,128)S(1)} %get-tuple-element.13), channel_id=1, source_target_pairs={{0,8},{4,12},{8,0},{12,4},{16,24},{20,28},{24,16},{28,20},{1,9},{5... | collective-permute-start | bytes 786440 | tf_op jit(solution)/shard_map/ppermute | solution.py:297
  44.7 33.7 %collective-permute-start.12 = (f32[128,512]{1,0:T(8,128)S(1)}, f32[128,512]{1,0:T(8,128)S(1)}, u32[]{:S(2)}, u32[]{:S(2)}) collective-permute-start(f32[128,512]{1,0:T(8,128)S(1)} %get-tuple-element.15), channel_id=1, source_target_pairs={{0,16},{4,20},{8,24},{12,28},{16,0},{20,4},{24,8},{28,12},{1,17},{... | collective-permute-start | bytes 786440 | tf_op jit(solution)/shard_map/ppermute | solution.py:297
  46.2 32.2 %collective-permute-start.13 = (f32[128,512]{1,0:T(8,128)S(1)}, f32[128,512]{1,0:T(8,128)S(1)}, u32[]{:S(2)}, u32[]{:S(2)}) collective-permute-start(f32[128,512]{1,0:T(8,128)S(1)} %get-tuple-element.14), channel_id=1, source_target_pairs={{0,24},{4,28},{8,16},{12,20},{16,8},{20,12},{24,0},{28,4},{1,25},{... | collective-permute-start | bytes 786440 | tf_op jit(solution)/shard_map/ppermute | solution.py:297

commit v2 on v1

--- a/solution.py
+++ b/solution.py
@@ -181,109 +181,121 @@
         out_shape=(jax.ShapeDtypeStruct((ro,n),f32),jax.ShapeDtypeStruct((n,n),f32)),
         in_specs=[pl.BlockSpec(memory_space=pltpu.SMEM),vm,vm],out_specs=(vm,vm),
         scratch_shapes=[V(nb,nj),V(nb+1,nj),V(nj,nb+1),V(nb,nb),V(nb+1,nb),V(nb,nb+1),V(nb)]+[V()]*8,
+        compiler_params=pltpu.CompilerParams(vmem_limit_bytes=24<<20),
         name='chol')(off,panel,own)
 
 
 LOG2E = 1.4426950408889634
 
 
-def row_norms(x, scale):
+def near(x):
+    return pltpu.with_memory_space_constraint(x, pltpu.VMEM)
+
+
+def square_parts(x):
     sq = jnp.square(x.astype(jnp.float32))
     hi = sq.astype(jnp.bfloat16)
-    lo = (sq - hi.astype(jnp.float32)).astype(jnp.bfloat16)
+    return hi, (sq - hi.astype(jnp.float32)).astype(jnp.bfloat16)
+
+
+def nt(a, b):
+    return lax.dot_general(a, b, (((1,), (1,)), ((), ())), preferred_element_type=jnp.float32)
+
+
+def row_norms(x, scale):
+    hi, lo = square_parts(x)
     one = jnp.ones((8, x.shape[1]), jnp.bfloat16)
-    dims = (((1,), (1,)), ((), ()))
-    out = lax.dot_general(one, hi, dims, preferred_element_type=jnp.float32)
-    out = out + lax.dot_general(one, lo, dims, preferred_element_type=jnp.float32)
-    return out[0:1] * scale
+    return (nt(one, hi) + nt(one, lo))[0:1] * scale
 
 
 def col_norms(x, scale):
-    return jnp.sum(jnp.square(x.astype(jnp.float32)), axis=1, keepdims=True) * scale
+    hi, lo = square_parts(x)
+    one = jnp.ones((x.shape[1], B), jnp.bfloat16)
+    dot = lambda a: jnp.dot(a, one, preferred_element_type=jnp.float32)
+    return (dot(hi) + dot(lo)) * scale
 
 
 def kern_tile(x, y, xcol, yrow):
-    dot = lax.dot_general(x, y, (((1,), (1,)), ((), ())), preferred_element_type=jnp.float32)
-    arg = jnp.minimum(dot * (4.0 * LOG2E / x.shape[1]) + (xcol + yrow), 0.0)
+    dot = nt(x, y)
+    both = jnp.concatenate([xcol] * (y.shape[0] // B), axis=1) + yrow
+    arg = jnp.minimum(dot * (4.0 * LOG2E / x.shape[1]) + both, 0.0)
     return jnp.exp2(arg).astype(jnp.bfloat16)
 
 
-def own_body(c_ref, s_ref, o_ref):
+def own_body(me_ref, c_ref, s_ref, k_ref, norm_ref, own_ref, *, row_dev):
     scale = -2.0 * LOG2E / c_ref.shape[1]
-    s = s_ref[...]
-    yrow = row_norms(s, scale)
-    for r in range(c_ref.shape[0] // B):
-        c = c_ref[r * B : (r + 1) * B, :]
-        o_ref[r * B : (r + 1) * B, :] = kern_tile(c, s, col_norms(c, scale), yrow)
-
-
-def own_kernel(centers, samples, tile=512):
+    at = pl.multiple_of(me_ref[0] * row_dev, row_dev)
+    own_ref[0:row_dev, :] = c_ref[pl.ds(at, row_dev), :]
+    if row_dev < own_ref.shape[0]:
+        own_ref[row_dev:, :] = jnp.zeros((own_ref.shape[0] - row_dev, own_ref.shape[1]), own_ref.dtype)
+    c = c_ref[...]
+    ccol = col_norms(c, scale)
+    tile = 2 * B
+    for t in range(0, s_ref.shape[0], tile):
+        s = s_ref[t : t + tile, :]
+        norm_ref[t : t + tile, :] = col_norms(s, scale)
+        k_ref[:, t : t + tile] = kern_tile(c, s, ccol, row_norms(s, scale))
+
+
+def own_kernel(me, centers, samples, row_dev):
     mc, d = centers.shape
     ns = samples.shape[0]
+    inside = pl.BlockSpec(memory_space=pltpu.VMEM)
     return pl.pallas_call(
-        own_body,
-        grid=(ns // tile,),
-        in_specs=[pl.BlockSpec((mc, d), lambda t: (0, 0)), pl.BlockSpec((tile, d), lambda t: (t, 0))],
-        out_specs=pl.BlockSpec((mc, tile), lambda t: (0, t)),
-        out_shape=jax.ShapeDtypeStruct((mc, ns), jnp.bfloat16),
+        functools.partial(own_body, row_dev=row_dev),
+        in_specs=[pl.BlockSpec(memory_space=pltpu.SMEM), inside, inside],
+        out_specs=(inside, inside, inside),
+        out_shape=(
+            pltpu.VMEM((mc, ns), jnp.bfloat16),
+            pltpu.VMEM((ns, B), jnp.float32),
+            pltpu.VMEM((row_dev + -row_dev % B, d), jnp.bfloat16),
+        ),
+        compiler_params=pltpu.CompilerParams(vmem_limit_bytes=16 << 20),
         name="kern_own",
-    )(centers, samples)
-
-
-def gram_body(me_ref, *refs, tiles):
-    pieces, (k_ref, s_ref, other_ref, mine_ref, panel_ref, acc_ref, row_ref) = refs[:-7], refs[-7:]
-    samps = len(pieces)
-    t = pl.program_id(0)
+    )(me, near(centers), samples)
+
+
+def gram_body(me_ref, *refs, samps, tile):
+    pieces, (k_ref, s_ref, norm_ref) = refs[:samps], refs[samps : samps + 3]
+    panel_ref, other_ref = refs[samps + 3 : samps + 5]
+    mine, (acc_ref, kp_ref) = refs[samps + 5 : -2], refs[-2:]
     me = me_ref[0]
-    scale = -2.0 * LOG2E / s_ref.shape[1]
-
-    @pl.when(t == 0)
-    def _():
-        rows = pieces[0].shape[0]
-        for d in range(samps):
-            at = pl.multiple_of((me ^ d) * rows, rows)
-            panel_ref[pl.ds(at, rows), :] = pieces[d][...]
-        row_ref[...] = row_norms(panel_ref[...], scale)
-        acc_ref[...] = jnp.zeros_like(acc_ref)
-
+    rows = pieces[0].shape[0]
+    for d in range(samps):
+        panel_ref[pl.ds(pl.multiple_of((me ^ d) * rows, rows), rows), :] = pieces[d][...]
     panel = panel_ref[...]
-    yrow = row_ref[...]
-    kp = []
-    for r in range(s_ref.shape[0] // B):
-        s = s_ref[r * B : (r + 1) * B, :]
-        kp.append(kern_tile(s, panel, col_norms(s, scale), yrow))
-    acc_ref[...] += jnp.dot(k_ref[...], jnp.concatenate(kp, axis=0), preferred_element_type=jnp.float32)
-
-    @pl.when(t == tiles - 1)
-    def _():
-        side = me & 1
-        k = me >> 1
-        rows = other_ref.shape[1]
-        for d in range(samps // 2):
-            at = (k ^ d) * 2
-            mine_ref[d] = acc_ref[pl.ds(pl.multiple_of((at + side) * rows, rows), rows), :]
-            other_ref[d] = acc_ref[pl.ds(pl.multiple_of((at + 1 - side) * rows, rows), rows), :]
-
-
-def gram_kernel(me, pieces, kern_own, samples, tile=512):
+    yrow = row_norms(panel, -2.0 * LOG2E / s_ref.shape[1])
+    for t in range(0, s_ref.shape[0], tile):
+        kp_ref[t : t + tile, :] = kern_tile(s_ref[t : t + tile, :], panel, norm_ref[t : t + tile, :], yrow)
+    acc_ref[...] = jnp.dot(k_ref[...], kp_ref[...], preferred_element_type=jnp.float32)
+    side = me & 1
+    k = me >> 1
+    rows = other_ref.shape[1]
+    for d in range(samps // 2):
+        at = (k ^ d) * 2
+        mine[d][...] = acc_ref[pl.ds(pl.multiple_of((at + side) * rows, rows), rows), :]
+        other_ref[d] = acc_ref[pl.ds(pl.multiple_of((at + 1 - side) * rows, rows), rows), :]
+
+
+def gram_kernel(me, pieces, kern_own, samples, norms, tile=512):
     samps = len(pieces)
     mc, ns = kern_own.shape
-    d = samples.shape[1]
     width = samps * pieces[0].shape[0]
-    rows = mc // samps
     inside = pl.BlockSpec(memory_space=pltpu.VMEM)
-    half = jax.ShapeDtypeStruct((samps // 2, rows, width), jnp.float32)
+    shape = (mc // samps, width)
     return pl.pallas_call(
-        functools.partial(gram_body, tiles=ns // tile),
-        grid=(ns // tile,),
-        in_specs=[pl.BlockSpec(memory_space=pltpu.SMEM)]
-        + [inside] * samps
-        + [pl.BlockSpec((mc, tile), lambda t: (0, t)), pl.BlockSpec((tile, d), lambda t: (t, 0))],
-        out_specs=(inside, inside, inside),
-        out_shape=(half, half, jax.ShapeDtypeStruct((width, d), jnp.bfloat16)),
-        scratch_shapes=[pltpu.VMEM((mc, width), jnp.float32), pltpu.VMEM((1, width), jnp.float32)],
+        functools.partial(gram_body, samps=samps, tile=tile),
+        in_specs=[pl.BlockSpec(memory_space=pltpu.SMEM)] + [inside] * (samps + 3),
+        out_specs=(inside,) * (2 + samps // 2),
+        out_shape=(
+            pltpu.VMEM((width, samples.shape[1]), jnp.bfloat16),
+            pltpu.VMEM((samps // 2,) + shape, jnp.float32),
+        )
+        + (pltpu.VMEM(shape, jnp.float32),) * (samps // 2),
+        scratch_shapes=[pltpu.VMEM((mc, width), jnp.float32), pltpu.VMEM((ns, width), jnp.bfloat16)],
+        compiler_params=pltpu.CompilerParams(vmem_limit_bytes=16 << 20),
         name="gram",
-    )(me, *pieces, kern_own, samples)
+    )(me, *[near(x) for x in pieces], kern_own, samples, norms)
 
 
 from jax.sharding import PartitionSpec as P
@@ -316,12 +328,13 @@
     ctr_index = lax.axis_index("ctr").astype(jnp.int32)
     mc_dev = centers.shape[0]
     row_dev = mc_dev // samp_count
-    own = lax.dynamic_slice_in_dim(centers, samp_index * row_dev, row_dev, 0)
-    own = jnp.pad(own, ((0, -row_dev % B), (0, 0)))
+    me = samp_index.reshape(1)
+    samples = near(samples)
     pieces = panel_pieces(centers)
-    kern_own = own_kernel(centers, samples)
-    other, mine, panel = gram_kernel(samp_index.reshape(1), pieces, kern_own, samples)
-    half = mine + swap(other, "samp", 1)
+    kern_own, norms, own = own_kernel(me, centers, samples, row_dev)
+    panel, other, *mine = gram_kernel(me, pieces, kern_own, samples, norms)
+    other = swap(other, "samp", 1)
+    half = [mine[d] + other[d] for d in range(samp_count // 2)]
     total = half[0]
     for d in range(1, samp_count // 2):
         total = total + swap(half[d], "samp", 2 * d)

time: 79.6 us -> 69.9 us (0.88)
  Pallas kernels: 48.3 us -> 37.8 us
  other arithmetic: 3.1 us -> 1.84 us
  waiting for transfers between devices: 4.39 us -> 5.38 us
    pallas_call x2, Pallas kernels: 19.1 us -> 9.6 us  [the longest x1 5.31 us: own_kernel(): pl.pallas_call(functools.partial(own_body, row_dev=row_dev), in_specs=[pl...]
    unnamed x16 -> x6, local copies, waits for them, and re-layouts: 0.65 us -> 2.82 us
    dynamic_slice x1 -> x0, local copies, waits for them, and re-layouts: 1.57 us -> none  [local(): own = lax.dynamic_slice_in_dim(centers, samp_index * row_dev, row_dev, 0)]
    add x1, other arithmetic: 1.43 us -> 0.14 us  [local(): half = [mine[d] + other[d] for d in range(samp_count // 2)]]
    ppermute x3, starting transfers between devices: 8.3 us -> 9.56 us  [panel_pieces(): got = [lax.ppermute(chunk, 'ctr', [(0, d)]) for d in range(1, ctrs)]]
    pallas_call x1, Pallas kernels: 29.2 us -> 28.2 us  [chol_kernel(): pl.pallas_call(functools.partial(body, own=ro), out_shape=(jax.ShapeDtype...]
    ppermute x11, waiting for transfers between devices: 2.52 us -> 3.42 us  [swap(): return lax.ppermute(x, axis, [(i, i ^ d) for i in range(n)])]
  transfers between devices with their start and end apart: 14 -> 14, of which waited for: 3 -> 5; matrix products, arithmetic and copies ran while one was open for 2% -> 0% of each run, Pallas kernels for 49% -> 48%
where the time goes in v2:
time: 69.9 us; the launch traced here: 69.6 us
  Pallas kernels  37.8 us (54%)
  starting transfers between devices  20.1 us (29%)
  waiting for transfers between devices  5.38 us (8%)
  local copies, waits for them, and re-layouts  3.67 us (5%)
  other arithmetic  1.84 us (3%)
  between operations  0.76 us (1%)
    pallas_call x1, Pallas kernels, chol_kernel(): pl.pallas_call(functools.partial(body, own=ro), out_shape=(jax.ShapeDtype...  28.2 us
    ppermute x11, starting transfers between devices, swap(): return lax.ppermute(x, axis, [(i, i ^ d) for i in range(n)])  10.6 us
    ppermute x3, starting transfers between devices, panel_pieces(): got = [lax.ppermute(chunk, 'ctr', [(0, d)]) for d in range(1, ctrs)]  9.56 us
    pallas_call x1, Pallas kernels, own_kernel(): pl.pallas_call(functools.partial(own_body, row_dev=row_dev), in_specs=[pl...  5.31 us
    pallas_call x1, Pallas kernels, gram_kernel(): pl.pallas_call(functools.partial(gram_body, samps=samps, tile=tile), in_s...  4.29 us
    ppermute x11, waiting for transfers between devices, swap(): return lax.ppermute(x, axis, [(i, i ^ d) for i in range(n)])  3.42 us
    unnamed x6, local copies, waits for them, and re-layouts  2.82 us
    ppermute x3, waiting for transfers between devices, panel_pieces(): got = [lax.ppermute(chunk, 'ctr', [(0, d)]) for d in range(1, ctrs)]  1.96 us
  transfers between devices with their start and end apart: 14, of which 5 were waited for; matrix products, arithmetic and copies ran while one was open for 0% of the time, Pallas kernels for 48%

profile of v2, /device:TPU:0, one launch (start us, length us, event | category | flops | bytes accessed | tf_op | source)
XLA Modules:
  0.0 69.6 jit_solution(4104764043128183755)
XLA Ops:
  0.6 0.8 %constant_dynamic-slice_fusion = bf16[64,512]{1,0:T(8,128)(2,1)S(1)} fusion(bf16[1024,512]{1,0:T(8,128)(2,1)} %c_ref.1, s32[]{:T(128)S(6)} %select_n.12), kind=kLoop, calls=%fused_computation.14 | loop fusion | bytes 131076 | tf_op jit(solution)/shard_map/dynamic_slice | solution.py:316
  1.5 7.0 %collective-permute-start.2 = (bf16[64,512]{1,0:T(8,128)(2,1)S(1)}, bf16[64,512]{1,0:T(8,128)(2,1)S(1)}, u32[]{:S(2)}, u32[]{:S(2)}) collective-permute-start(bf16[64,512]{1,0:T(8,128)(2,1)S(1)} %constant_dynamic-slice_fusion), channel_id=1, source_target_pairs={{0,3},{4,7},{8,11},{12,15},{16,19},{20,23},{24,27},{28,31}} | collective-permute-start | bytes 196616 | tf_op jit(solution)/shard_map/ppermute | solution.py:317
  8.5 1.3 %collective-permute-start.1 = (bf16[64,512]{1,0:T(8,128)(2,1)S(1)}, bf16[64,512]{1,0:T(8,128)(2,1)S(1)}, u32[]{:S(2)}, u32[]{:S(2)}) collective-permute-start(bf16[64,512]{1,0:T(8,128)(2,1)S(1)} %constant_dynamic-slice_fusion), channel_id=1, source_target_pairs={{0,2},{4,6},{8,10},{12,14},{16,18},{20,22},{24,26},{28,30}} | collective-permute-start | bytes 196616 | tf_op jit(solution)/shard_map/ppermute | solution.py:317
  9.8 1.3 %collective-permute-start = (bf16[64,512]{1,0:T(8,128)(2,1)S(1)}, bf16[64,512]{1,0:T(8,128)(2,1)S(1)}, u32[]{:S(2)}, u32[]{:S(2)}) collective-permute-start(bf16[64,512]{1,0:T(8,128)(2,1)S(1)} %constant_dynamic-slice_fusion), channel_id=1, source_target_pairs={{0,1},{4,5},{8,9},{12,13},{16,17},{20,21},{24,25},{28,29}} | collective-permute-start | bytes 196616 | tf_op jit(solution)/shard_map/ppermute | solution.py:317
  11.1 0.0 collective-permute-done.2
  11.1 1.1 %collective-permute-done.1 = bf16[64,512]{1,0:T(8,128)(2,1)S(1)} collective-permute-done((bf16[64,512]{1,0:T(8,128)(2,1)S(1)}, bf16[64,512]{1,0:T(8,128)(2,1)S(1)}, u32[]{:S(2)}, u32[]{:S(2)}) %collective-permute-start.1) | collective-permute-done | bytes 65568 | tf_op jit(solution)/shard_map/ppermute | solution.py:317
  12.2 0.8 %collective-permute-done = bf16[64,512]{1,0:T(8,128)(2,1)S(1)} collective-permute-done((bf16[64,512]{1,0:T(8,128)(2,1)S(1)}, bf16[64,512]{1,0:T(8,128)(2,1)S(1)}, u32[]{:S(2)}, u32[]{:S(2)}) %collective-permute-start) | collective-permute-done | bytes 65568 | tf_op jit(solution)/shard_map/ppermute | solution.py:317
  13.0 0.9 %add_select_fusion.refs_0_ = bf16[64,512]{1,0:T(8,128)(2,1)S(1)} fusion(bf16[64,512]{1,0:T(8,128)(2,1)S(1)} %collective-permute-done.2, bf16[64,512]{1,0:T(8,128)(2,1)S(1)} %collective-permute-done, bf16[64,512]{1,0:T(8,128)(2,1)S(1)} %collective-permute-done.1, pred[]{:T(512)S(6)} %eq.3, bf16[1024,512]{1,0:T(8,128)(2,1)} %c_ref.1, s32[]{:T(128)S(6)} %select_n.12), kind=kLoop, calls=%fused_computation.13 | loop fusion | flops 229376 | bytes 327685 | tf_op jit(solution)/shard_map/jit(_where)/select_n | solution.py:321
  13.9 1.6 %collective-permute-start.9 = (bf16[64,512]{1,0:T(8,128)(2,1)S(1)}, bf16[64,512]{1,0:T(8,128)(2,1)S(1)}, u32[]{:S(2)}, u32[]{:S(2)}) collective-permute-start(bf16[64,512]{1,0:T(8,128)(2,1)S(1)} %add_select_fusion.refs_0_), channel_id=1, source_target_pairs={{0,28},{4,24},{8,20},{12,16},{16,12},{20,8},{24,4},{28,0},{1,29},{... | collective-permute-start | bytes 196616 | tf_op jit(solution)/shard_map/ppermute | solution.py:309
  15.5 1.0 %collective-permute-start.8 = (bf16[64,512]{1,0:T(8,128)(2,1)S(1)}, bf16[64,512]{1,0:T(8,128)(2,1)S(1)}, u32[]{:S(2)}, u32[]{:S(2)}) collective-permute-start(bf16[64,512]{1,0:T(8,128)(2,1)S(1)} %add_select_fusion.refs_0_), channel_id=1, source_target_pairs={{0,24},{4,28},{8,16},{12,20},{16,8},{20,12},{24,0},{28,4},{1,25},{... | collective-permute-start | bytes 196616 | tf_op jit(solution)/shard_map/ppermute | solution.py:309
  16.5 1.4 %collective-permute-start.7 = (bf16[64,512]{1,0:T(8,128)(2,1)S(1)}, bf16[64,512]{1,0:T(8,128)(2,1)S(1)}, u32[]{:S(2)}, u32[]{:S(2)}) collective-permute-start(bf16[64,512]{1,0:T(8,128)(2,1)S(1)} %add_select_fusion.refs_0_), channel_id=1, source_target_pairs={{0,20},{4,16},{8,28},{12,24},{16,4},{20,0},{24,12},{28,8},{1,21},{... | collective-permute-start | bytes 196616 | tf_op jit(solution)/shard_map/ppermute | solution.py:309
  17.9 0.5 collective-permute-start.6
  18.4 0.7 %collective-permute-start.5 = (bf16[64,512]{1,0:T(8,128)(2,1)S(1)}, bf16[64,512]{1,0:T(8,128)(2,1)S(1)}, u32[]{:S(2)}, u32[]{:S(2)}) collective-permute-start(bf16[64,512]{1,0:T(8,128)(2,1)S(1)} %add_select_fusion.refs_0_), channel_id=1, source_target_pairs={{0,12},{4,8},{8,4},{12,0},{16,28},{20,24},{24,20},{28,16},{1,13},{... | collective-permute-start | bytes 196616 | tf_op jit(solution)/shard_map/ppermute | solution.py:309
  19.1 0.1 collective-permute-done.9.refs_7_
  19.2 1.3 %collective-permute-start.4 = (bf16[64,512]{1,0:T(8,128)(2,1)S(1)}, bf16[64,512]{1,0:T(8,128)(2,1)S(1)}, u32[]{:S(2)}, u32[]{:S(2)}) collective-permute-start(bf16[64,512]{1,0:T(8,128)(2,1)S(1)} %add_select_fusion.refs_0_), channel_id=1, source_target_pairs={{0,8},{4,12},{8,0},{12,4},{16,24},{20,28},{24,16},{28,20},{1,9},{5... | collective-permute-start | bytes 196616 | tf_op jit(solution)/shard_map/ppermute | solution.py:309
  20.5 1.0 %collective-permute-done.8.refs_6_ = bf16[64,512]{1,0:T(8,128)(2,1)S(1)} collective-permute-done((bf16[64,512]{1,0:T(8,128)(2,1)S(1)}, bf16[64,512]{1,0:T(8,128)(2,1)S(1)}, u32[]{:S(2)}, u32[]{:S(2)}) %collective-permute-start.8) | collective-permute-done | bytes 65568 | tf_op jit(solution)/shard_map/ppermute | solution.py:309
  21.5 0.1 collective-permute-start.3
  21.5 0.0 copy-start
  21.5 1.6 %copy-done = bf16[2048,512]{1,0:T(8,128)(2,1)S(1)} copy-done((bf16[2048,512]{1,0:T(8,128)(2,1)S(1)}, bf16[2048,512]{1,0:T(8,128)(2,1)}, u32[]{:S(2)}) %copy-start) | copy-done | bytes 2097176
  23.1 0.0 copy-start.2
  23.1 1.2 %copy-done.2 = bf16[1024,512]{1,0:T(8,128)(2,1)S(1)} copy-done((bf16[1024,512]{1,0:T(8,128)(2,1)S(1)}, bf16[1024,512]{1,0:T(8,128)(2,1)}, u32[]{:S(2)}) %copy-start.2) | copy-done | bytes 1048600
  24.4 0.0 copy-start.1
  24.4 5.3 %kern_own.1 = (bf16[1024,2048]{1,0:T(8,128)(2,1)S(1)}, f32[2048,128]{1,0:T(8,128)S(1)}, bf16[128,512]{1,0:T(8,128)(2,1)S(1)}) custom-call(s32[1]{0:T(128)} %bitcast.me_ref, bf16[1024,512]{1,0:T(8,128)(2,1)S(1)} %copy-done.2, bf16[2048,512]{1,0:T(8,128)(2,1)S(1)} %copy-done), custom_call_target="tpu_custom_call" | custom-call | tf_op jit(solution)/shard_map/kern_own/pallas_call | solution.py:244
  29.7 0.0 collective-permute-done.7.refs_5_
  29.7 0.0 collective-permute-done.6.refs_4_
  29.7 0.0 collective-permute-done.5.refs_3_
  29.7 0.0 collective-permute-done.4.refs_2_
  29.7 0.0 collective-permute-done.3.refs_1_
  29.7 0.0 copy-done.1
  29.7 4.3 %gram.1 = (bf16[512,512]{1,0:T(8,128)(2,1)S(1)}, f32[4,128,512]{2,1,0:T(8,128)S(1)}, f32[128,512]{1,0:T(8,128)S(1)}, f32[128,512]{1,0:T(8,128)S(1)}, f32[128,512]{1,0:T(8,128)S(1)}, /*index=5*/f32[128,512]{1,0:T(8,128)S(1)}) custom-call(s32[1]{0:T(128)} %bitcast.me_ref, bf16[64,512]{1,0:T(8,128)(2,1)S(1)} %add_select_fusion.refs_0_, ...), custom_call_target="tpu_custom_call" | custom-call | tf_op jit(solution)/shard_map/gram/pallas_call | solution.py:286
  34.0 0.5 collective-permute-start.10
  34.6 2.3 %collective-permute-done.10 = f32[4,128,512]{2,1,0:T(8,128)S(1)} collective-permute-done((f32[4,128,512]{2,1,0:T(8,128)S(1)}, f32[4,128,512]{2,1,0:T(8,128)S(1)}, u32[]{:S(2)}, u32[]{:S(2)}) %collective-permute-start.10) | collective-permute-done | bytes 1048608 | tf_op jit(solution)/shard_map/ppermute | solution.py:309
  36.8 0.1 fusion.2
  37.0 0.6 collective-permute-start.11
  37.6 1.8 %collective-permute-start.13 = (f32[128,512]{1,0:T(8,128)S(1)}, f32[128,512]{1,0:T(8,128)S(1)}, u32[]{:S(2)}, u32[]{:S(2)}) collective-permute-start(f32[128,512]{1,0:T(8,128)S(1)} %get-tuple-element.26), channel_id=1, source_target_pairs={{0,24},{4,28},{8,16},{12,20},{16,8},{20,12},{24,0},{28,4},{1,25},{... | collective-permute-start | bytes 786440 | tf_op jit(solution)/shard_map/ppermute | solution.py:309
  39.4 1.2 %collective-permute-start.12 = (f32[128,512]{1,0:T(8,128)S(1)}, f32[128,512]{1,0:T(8,128)S(1)}, u32[]{:S(2)}, u32[]{:S(2)}) collective-permute-start(f32[128,512]{1,0:T(8,128)S(1)} %get-tuple-element.27), channel_id=1, source_target_pairs={{0,16},{4,20},{8,24},{12,28},{16,0},{20,4},{24,8},{28,12},{1,17},{... | collective-permute-start | bytes 786440 | tf_op jit(solution)/shard_map/ppermute | solution.py:309
  40.5 28.2 %chol.1 = (f32[128,512]{1,0:T(8,128)}, f32[512,512]{1,0:T(8,128)}) custom-call(s32[1]{0:T(128)} %bitcast.6.off_ref, bf16[512,512]{1,0:T(8,128)(2,1)S(1)} %get-tuple-element.21.panel_ref, bf16[128,512]{1,0:T(8,128)(2,1)S(1)} %get-tuple-element.22.own_ref), custom_call_target="tpu_custom_call" | custom-call | tf_op jit(solution)/shard_map/chol/pallas_call | solution.py:180
  68.7 0.0 collective-permute-done.11
  68.7 0.0 collective-permute-done.13
  68.7 0.0 collective-permute-done.12
  68.7 0.8 %fusion.8 = f32[1,128,512]{2,1,0:T(8,128)} fusion(f32[128,512]{1,0:T(8,128)S(1)} %collective-permute-done.13, f32[128,512]{1,0:T(8,128)S(1)} %collective-permute-done.12, f32[128,512]{1,0:T(8,128)S(1)} %collective-permute-done.11, f32[128,512]{1,0:T(8,128)S(1)} %get-tuple-element.16, f32[4,128,512]{2,1,0:T(8,128)S(1)} %collective-permute-done.10), kind=kLoop, calls=%fused_computation.12 | loop fusion | flops 327680 | bytes 1572864 | tf_op jit(solution)/shard_map/broadcast_in_dim | solution.py:344
Async XLA Ops:
  1.5 9.6 %collective-permute-start.2 = (bf16[64,512]{1,0:T(8,128)(2,1)S(1)}, bf16[64,512]{1,0:T(8,128)(2,1)S(1)}, u32[]{:S(2)}, u32[]{:S(2)}) collective-permute-start(bf16[64,512]{1,0:T(8,128)(2,1)S(1)} %constant_dynamic-slice_fusion), channel_id=1, source_target_pairs={{0,3},{4,7},{8,11},{12,15},{16,19},{20,23},{24,27},{28,31}} | collective-permute-start | bytes 196616 | tf_op jit(solution)/shard_map/ppermute | solution.py:317
  8.5 3.8 %collective-permute-start.1 = (bf16[64,512]{1,0:T(8,128)(2,1)S(1)}, bf16[64,512]{1,0:T(8,128)(2,1)S(1)}, u32[]{:S(2)}, u32[]{:S(2)}) collective-permute-start(bf16[64,512]{1,0:T(8,128)(2,1)S(1)} %constant_dynamic-slice_fusion), channel_id=1, source_target_pairs={{0,2},{4,6},{8,10},{12,14},{16,18},{20,22},{24,26},{28,30}} | collective-permute-start | bytes 196616 | tf_op jit(solution)/shard_map/ppermute | solution.py:317
  9.8 3.3 %collective-permute-start = (bf16[64,512]{1,0:T(8,128)(2,1)S(1)}, bf16[64,512]{1,0:T(8,128)(2,1)S(1)}, u32[]{:S(2)}, u32[]{:S(2)}) collective-permute-start(bf16[64,512]{1,0:T(8,128)(2,1)S(1)} %constant_dynamic-slice_fusion), channel_id=1, source_target_pairs={{0,1},{4,5},{8,9},{12,13},{16,17},{20,21},{24,25},{28,29}} | collective-permute-start | bytes 196616 | tf_op jit(solution)/shard_map/ppermute | solution.py:317
  13.9 5.3 %collective-permute-start.9 = (bf16[64,512]{1,0:T(8,128)(2,1)S(1)}, bf16[64,512]{1,0:T(8,128)(2,1)S(1)}, u32[]{:S(2)}, u32[]{:S(2)}) collective-permute-start(bf16[64,512]{1,0:T(8,128)(2,1)S(1)} %add_select_fusion.refs_0_), channel_id=1, source_target_pairs={{0,28},{4,24},{8,20},{12,16},{16,12},{20,8},{24,4},{28,0},{1,29},{... | collective-permute-start | bytes 196616 | tf_op jit(solution)/shard_map/ppermute | solution.py:309
  15.5 5.9 %collective-permute-start.8 = (bf16[64,512]{1,0:T(8,128)(2,1)S(1)}, bf16[64,512]{1,0:T(8,128)(2,1)S(1)}, u32[]{:S(2)}, u32[]{:S(2)}) collective-permute-start(bf16[64,512]{1,0:T(8,128)(2,1)S(1)} %add_select_fusion.refs_0_), channel_id=1, source_target_pairs={{0,24},{4,28},{8,16},{12,20},{16,8},{20,12},{24,0},{28,4},{1,25},{... | collective-permute-start | bytes 196616 | tf_op jit(solution)/shard_map/ppermute | solution.py:309
  16.5 13.2 %collective-permute-start.7 = (bf16[64,512]{1,0:T(8,128)(2,1)S(1)}, bf16[64,512]{1,0:T(8,128)(2,1)S(1)}, u32[]{:S(2)}, u32[]{:S(2)}) collective-permute-start(bf16[64,512]{1,0:T(8,128)(2,1)S(1)} %add_select_fusion.refs_0_), channel_id=1, source_target_pairs={{0,20},{4,16},{8,28},{12,24},{16,4},{20,0},{24,12},{28,8},{1,21},{... | collective-permute-start | bytes 196616 | tf_op jit(solution)/shard_map/ppermute | solution.py:309
  17.9 11.8 %collective-permute-start.6 = (bf16[64,512]{1,0:T(8,128)(2,1)S(1)}, bf16[64,512]{1,0:T(8,128)(2,1)S(1)}, u32[]{:S(2)}, u32[]{:S(2)}) collective-permute-start(bf16[64,512]{1,0:T(8,128)(2,1)S(1)} %add_select_fusion.refs_0_), channel_id=1, source_target_pairs={{0,16},{4,20},{8,24},{12,28},{16,0},{20,4},{24,8},{28,12},{1,17},{... | collective-permute-start | bytes 196616 | tf_op jit(solution)/shard_map/ppermute | solution.py:309
  18.4 11.3 %collective-permute-start.5 = (bf16[64,512]{1,0:T(8,128)(2,1)S(1)}, bf16[64,512]{1,0:T(8,128)(2,1)S(1)}, u32[]{:S(2)}, u32[]{:S(2)}) collective-permute-start(bf16[64,512]{1,0:T(8,128)(2,1)S(1)} %add_select_fusion.refs_0_), channel_id=1, source_target_pairs={{0,12},{4,8},{8,4},{12,0},{16,28},{20,24},{24,20},{28,16},{1,13},{... | collective-permute-start | bytes 196616 | tf_op jit(solution)/shard_map/ppermute | solution.py:309
  19.2 10.5 %collective-permute-start.4 = (bf16[64,512]{1,0:T(8,128)(2,1)S(1)}, bf16[64,512]{1,0:T(8,128)(2,1)S(1)}, u32[]{:S(2)}, u32[]{:S(2)}) collective-permute-start(bf16[64,512]{1,0:T(8,128)(2,1)S(1)} %add_select_fusion.refs_0_), channel_id=1, source_target_pairs={{0,8},{4,12},{8,0},{12,4},{16,24},{20,28},{24,16},{28,20},{1,9},{5... | collective-permute-start | bytes 196616 | tf_op jit(solution)/shard_map/ppermute | solution.py:309
  21.5 8.2 %collective-permute-start.3 = (bf16[64,512]{1,0:T(8,128)(2,1)S(1)}, bf16[64,512]{1,0:T(8,128)(2,1)S(1)}, u32[]{:S(2)}, u32[]{:S(2)}) collective-permute-start(bf16[64,512]{1,0:T(8,128)(2,1)S(1)} %add_select_fusion.refs_0_), channel_id=1, source_target_pairs={{0,4},{4,0},{8,12},{12,8},{16,20},{20,16},{24,28},{28,24},{1,5},{5... | collective-permute-start | bytes 196616 | tf_op jit(solution)/shard_map/ppermute | solution.py:309
  21.5 1.6 %copy-start = (bf16[2048,512]{1,0:T(8,128)(2,1)S(1)}, bf16[2048,512]{1,0:T(8,128)(2,1)}, u32[]{:S(2)}) copy-start(bf16[2048,512]{1,0:T(8,128)(2,1)} %refs_9_.1) | copy-start | bytes 6291460
  23.1 1.2 %copy-start.2 = (bf16[1024,512]{1,0:T(8,128)(2,1)S(1)}, bf16[1024,512]{1,0:T(8,128)(2,1)}, u32[]{:S(2)}) copy-start(bf16[1024,512]{1,0:T(8,128)(2,1)} %c_ref.1) | copy-start | bytes 3145732
  24.4 5.4 %copy-start.1 = (bf16[2048,512]{1,0:T(8,128)(2,1)S(1)}, bf16[2048,512]{1,0:T(8,128)(2,1)}, u32[]{:S(2)}) copy-start(bf16[2048,512]{1,0:T(8,128)(2,1)} %refs_9_.1) | copy-start | bytes 6291460
  34.0 2.8 %collective-permute-start.10 = (f32[4,128,512]{2,1,0:T(8,128)S(1)}, f32[4,128,512]{2,1,0:T(8,128)S(1)}, u32[]{:S(2)}, u32[]{:S(2)}) collective-permute-start(f32[4,128,512]{2,1,0:T(8,128)S(1)} %get-tuple-element.17), channel_id=1, source_target_pairs={{0,4},{4,0},{8,12},{12,8},{16,20},{20,16},{24,28},{28,24},{1,5},{5... | collective-permute-start | bytes 3145736 | tf_op jit(solution)/shard_map/ppermute | solution.py:309
  37.0 31.7 %collective-permute-start.11 = (f32[128,512]{1,0:T(8,128)S(1)}, f32[128,512]{1,0:T(8,128)S(1)}, u32[]{:S(2)}, u32[]{:S(2)}) collective-permute-start(f32[128,512]{1,0:T(8,128)S(1)} %get-tuple-element.25), channel_id=1, source_target_pairs={{0,8},{4,12},{8,0},{12,4},{16,24},{20,28},{24,16},{28,20},{1,9},{5... | collective-permute-start | bytes 786440 | tf_op jit(solution)/shard_map/ppermute | solution.py:309
  37.6 31.1 %collective-permute-start.13 = (f32[128,512]{1,0:T(8,128)S(1)}, f32[128,512]{1,0:T(8,128)S(1)}, u32[]{:S(2)}, u32[]{:S(2)}) collective-permute-start(f32[128,512]{1,0:T(8,128)S(1)} %get-tuple-element.26), channel_id=1, source_target_pairs={{0,24},{4,28},{8,16},{12,20},{16,8},{20,12},{24,0},{28,4},{1,25},{... | collective-permute-start | bytes 786440 | tf_op jit(solution)/shard_map/ppermute | solution.py:309
  39.4 29.4 %collective-permute-start.12 = (f32[128,512]{1,0:T(8,128)S(1)}, f32[128,512]{1,0:T(8,128)S(1)}, u32[]{:S(2)}, u32[]{:S(2)}) collective-permute-start(f32[128,512]{1,0:T(8,128)S(1)} %get-tuple-element.27), channel_id=1, source_target_pairs={{0,16},{4,20},{8,24},{12,28},{16,0},{20,4},{24,8},{28,12},{1,17},{... | collective-permute-start | bytes 786440 | tf_op jit(solution)/shard_map/ppermute | solution.py:309

commit v3 on v2

--- a/solution.py
+++ b/solution.py
@@ -13,7 +13,7 @@
 def lanebc(x,c): return jnp.broadcast_to(x[:,c:c+1],(8,B))
 def subbc(x,j): return jnp.broadcast_to(x[j:j+1,:],(8,B))
 
-def factor128(probs):
+def factor128(probs, fills=()):
     row=lax.broadcasted_iota(jnp.int32,(B,B),0)
     lane=lax.broadcasted_iota(jnp.int32,(B,B),1)
     n=VB//8
@@ -49,9 +49,13 @@
                         X[z]=X[z]-cj*ur; Y[z]=Y[z]-cj*wr
         e=base+VB
         if e<B:
+            zs=[]
             for r,w,u,m in probs:
                 ub=u[base:e,:]; mb=m[base:e,:]
-                z=mmul(ub.T[e:,:],jnp.concatenate([ub,mb],axis=1))
+                zs.append(mmul(ub.T[e:,:],jnp.concatenate([ub,mb],axis=1)))
+            gaps=B//VB-1
+            for f in fills[b::gaps]: f()
+            for (r,w,u,m),z in zip(probs,zs):
                 r[e:,:]=r[e:,:]-z[:,:B]
                 w[e:,:]=w[e:,:]-z[:,B:]
     for r,w,u,m in probs: u[...]=jnp.where(lane>=row,u[...],0.0)
@@ -93,35 +97,51 @@
         l_ref[j,K]=v.T
 
 def trail(a_ref,u_ref,l_ref,Kp,nb,nj):
-    for i in range(1,nb):
+    def one(i):
         z=mmul(l_ref[i,Kp],jnp.concatenate([u_ref[Kp,j] for j in range(i,nj)],axis=1))
         for j in range(i,nj):
             a_ref[i,j]=a_ref[i,j]-z[:,(j-i)*B:(j-i+1)*B]
-
-def body(off_ref,panel_ref,own_ref,chol_ref,prec_ref,a_ref,u_ref,l_ref,s_ref,v_ref,h_ref,ms_ref,r0,w0,k0,m0,r1,w1,k1,m1,*,own):
-    nb=panel_ref.shape[0]//B; no=own//B; nj=nb+no
+    return [functools.partial(one,i) for i in range(1,nb)]
+
+def init_body(off_ref,panel_ref,own_ref,a_ref,s_ref,*,own):
+    nb=panel_ref.shape[0]//B; no=own//B
+    kern_init(off_ref,panel_ref,own_ref,a_ref,nb,no)
+    kr=[jnp.concatenate([a_ref[i,j] for j in range(nb)],axis=1) for i in range(nb)]
+    kc=jnp.concatenate(kr,axis=0)
+    for i in range(nb):
+        z=mmul(kr[i],kc[:,i*B:])+SHIFT*kr[i][:,i*B:]
+        for j in range(nb):
+            s_ref[i,j]=z[:,(j-i)*B:(j-i+1)*B] if j>=i else jnp.zeros((B,B),jnp.float32)
+
+def init_kernel(off,panel,own):
+    ro=own.shape[0]; nb=panel.shape[0]//B; no=ro//B
+    vm=pl.BlockSpec(memory_space=pltpu.VMEM)
+    V=lambda *s: pltpu.VMEM(s+(B,B),jnp.float32)
+    return pl.pallas_call(functools.partial(init_body,own=ro),
+        out_shape=(V(nb,nb+no),V(nb,nb)),
+        in_specs=[pl.BlockSpec(memory_space=pltpu.SMEM),vm,vm],out_specs=(vm,vm),
+        compiler_params=pltpu.CompilerParams(vmem_limit_bytes=16<<20),
+        name='kern_center')(off,panel,own)
+
+def body(ain_ref,sin_ref,chol_ref,prec_ref,a_ref,u_ref,l_ref,s_ref,v_ref,h_ref,ms_ref,r0,w0,k0,m0,r1,w1,k1,m1):
+    nb,nj=ain_ref.shape[:2]; no=nj-nb
     eye=lax.broadcasted_iota(jnp.int32,(B,B),0)==lax.broadcasted_iota(jnp.int32,(B,B),1)
-    kern_init(off_ref,panel_ref,own_ref,a_ref,nb,no)
     zero=jnp.zeros((B,B),jnp.float32)
     for j in range(nj):
         u_ref[nb,j]=zero; l_ref[j,nb]=zero
     for j in range(nb):
         v_ref[nb,j]=zero; h_ref[j,nb]=zero
-    kr=[jnp.concatenate([a_ref[i,j] for j in range(nb)],axis=1) for i in range(nb)]
-    kc=jnp.concatenate(kr,axis=0)
     top=None
     for i in range(nb):
-        z=mmul(kr[i],kc[:,i*B:])+SHIFT*kr[i][:,i*B:]
-        for j in range(i,nb):
-            s_ref[i,j]=z[:,(j-i)*B:(j-i+1)*B]
-        d=jnp.where(eye,s_ref[i,i],0.0)
+        for j in range(nj): a_ref[i,j]=ain_ref[i,j]
+        for j in range(nb): s_ref[i,j]=sin_ref[i,j]
+        d=jnp.where(eye,sin_ref[i,i],0.0)
         top=d if top is None else jnp.maximum(top,d)
-    r0[...]=a_ref[0,0]; r1[...]=s_ref[0,0]
+    r0[...]=ain_ref[0,0]; r1[...]=sin_ref[0,0]
     def step(K,low):
         Kp=jnp.where(K==0,nb,K-1)
-        factor128([(r0,w0,k0,m0),(r1,w1,k1,m1)])
-        trail(a_ref,u_ref,l_ref,Kp,nb,nj)
-        trail(s_ref,v_ref,h_ref,Kp,nb,nb)
+        fills=trail(a_ref,u_ref,l_ref,Kp,nb,nj)+trail(s_ref,v_ref,h_ref,Kp,nb,nb)[::-1]
+        factor128([(r0,w0,k0,m0),(r1,w1,k1,m1)],fills)
         ms_ref[K]=m0[...]
         put(m0[...],k0[...],[a_ref[K,j] for j in range(nj)],K,nb,u_ref,l_ref)
         put(m1[...],k1[...],[s_ref[K,j] for j in range(nb)],K,nb,v_ref,h_ref)
@@ -161,8 +181,7 @@
         r1[...]=s_ref[0,0]
         def again(K,carry):
             Kp=jnp.where(K==0,nb,K-1)
-            factor128([(r1,w1,k1,m1)])
-            trail(s_ref,v_ref,h_ref,Kp,nb,nb)
+            factor128([(r1,w1,k1,m1)],trail(s_ref,v_ref,h_ref,Kp,nb,nb))
             put(m1[...],k1[...],[s_ref[K,j] for j in range(nb)],K,nb,v_ref,h_ref)
             K1=jnp.minimum(K+1,nb-1)
             r1[...]=s_ref[K1,K1]-mmul(h_ref[K1,K],v_ref[K,K1])
@@ -172,17 +191,20 @@
             for C in range(nb):
                 prec_ref[J*B:(J+1)*B,C*B:(C+1)*B]=h_ref[J,C]
 
-def chol_kernel(off,panel,own):
-    n=panel.shape[0]; ro=own.shape[0]; nb=n//B; no=ro//B; nj=nb+no
+def factor_kernel(a,s):
+    nb,nj=a.shape[:2]; no=nj-nb
     vm=pl.BlockSpec(memory_space=pltpu.VMEM)
     f32=jnp.float32
     V=lambda *s: pltpu.VMEM(s+(B,B),f32)
-    return pl.pallas_call(functools.partial(body,own=ro),
-        out_shape=(jax.ShapeDtypeStruct((ro,n),f32),jax.ShapeDtypeStruct((n,n),f32)),
-        in_specs=[pl.BlockSpec(memory_space=pltpu.SMEM),vm,vm],out_specs=(vm,vm),
+    return pl.pallas_call(body,
+        out_shape=(jax.ShapeDtypeStruct((no*B,nb*B),f32),jax.ShapeDtypeStruct((nb*B,nb*B),f32)),
+        in_specs=[vm,vm],out_specs=(vm,vm),
         scratch_shapes=[V(nb,nj),V(nb+1,nj),V(nj,nb+1),V(nb,nb),V(nb+1,nb),V(nb,nb+1),V(nb)]+[V()]*8,
         compiler_params=pltpu.CompilerParams(vmem_limit_bytes=24<<20),
-        name='chol')(off,panel,own)
+        name='chol')(a,s)
+
+def chol_kernel(off,panel,own):
+    return factor_kernel(*init_kernel(off,panel,own))
 
 
 LOG2E = 1.4426950408889634
@@ -190,6 +212,10 @@
 
 def near(x):
     return pltpu.with_memory_space_constraint(x, pltpu.VMEM)
+
+
+def far(x):
+    return pltpu.with_memory_space_constraint(x, pltpu.HBM)
 
 
 def square_parts(x):
@@ -222,37 +248,54 @@
     return jnp.exp2(arg).astype(jnp.bfloat16)
 
 
-def own_body(me_ref, c_ref, s_ref, k_ref, norm_ref, own_ref, *, row_dev):
+def own_body(me_ref, c_hbm, s_hbm, k_ref, norm_ref, own_ref, s_ref, c_ref, c_sem, s_sem, *, row_dev, tile):
     scale = -2.0 * LOG2E / c_ref.shape[1]
+    tiles = s_ref.shape[0] // tile
+    first = pltpu.make_async_copy(c_hbm, c_ref, c_sem)
+    first.start()
+    copies = []
+    for t in range(tiles):
+        part = pl.ds(t * tile, tile)
+        copies.append(pltpu.make_async_copy(s_hbm.at[part], s_ref.at[part], s_sem.at[t]))
+        copies[-1].start()
+    first.wait()
     at = pl.multiple_of(me_ref[0] * row_dev, row_dev)
     own_ref[0:row_dev, :] = c_ref[pl.ds(at, row_dev), :]
     if row_dev < own_ref.shape[0]:
         own_ref[row_dev:, :] = jnp.zeros((own_ref.shape[0] - row_dev, own_ref.shape[1]), own_ref.dtype)
     c = c_ref[...]
     ccol = col_norms(c, scale)
-    tile = 2 * B
-    for t in range(0, s_ref.shape[0], tile):
-        s = s_ref[t : t + tile, :]
-        norm_ref[t : t + tile, :] = col_norms(s, scale)
-        k_ref[:, t : t + tile] = kern_tile(c, s, ccol, row_norms(s, scale))
-
-
-def own_kernel(me, centers, samples, row_dev):
+    for t in range(tiles):
+        copies[t].wait()
+        part = slice(t * tile, (t + 1) * tile)
+        s = s_ref[part, :]
+        norm_ref[part, :] = col_norms(s, scale)
+        k_ref[:, part] = kern_tile(c, s, ccol, row_norms(s, scale))
+
+
+def own_kernel(me, centers, samples, row_dev, tile=512):
     mc, d = centers.shape
     ns = samples.shape[0]
     inside = pl.BlockSpec(memory_space=pltpu.VMEM)
+    outside = pl.BlockSpec(memory_space=pltpu.HBM)
     return pl.pallas_call(
-        functools.partial(own_body, row_dev=row_dev),
-        in_specs=[pl.BlockSpec(memory_space=pltpu.SMEM), inside, inside],
-        out_specs=(inside, inside, inside),
+        functools.partial(own_body, row_dev=row_dev, tile=tile),
+        in_specs=[pl.BlockSpec(memory_space=pltpu.SMEM), outside, outside],
+        out_specs=(inside,) * 4,
         out_shape=(
             pltpu.VMEM((mc, ns), jnp.bfloat16),
             pltpu.VMEM((ns, B), jnp.float32),
             pltpu.VMEM((row_dev + -row_dev % B, d), jnp.bfloat16),
+            pltpu.VMEM((ns, d), jnp.bfloat16),
         ),
+        scratch_shapes=[
+            pltpu.VMEM((mc, d), jnp.bfloat16),
+            pltpu.SemaphoreType.DMA(()),
+            pltpu.SemaphoreType.DMA((ns // tile,)),
+        ],
         compiler_params=pltpu.CompilerParams(vmem_limit_bytes=16 << 20),
         name="kern_own",
-    )(me, near(centers), samples)
+    )(me, far(centers), far(samples))
 
 
 def gram_body(me_ref, *refs, samps, tile):
@@ -329,18 +372,19 @@
     mc_dev = centers.shape[0]
     row_dev = mc_dev // samp_count
     me = samp_index.reshape(1)
-    samples = near(samples)
     pieces = panel_pieces(centers)
-    kern_own, norms, own = own_kernel(me, centers, samples, row_dev)
-    panel, other, *mine = gram_kernel(me, pieces, kern_own, samples, norms)
+    kern_own, norms, own, held = own_kernel(me, centers, samples, row_dev)
+    panel, other, *mine = gram_kernel(me, pieces, kern_own, held, norms)
     other = swap(other, "samp", 1)
+    off = (ctr_index * mc_dev + samp_index * row_dev).reshape(1)
+    first, second = init_kernel(off, panel, own)
+    other, first, second = lax.optimization_barrier((other, first, second))
     half = [mine[d] + other[d] for d in range(samp_count // 2)]
     total = half[0]
     for d in range(1, samp_count // 2):
         total = total + swap(half[d], "samp", 2 * d)
     gram = total * (GRAM_SCALE / (samples.shape[0] * samp_count))
-    off = (ctr_index * mc_dev + samp_index * row_dev).reshape(1)
-    chol, precond = chol_kernel(off, panel, own)
+    chol, precond = factor_kernel(first, second)
     return (gram[None], chol[None, :row_dev], precond)
 
 

time: 69.9 us -> 71.3 us (1.020)
  Pallas kernels: 37.8 us -> 41.9 us
  local copies, waits for them, and re-layouts: 3.67 us -> 0.85 us
  other arithmetic: 1.84 us -> 4.07 us
  waiting for transfers between devices: 5.38 us -> 3.23 us
    pallas_call x2 -> x3, Pallas kernels: 33.5 us -> 37.6 us  [the longest x1 26.1 us: factor_kernel(): pl.pallas_call(body, out_shape=(jax.ShapeDtypeStruct((no * B, nb * B), f3...]
    unnamed x6 -> x0, local copies, waits for them, and re-layouts: 2.82 us -> none
    ppermute x11, waiting for transfers between devices: 3.42 us -> 1.27 us  [swap(): return lax.ppermute(x, axis, [(i, i ^ d) for i in range(n)])]
    add x1, other arithmetic: 0.14 us -> 1.42 us  [local(): half = [mine[d] + other[d] for d in range(samp_count // 2)]]
    broadcast_in_dim x1, other arithmetic: 0.82 us -> 1.77 us  [local(): return (gram[None], chol[None, :row_dev], precond)]
  transfers between devices with their start and end apart: 14 -> 14, of which waited for: 5 -> 5; matrix products, arithmetic and copies ran while one was open for 0% -> 0% of each run, Pallas kernels for 48% -> 53%
where the time goes in v3:
time: 71.3 us; the launch traced here: 71 us
  Pallas kernels  41.9 us (59%)
  starting transfers between devices  20.1 us (28%)
  other arithmetic  4.07 us (6%)
  waiting for transfers between devices  3.23 us (5%)
  local copies, waits for them, and re-layouts  0.85 us (1%)
  between operations  0.76 us (1%)
    pallas_call x1, Pallas kernels, factor_kernel(): pl.pallas_call(body, out_shape=(jax.ShapeDtypeStruct((no * B, nb * B), f3...  26.1 us
    ppermute x11, starting transfers between devices, swap(): return lax.ppermute(x, axis, [(i, i ^ d) for i in range(n)])  10.6 us
    ppermute x3, starting transfers between devices, panel_pieces(): got = [lax.ppermute(chunk, 'ctr', [(0, d)]) for d in range(1, ctrs)]  9.56 us
    pallas_call x1, Pallas kernels, own_kernel(): pl.pallas_call(functools.partial(own_body, row_dev=row_dev, tile=tile), i...  9.3 us
    pallas_call x1, Pallas kernels, gram_kernel(): pl.pallas_call(functools.partial(gram_body, samps=samps, tile=tile), in_s...  4.29 us
    pallas_call x1, Pallas kernels, init_kernel(): pl.pallas_call(functools.partial(init_body, own=ro), out_shape=(V(nb, nb...  2.27 us
    ppermute x3, waiting for transfers between devices, panel_pieces(): got = [lax.ppermute(chunk, 'ctr', [(0, d)]) for d in range(1, ctrs)]  1.96 us
    broadcast_in_dim x1, other arithmetic, local(): return (gram[None], chol[None, :row_dev], precond)  1.77 us
  transfers between devices with their start and end apart: 14, of which 5 were waited for; matrix products, arithmetic and copies ran while one was open for 0% of the time, Pallas kernels for 53%

profile of v3, /device:TPU:0, one launch (start us, length us, event | category | flops | bytes accessed | tf_op | source)
XLA Modules:
  0.0 71.0 jit_solution(8827082221550948925)
XLA Ops:
  0.6 0.8 %constant_dynamic-slice_fusion = bf16[64,512]{1,0:T(8,128)(2,1)S(1)} fusion(bf16[1024,512]{1,0:T(8,128)(2,1)} %c_hbm.1, s32[]{:T(128)S(6)} %select_n.12), kind=kLoop, calls=%fused_computation.10 | loop fusion | bytes 131076 | tf_op jit(solution)/shard_map/dynamic_slice | solution.py:359
  1.5 7.0 %collective-permute-start.2 = (bf16[64,512]{1,0:T(8,128)(2,1)S(1)}, bf16[64,512]{1,0:T(8,128)(2,1)S(1)}, u32[]{:S(2)}, u32[]{:S(2)}) collective-permute-start(bf16[64,512]{1,0:T(8,128)(2,1)S(1)} %constant_dynamic-slice_fusion), channel_id=1, source_target_pairs={{0,3},{4,7},{8,11},{12,15},{16,19},{20,23},{24,27},{28,31}} | collective-permute-start | bytes 196616 | tf_op jit(solution)/shard_map/ppermute | solution.py:360
  8.5 1.3 %collective-permute-start.1 = (bf16[64,512]{1,0:T(8,128)(2,1)S(1)}, bf16[64,512]{1,0:T(8,128)(2,1)S(1)}, u32[]{:S(2)}, u32[]{:S(2)}) collective-permute-start(bf16[64,512]{1,0:T(8,128)(2,1)S(1)} %constant_dynamic-slice_fusion), channel_id=1, source_target_pairs={{0,2},{4,6},{8,10},{12,14},{16,18},{20,22},{24,26},{28,30}} | collective-permute-start | bytes 196616 | tf_op jit(solution)/shard_map/ppermute | solution.py:360
  9.8 1.3 %collective-permute-start = (bf16[64,512]{1,0:T(8,128)(2,1)S(1)}, bf16[64,512]{1,0:T(8,128)(2,1)S(1)}, u32[]{:S(2)}, u32[]{:S(2)}) collective-permute-start(bf16[64,512]{1,0:T(8,128)(2,1)S(1)} %constant_dynamic-slice_fusion), channel_id=1, source_target_pairs={{0,1},{4,5},{8,9},{12,13},{16,17},{20,21},{24,25},{28,29}} | collective-permute-start | bytes 196616 | tf_op jit(solution)/shard_map/ppermute | solution.py:360
  11.1 0.0 collective-permute-done.2
  11.1 1.1 %collective-permute-done.1 = bf16[64,512]{1,0:T(8,128)(2,1)S(1)} collective-permute-done((bf16[64,512]{1,0:T(8,128)(2,1)S(1)}, bf16[64,512]{1,0:T(8,128)(2,1)S(1)}, u32[]{:S(2)}, u32[]{:S(2)}) %collective-permute-start.1) | collective-permute-done | bytes 65568 | tf_op jit(solution)/shard_map/ppermute | solution.py:360
  12.2 0.8 %collective-permute-done = bf16[64,512]{1,0:T(8,128)(2,1)S(1)} collective-permute-done((bf16[64,512]{1,0:T(8,128)(2,1)S(1)}, bf16[64,512]{1,0:T(8,128)(2,1)S(1)}, u32[]{:S(2)}, u32[]{:S(2)}) %collective-permute-start) | collective-permute-done | bytes 65568 | tf_op jit(solution)/shard_map/ppermute | solution.py:360
  13.0 0.9 %add_select_fusion.refs_0_ = bf16[64,512]{1,0:T(8,128)(2,1)S(1)} fusion(bf16[64,512]{1,0:T(8,128)(2,1)S(1)} %collective-permute-done.2, bf16[64,512]{1,0:T(8,128)(2,1)S(1)} %collective-permute-done, bf16[64,512]{1,0:T(8,128)(2,1)S(1)} %collective-permute-done.1, pred[]{:T(512)S(6)} %eq.3, bf16[1024,512]{1,0:T(8,128)(2,1)} %c_hbm.1, s32[]{:T(128)S(6)} %select_n.12), kind=kLoop, calls=%fused_computation.9 | loop fusion | flops 229376 | bytes 327685 | tf_op jit(solution)/shard_map/jit(_where)/select_n | solution.py:364
  13.9 1.6 %collective-permute-start.9 = (bf16[64,512]{1,0:T(8,128)(2,1)S(1)}, bf16[64,512]{1,0:T(8,128)(2,1)S(1)}, u32[]{:S(2)}, u32[]{:S(2)}) collective-permute-start(bf16[64,512]{1,0:T(8,128)(2,1)S(1)} %add_select_fusion.refs_0_), channel_id=1, source_target_pairs={{0,28},{4,24},{8,20},{12,16},{16,12},{20,8},{24,4},{28,0},{1,29},{... | collective-permute-start | bytes 196616 | tf_op jit(solution)/shard_map/ppermute | solution.py:352
  15.5 1.0 %collective-permute-start.8 = (bf16[64,512]{1,0:T(8,128)(2,1)S(1)}, bf16[64,512]{1,0:T(8,128)(2,1)S(1)}, u32[]{:S(2)}, u32[]{:S(2)}) collective-permute-start(bf16[64,512]{1,0:T(8,128)(2,1)S(1)} %add_select_fusion.refs_0_), channel_id=1, source_target_pairs={{0,24},{4,28},{8,16},{12,20},{16,8},{20,12},{24,0},{28,4},{1,25},{... | collective-permute-start | bytes 196616 | tf_op jit(solution)/shard_map/ppermute | solution.py:352
  16.5 1.4 %collective-permute-start.7 = (bf16[64,512]{1,0:T(8,128)(2,1)S(1)}, bf16[64,512]{1,0:T(8,128)(2,1)S(1)}, u32[]{:S(2)}, u32[]{:S(2)}) collective-permute-start(bf16[64,512]{1,0:T(8,128)(2,1)S(1)} %add_select_fusion.refs_0_), channel_id=1, source_target_pairs={{0,20},{4,16},{8,28},{12,24},{16,4},{20,0},{24,12},{28,8},{1,21},{... | collective-permute-start | bytes 196616 | tf_op jit(solution)/shard_map/ppermute | solution.py:352
  17.9 0.5 collective-permute-start.6
  18.4 0.7 collective-permute-start.5
  19.1 0.1 collective-permute-done.9.refs_7_
  19.2 1.3 %collective-permute-start.4 = (bf16[64,512]{1,0:T(8,128)(2,1)S(1)}, bf16[64,512]{1,0:T(8,128)(2,1)S(1)}, u32[]{:S(2)}, u32[]{:S(2)}) collective-permute-start(bf16[64,512]{1,0:T(8,128)(2,1)S(1)} %add_select_fusion.refs_0_), channel_id=1, source_target_pairs={{0,8},{4,12},{8,0},{12,4},{16,24},{20,28},{24,16},{28,20},{1,9},{5... | collective-permute-start | bytes 196616 | tf_op jit(solution)/shard_map/ppermute | solution.py:352
  20.5 1.0 %collective-permute-done.8.refs_6_ = bf16[64,512]{1,0:T(8,128)(2,1)S(1)} collective-permute-done((bf16[64,512]{1,0:T(8,128)(2,1)S(1)}, bf16[64,512]{1,0:T(8,128)(2,1)S(1)}, u32[]{:S(2)}, u32[]{:S(2)}) %collective-permute-start.8) | collective-permute-done | bytes 65568 | tf_op jit(solution)/shard_map/ppermute | solution.py:352
  21.5 0.1 collective-permute-start.3
  21.5 9.3 %kern_own.1 = (bf16[1024,2048]{1,0:T(8,128)(2,1)S(1)}, f32[2048,128]{1,0:T(8,128)S(1)}, bf16[128,512]{1,0:T(8,128)(2,1)S(1)}, bf16[2048,512]{1,0:T(8,128)(2,1)S(1)}) custom-call(s32[1]{0:T(128)} %bitcast.me_ref, bf16[1024,512]{1,0:T(8,128)(2,1)} %c_hbm.1, bf16[2048,512]{1,0:T(8,128)(2,1)} %s_hbm.1), custom_call_target="tpu_custom_call" | custom-call | tf_op jit(solution)/shard_map/kern_own/pallas_call | solution.py:281
  30.9 0.0 collective-permute-done.7.refs_5_
  30.9 0.0 collective-permute-done.6.refs_4_
  30.9 0.0 collective-permute-done.5.refs_3_
  30.9 0.0 collective-permute-done.4.refs_2_
  30.9 0.0 collective-permute-done.3.refs_1_
  30.9 4.3 %gram.1 = (bf16[512,512]{1,0:T(8,128)(2,1)S(1)}, f32[4,128,512]{2,1,0:T(8,128)S(1)}, f32[128,512]{1,0:T(8,128)S(1)}, f32[128,512]{1,0:T(8,128)S(1)}, f32[128,512]{1,0:T(8,128)S(1)}, /*index=5*/f32[128,512]{1,0:T(8,128)S(1)}) custom-call(s32[1]{0:T(128)} %bitcast.me_ref, bf16[64,512]{1,0:T(8,128)(2,1)S(1)} %add_select_fusion.refs_0_, ...), custom_call_target="tpu_custom_call" | custom-call | tf_op jit(solution)/shard_map/gram/pallas_call | solution.py:329
  35.2 0.5 collective-permute-start.10
  35.7 2.3 %kern_center.1 = (f32[4,5,128,128]{3,2,1,0:T(8,128)S(1)}, f32[4,4,128,128]{3,2,1,0:T(8,128)S(1)}) custom-call(s32[1]{0:T(128)} %bitcast.1.off_ref, bf16[512,512]{1,0:T(8,128)(2,1)S(1)} %get-tuple-element.25.panel_ref, bf16[128,512]{1,0:T(8,128)(2,1)S(1)} %get-tuple-element.26.own_ref), custom_call_target="tpu_custom_call" | custom-call | tf_op jit(solution)/shard_map/kern_center/pallas_call | solution.py:120
  38.0 0.1 collective-permute-done.10
  38.1 1.4 %bitcast_add_fusion.2 = (f32[128,512]{1,0:T(8,128)S(1)}, f32[128,512]{1,0:T(8,128)S(1)}, f32[128,512]{1,0:T(8,128)S(1)}) fusion(f32[128,512]{1,0:T(8,128)S(1)} %get-tuple-element.30, f32[4,128,512]{2,1,0:T(8,128)} %collective-permute-done.10, f32[128,512]{1,0:T(8,128)S(1)} %get-tuple-element.32, f32[128,512]{1,0:T(8,128)S(1)} %get-tuple-element.31), kind=kLoop, calls=%fused_computation.2 | loop fusion | flops 196608 | bytes 2359296 | tf_op jit(solution)/shard_map/add | solution.py:382
  39.6 0.6 collective-permute-start.11
  40.2 1.8 %collective-permute-start.13 = (f32[128,512]{1,0:T(8,128)S(1)}, f32[128,512]{1,0:T(8,128)S(1)}, u32[]{:S(2)}, u32[]{:S(2)}) collective-permute-start(f32[128,512]{1,0:T(8,128)S(1)} %get-tuple-element.38), channel_id=1, source_target_pairs={{0,24},{4,28},{8,16},{12,20},{16,8},{20,12},{24,0},{28,4},{1,25},{... | collective-permute-start | bytes 786440 | tf_op jit(solution)/shard_map/ppermute | solution.py:352
  41.9 1.2 %collective-permute-start.12 = (f32[128,512]{1,0:T(8,128)S(1)}, f32[128,512]{1,0:T(8,128)S(1)}, u32[]{:S(2)}, u32[]{:S(2)}) collective-permute-start(f32[128,512]{1,0:T(8,128)S(1)} %get-tuple-element.39), channel_id=1, source_target_pairs={{0,16},{4,20},{8,24},{12,28},{16,0},{20,4},{24,8},{28,12},{1,17},{... | collective-permute-start | bytes 786440 | tf_op jit(solution)/shard_map/ppermute | solution.py:352
  43.1 26.1 %chol.1 = (f32[128,512]{1,0:T(8,128)}, f32[512,512]{1,0:T(8,128)}) custom-call(f32[4,5,128,128]{3,2,1,0:T(8,128)S(1)} %get-tuple-element.33.ain_ref, f32[4,4,128,128]{3,2,1,0:T(8,128)S(1)} %get-tuple-element.34.sin_ref), custom_call_target="tpu_custom_call" | custom-call | tf_op jit(solution)/shard_map/chol/pallas_call | solution.py:199
  69.2 0.0 collective-permute-done.11
  69.2 0.0 collective-permute-done.13
  69.2 0.0 collective-permute-done.12
  69.2 1.8 %fusion.4 = f32[1,128,512]{2,1,0:T(8,128)} fusion(f32[128,512]{1,0:T(8,128)S(1)} %collective-permute-done.13, f32[128,512]{1,0:T(8,128)S(1)} %collective-permute-done.12, f32[128,512]{1,0:T(8,128)S(1)} %collective-permute-done.11, f32[128,512]{1,0:T(8,128)S(1)} %get-tuple-element.23, f32[4,128,512]{2,1,0:T(8,128)} %collective-permute-done.10), kind=kLoop, calls=%fused_computation.8 | loop fusion | flops 327680 | bytes 1572864 | tf_op jit(solution)/shard_map/broadcast_in_dim | solution.py:388
Async XLA Ops:
  1.5 9.6 %collective-permute-start.2 = (bf16[64,512]{1,0:T(8,128)(2,1)S(1)}, bf16[64,512]{1,0:T(8,128)(2,1)S(1)}, u32[]{:S(2)}, u32[]{:S(2)}) collective-permute-start(bf16[64,512]{1,0:T(8,128)(2,1)S(1)} %constant_dynamic-slice_fusion), channel_id=1, source_target_pairs={{0,3},{4,7},{8,11},{12,15},{16,19},{20,23},{24,27},{28,31}} | collective-permute-start | bytes 196616 | tf_op jit(solution)/shard_map/ppermute | solution.py:360
  8.5 3.8 %collective-permute-start.1 = (bf16[64,512]{1,0:T(8,128)(2,1)S(1)}, bf16[64,512]{1,0:T(8,128)(2,1)S(1)}, u32[]{:S(2)}, u32[]{:S(2)}) collective-permute-start(bf16[64,512]{1,0:T(8,128)(2,1)S(1)} %constant_dynamic-slice_fusion), channel_id=1, source_target_pairs={{0,2},{4,6},{8,10},{12,14},{16,18},{20,22},{24,26},{28,30}} | collective-permute-start | bytes 196616 | tf_op jit(solution)/shard_map/ppermute | solution.py:360
  9.8 3.3 %collective-permute-start = (bf16[64,512]{1,0:T(8,128)(2,1)S(1)}, bf16[64,512]{1,0:T(8,128)(2,1)S(1)}, u32[]{:S(2)}, u32[]{:S(2)}) collective-permute-start(bf16[64,512]{1,0:T(8,128)(2,1)S(1)} %constant_dynamic-slice_fusion), channel_id=1, source_target_pairs={{0,1},{4,5},{8,9},{12,13},{16,17},{20,21},{24,25},{28,29}} | collective-permute-start | bytes 196616 | tf_op jit(solution)/shard_map/ppermute | solution.py:360
  13.9 5.3 %collective-permute-start.9 = (bf16[64,512]{1,0:T(8,128)(2,1)S(1)}, bf16[64,512]{1,0:T(8,128)(2,1)S(1)}, u32[]{:S(2)}, u32[]{:S(2)}) collective-permute-start(bf16[64,512]{1,0:T(8,128)(2,1)S(1)} %add_select_fusion.refs_0_), channel_id=1, source_target_pairs={{0,28},{4,24},{8,20},{12,16},{16,12},{20,8},{24,4},{28,0},{1,29},{... | collective-permute-start | bytes 196616 | tf_op jit(solution)/shard_map/ppermute | solution.py:352
  15.5 5.9 %collective-permute-start.8 = (bf16[64,512]{1,0:T(8,128)(2,1)S(1)}, bf16[64,512]{1,0:T(8,128)(2,1)S(1)}, u32[]{:S(2)}, u32[]{:S(2)}) collective-permute-start(bf16[64,512]{1,0:T(8,128)(2,1)S(1)} %add_select_fusion.refs_0_), channel_id=1, source_target_pairs={{0,24},{4,28},{8,16},{12,20},{16,8},{20,12},{24,0},{28,4},{1,25},{... | collective-permute-start | bytes 196616 | tf_op jit(solution)/shard_map/ppermute | solution.py:352
  16.5 14.3 %collective-permute-start.7 = (bf16[64,512]{1,0:T(8,128)(2,1)S(1)}, bf16[64,512]{1,0:T(8,128)(2,1)S(1)}, u32[]{:S(2)}, u32[]{:S(2)}) collective-permute-start(bf16[64,512]{1,0:T(8,128)(2,1)S(1)} %add_select_fusion.refs_0_), channel_id=1, source_target_pairs={{0,20},{4,16},{8,28},{12,24},{16,4},{20,0},{24,12},{28,8},{1,21},{... | collective-permute-start | bytes 196616 | tf_op jit(solution)/shard_map/ppermute | solution.py:352
  17.9 13.0 %collective-permute-start.6 = (bf16[64,512]{1,0:T(8,128)(2,1)S(1)}, bf16[64,512]{1,0:T(8,128)(2,1)S(1)}, u32[]{:S(2)}, u32[]{:S(2)}) collective-permute-start(bf16[64,512]{1,0:T(8,128)(2,1)S(1)} %add_select_fusion.refs_0_), channel_id=1, source_target_pairs={{0,16},{4,20},{8,24},{12,28},{16,0},{20,4},{24,8},{28,12},{1,17},{... | collective-permute-start | bytes 196616 | tf_op jit(solution)/shard_map/ppermute | solution.py:352
  18.4 12.5 %collective-permute-start.5 = (bf16[64,512]{1,0:T(8,128)(2,1)S(1)}, bf16[64,512]{1,0:T(8,128)(2,1)S(1)}, u32[]{:S(2)}, u32[]{:S(2)}) collective-permute-start(bf16[64,512]{1,0:T(8,128)(2,1)S(1)} %add_select_fusion.refs_0_), channel_id=1, source_target_pairs={{0,12},{4,8},{8,4},{12,0},{16,28},{20,24},{24,20},{28,16},{1,13},{... | collective-permute-start | bytes 196616 | tf_op jit(solution)/shard_map/ppermute | solution.py:352
  19.2 11.7 %collective-permute-start.4 = (bf16[64,512]{1,0:T(8,128)(2,1)S(1)}, bf16[64,512]{1,0:T(8,128)(2,1)S(1)}, u32[]{:S(2)}, u32[]{:S(2)}) collective-permute-start(bf16[64,512]{1,0:T(8,128)(2,1)S(1)} %add_select_fusion.refs_0_), channel_id=1, source_target_pairs={{0,8},{4,12},{8,0},{12,4},{16,24},{20,28},{24,16},{28,20},{1,9},{5... | collective-permute-start | bytes 196616 | tf_op jit(solution)/shard_map/ppermute | solution.py:352
  21.5 9.4 %collective-permute-start.3 = (bf16[64,512]{1,0:T(8,128)(2,1)S(1)}, bf16[64,512]{1,0:T(8,128)(2,1)S(1)}, u32[]{:S(2)}, u32[]{:S(2)}) collective-permute-start(bf16[64,512]{1,0:T(8,128)(2,1)S(1)} %add_select_fusion.refs_0_), channel_id=1, source_target_pairs={{0,4},{4,0},{8,12},{12,8},{16,20},{20,16},{24,28},{28,24},{1,5},{5... | collective-permute-start | bytes 196616 | tf_op jit(solution)/shard_map/ppermute | solution.py:352
  35.2 2.9 %collective-permute-start.10 = (f32[4,128,512]{2,1,0:T(8,128)S(1)}, f32[4,128,512]{2,1,0:T(8,128)}, u32[]{:S(2)}, u32[]{:S(2)}) collective-permute-start(f32[4,128,512]{2,1,0:T(8,128)S(1)} %get-tuple-element.24), channel_id=1, source_target_pairs={{0,4},{4,0},{8,12},{12,8},{16,20},{20,16},{24,28},{28,24},{1,5},{5... | collective-permute-start | bytes 3145736 | tf_op jit(solution)/shard_map/ppermute | solution.py:352
  39.6 29.6 %collective-permute-start.11 = (f32[128,512]{1,0:T(8,128)S(1)}, f32[128,512]{1,0:T(8,128)S(1)}, u32[]{:S(2)}, u32[]{:S(2)}) collective-permute-start(f32[128,512]{1,0:T(8,128)S(1)} %get-tuple-element.37), channel_id=1, source_target_pairs={{0,8},{4,12},{8,0},{12,4},{16,24},{20,28},{24,16},{28,20},{1,9},{5... | collective-permute-start | bytes 786440 | tf_op jit(solution)/shard_map/ppermute | solution.py:352
  40.2 29.0 %collective-permute-start.13 = (f32[128,512]{1,0:T(8,128)S(1)}, f32[128,512]{1,0:T(8,128)S(1)}, u32[]{:S(2)}, u32[]{:S(2)}) collective-permute-start(f32[128,512]{1,0:T(8,128)S(1)} %get-tuple-element.38), channel_id=1, source_target_pairs={{0,24},{4,28},{8,16},{12,20},{16,8},{20,12},{24,0},{28,4},{1,25},{... | collective-permute-start | bytes 786440 | tf_op jit(solution)/shard_map/ppermute | solution.py:352
  41.9 27.3 %collective-permute-start.12 = (f32[128,512]{1,0:T(8,128)S(1)}, f32[128,512]{1,0:T(8,128)S(1)}, u32[]{:S(2)}, u32[]{:S(2)}) collective-permute-start(f32[128,512]{1,0:T(8,128)S(1)} %get-tuple-element.39), channel_id=1, source_target_pairs={{0,16},{4,20},{8,24},{12,28},{16,0},{20,4},{24,8},{28,12},{1,17},{... | collective-permute-start | bytes 786440 | tf_op jit(solution)/shard_map/ppermute | solution.py:352

commit v4 on v3

--- a/solution.py
+++ b/solution.py
@@ -218,6 +218,68 @@
     return pltpu.with_memory_space_constraint(x, pltpu.HBM)
 
 
+def load_body(c_hbm, s_hbm, c_ref, s_ref, sem, *, parts):
+    copies = []
+    for t, (src, dst) in enumerate([(c_hbm, c_ref)] + [(s_hbm, s_ref)] * parts):
+        rows = src.shape[0] // (parts if t else 1)
+        part = pl.ds((t - 1) * rows if t else 0, rows)
+        copies.append(pltpu.make_async_copy(src.at[part], dst.at[part], sem.at[t]))
+        copies[-1].start()
+    for copy in copies:
+        copy.wait()
+
+
+def load_kernel(centers, samples, parts=2):
+    outside = pl.BlockSpec(memory_space=pltpu.HBM)
+    inside = pl.BlockSpec(memory_space=pltpu.VMEM)
+    return pl.pallas_call(
+        functools.partial(load_body, parts=parts),
+        in_specs=[outside, outside],
+        out_specs=(inside, inside),
+        out_shape=(pltpu.VMEM(centers.shape, centers.dtype), pltpu.VMEM(samples.shape, samples.dtype)),
+        scratch_shapes=[pltpu.SemaphoreType.DMA((1 + parts,))],
+        compiler_params=pltpu.CompilerParams(vmem_limit_bytes=4 << 20),
+        name="load",
+    )(far(centers), far(samples))
+
+
+def pair_body(other_ref, *refs):
+    n = len(refs) // 2
+    for d in range(n):
+        refs[n + d][...] = refs[d][...] + other_ref[d]
+
+
+def pair_kernel(other, mine):
+    inside = pl.BlockSpec(memory_space=pltpu.VMEM)
+    return pl.pallas_call(
+        pair_body,
+        in_specs=[inside] * (1 + len(mine)),
+        out_specs=[inside] * len(mine),
+        out_shape=[pltpu.VMEM(x.shape, x.dtype) for x in mine],
+        compiler_params=pltpu.CompilerParams(vmem_limit_bytes=4 << 20),
+        name="pair_sum",
+    )(near(other), *[near(x) for x in mine])
+
+
+def total_body(*refs, scale):
+    total = refs[0][...]
+    for ref in refs[1:-1]:
+        total = total + ref[...]
+    refs[-1][...] = total * scale
+
+
+def total_kernel(parts, scale):
+    inside = pl.BlockSpec(memory_space=pltpu.VMEM)
+    return pl.pallas_call(
+        functools.partial(total_body, scale=scale),
+        in_specs=[inside] * len(parts),
+        out_specs=inside,
+        out_shape=jax.ShapeDtypeStruct(parts[0].shape, parts[0].dtype),
+        compiler_params=pltpu.CompilerParams(vmem_limit_bytes=4 << 20),
+        name="gram_sum",
+    )(*[near(x) for x in parts])
+
+
 def square_parts(x):
     sq = jnp.square(x.astype(jnp.float32))
     hi = sq.astype(jnp.bfloat16)
@@ -248,54 +310,37 @@
     return jnp.exp2(arg).astype(jnp.bfloat16)
 
 
-def own_body(me_ref, c_hbm, s_hbm, k_ref, norm_ref, own_ref, s_ref, c_ref, c_sem, s_sem, *, row_dev, tile):
+def own_body(me_ref, c_ref, s_ref, k_ref, norm_ref, own_ref, *, row_dev):
     scale = -2.0 * LOG2E / c_ref.shape[1]
-    tiles = s_ref.shape[0] // tile
-    first = pltpu.make_async_copy(c_hbm, c_ref, c_sem)
-    first.start()
-    copies = []
-    for t in range(tiles):
-        part = pl.ds(t * tile, tile)
-        copies.append(pltpu.make_async_copy(s_hbm.at[part], s_ref.at[part], s_sem.at[t]))
-        copies[-1].start()
-    first.wait()
     at = pl.multiple_of(me_ref[0] * row_dev, row_dev)
     own_ref[0:row_dev, :] = c_ref[pl.ds(at, row_dev), :]
     if row_dev < own_ref.shape[0]:
         own_ref[row_dev:, :] = jnp.zeros((own_ref.shape[0] - row_dev, own_ref.shape[1]), own_ref.dtype)
     c = c_ref[...]
     ccol = col_norms(c, scale)
-    for t in range(tiles):
-        copies[t].wait()
-        part = slice(t * tile, (t + 1) * tile)
-        s = s_ref[part, :]
-        norm_ref[part, :] = col_norms(s, scale)
-        k_ref[:, part] = kern_tile(c, s, ccol, row_norms(s, scale))
-
-
-def own_kernel(me, centers, samples, row_dev, tile=512):
+    tile = 2 * B
+    for t in range(0, s_ref.shape[0], tile):
+        s = s_ref[t : t + tile, :]
+        norm_ref[t : t + tile, :] = col_norms(s, scale)
+        k_ref[:, t : t + tile] = kern_tile(c, s, ccol, row_norms(s, scale))
+
+
+def own_kernel(me, centers, samples, row_dev):
     mc, d = centers.shape
     ns = samples.shape[0]
     inside = pl.BlockSpec(memory_space=pltpu.VMEM)
-    outside = pl.BlockSpec(memory_space=pltpu.HBM)
     return pl.pallas_call(
-        functools.partial(own_body, row_dev=row_dev, tile=tile),
-        in_specs=[pl.BlockSpec(memory_space=pltpu.SMEM), outside, outside],
-        out_specs=(inside,) * 4,
+        functools.partial(own_body, row_dev=row_dev),
+        in_specs=[pl.BlockSpec(memory_space=pltpu.SMEM), inside, inside],
+        out_specs=(inside, inside, inside),
         out_shape=(
             pltpu.VMEM((mc, ns), jnp.bfloat16),
             pltpu.VMEM((ns, B), jnp.float32),
             pltpu.VMEM((row_dev + -row_dev % B, d), jnp.bfloat16),
-            pltpu.VMEM((ns, d), jnp.bfloat16),
         ),
-        scratch_shapes=[
-            pltpu.VMEM((mc, d), jnp.bfloat16),
-            pltpu.SemaphoreType.DMA(()),
-            pltpu.SemaphoreType.DMA((ns // tile,)),
-        ],
         compiler_params=pltpu.CompilerParams(vmem_limit_bytes=16 << 20),
         name="kern_own",
-    )(me, far(centers), far(samples))
+    )(me, centers, samples)
 
 
 def gram_body(me_ref, *refs, samps, tile):
@@ -352,17 +397,18 @@
     return lax.ppermute(x, axis, [(i, i ^ d) for i in range(n)])
 
 
-def panel_pieces(centers):
+def panel_pieces(centers, samples):
     ctrs = lax.axis_size("ctr")
     samps = lax.axis_size("samp")
     rows = PANEL // samps
     chunk = lax.dynamic_slice_in_dim(centers, lax.axis_index("samp") * rows, rows, 0)
     got = [lax.ppermute(chunk, "ctr", [(0, d)]) for d in range(1, ctrs)]
+    got, near_centers, near_samples = lax.optimization_barrier((got, *load_kernel(centers, samples)))
     total = got[0]
     for piece in got[1:]:
         total = total + piece
     chunk = jnp.where(lax.axis_index("ctr") == 0, chunk, total)
-    return [chunk] + [swap(chunk, "samp", d) for d in range(1, samps)]
+    return near_centers, near_samples, [chunk] + [swap(chunk, "samp", d) for d in range(1, samps)]
 
 
 def local(samples, centers):
@@ -372,19 +418,17 @@
     mc_dev = centers.shape[0]
     row_dev = mc_dev // samp_count
     me = samp_index.reshape(1)
-    pieces = panel_pieces(centers)
-    kern_own, norms, own, held = own_kernel(me, centers, samples, row_dev)
+    near_centers, held, pieces = panel_pieces(centers, samples)
+    kern_own, norms, own = own_kernel(me, near_centers, held, row_dev)
     panel, other, *mine = gram_kernel(me, pieces, kern_own, held, norms)
     other = swap(other, "samp", 1)
     off = (ctr_index * mc_dev + samp_index * row_dev).reshape(1)
     first, second = init_kernel(off, panel, own)
     other, first, second = lax.optimization_barrier((other, first, second))
-    half = [mine[d] + other[d] for d in range(samp_count // 2)]
-    total = half[0]
-    for d in range(1, samp_count // 2):
-        total = total + swap(half[d], "samp", 2 * d)
-    gram = total * (GRAM_SCALE / (samples.shape[0] * samp_count))
+    half = pair_kernel(other, mine)
+    parts = [half[0]] + [swap(half[d], "samp", 2 * d) for d in range(1, samp_count // 2)]
     chol, precond = factor_kernel(first, second)
+    gram = total_kernel(parts, GRAM_SCALE / (samples.shape[0] * samp_count))
     return (gram[None], chol[None, :row_dev], precond)
 
 

time: 71.3 us -> 66.1 us (0.927)
  other arithmetic: 4.07 us -> 0.87 us
  waiting for transfers between devices: 3.23 us -> 1.42 us
    ppermute x3, waiting for transfers between devices: 1.96 us -> 0.05 us  [panel_pieces(): got = [lax.ppermute(chunk, 'ctr', [(0, d)]) for d in range(1, ctrs)]]
    broadcast_in_dim x1 -> x0, other arithmetic: 1.77 us -> none  [local(): return (gram[None], chol[None, :row_dev], precond)]
    add x1 -> x0, other arithmetic: 1.42 us -> none  [local(): half = [mine[d] + other[d] for d in range(samp_count // 2)]]
    pallas_call x1 -> x4, Pallas kernels: 9.3 us -> 8.04 us  [the longest x1 5.3 us: own_kernel(): pl.pallas_call(functools.partial(own_body, row_dev=row_dev), in_specs=[pl...]
    pallas_call x1, Pallas kernels: 4.29 us -> 5.26 us  [gram_kernel(): pl.pallas_call(functools.partial(gram_body, samps=samps, tile=tile), in_s...]
  transfers between devices with their start and end apart: 14 -> 14, of which waited for: 5 -> 3; matrix products, arithmetic and copies ran while one was open for 0% -> 0% of each run, Pallas kernels for 53% -> 54%
where the time goes in v4:
time: 66.1 us; the launch traced here: 65.8 us
  Pallas kernels  41.8 us (63%)
  starting transfers between devices  20.1 us (30%)
  waiting for transfers between devices  1.42 us (2%)
  other arithmetic  0.87 us (1%)
  local copies, waits for them, and re-layouts  0.85 us (1%)
  between operations  0.76 us (1%)
    pallas_call x1, Pallas kernels, factor_kernel(): pl.pallas_call(body, out_shape=(jax.ShapeDtypeStruct((no * B, nb * B), f3...  26.2 us
    ppermute x11, starting transfers between devices, swap(): return lax.ppermute(x, axis, [(i, i ^ d) for i in range(n)])  10.5 us
    ppermute x3, starting transfers between devices, panel_pieces(): got = [lax.ppermute(chunk, 'ctr', [(0, d)]) for d in range(1, ctrs)]  9.56 us
    pallas_call x1, Pallas kernels, own_kernel(): pl.pallas_call(functools.partial(own_body, row_dev=row_dev), in_specs=[pl...  5.3 us
    pallas_call x1, Pallas kernels, gram_kernel(): pl.pallas_call(functools.partial(gram_body, samps=samps, tile=tile), in_s...  5.26 us
    pallas_call x1, Pallas kernels, init_kernel(): pl.pallas_call(functools.partial(init_body, own=ro), out_shape=(V(nb, nb...  2.27 us
    pallas_call x1, Pallas kernels, load_kernel(): pl.pallas_call(functools.partial(load_body, parts=parts), in_specs=[outsi...  1.89 us
    ppermute x11, waiting for transfers between devices, swap(): return lax.ppermute(x, axis, [(i, i ^ d) for i in range(n)])  1.37 us
  transfers between devices with their start and end apart: 14, of which 3 were waited for; matrix products, arithmetic and copies ran while one was open for 0% of the time, Pallas kernels for 54%

profile of v4, /device:TPU:0, one launch (start us, length us, event | category | flops | bytes accessed | tf_op | source)
XLA Modules:
  0.0 65.8 jit_solution(13374903068577656999)
XLA Ops:
  0.6 0.8 %constant_dynamic-slice_fusion = bf16[64,512]{1,0:T(8,128)(2,1)S(1)} fusion(bf16[1024,512]{1,0:T(8,128)(2,1)} %c_hbm.1, s32[]{:T(128)S(6)} %select_n.12), kind=kLoop, calls=%fused_computation.1 | loop fusion | bytes 131076 | tf_op jit(solution)/shard_map/dynamic_slice | solution.py:404
  1.5 7.0 %collective-permute-start.2 = (bf16[64,512]{1,0:T(8,128)(2,1)S(1)}, bf16[64,512]{1,0:T(8,128)(2,1)S(1)}, u32[]{:S(2)}, u32[]{:S(2)}) collective-permute-start(bf16[64,512]{1,0:T(8,128)(2,1)S(1)} %constant_dynamic-slice_fusion), channel_id=1, source_target_pairs={{0,3},{4,7},{8,11},{12,15},{16,19},{20,23},{24,27},{28,31}} | collective-permute-start | bytes 196616 | tf_op jit(solution)/shard_map/ppermute | solution.py:405
  8.5 1.3 %collective-permute-start.1 = (bf16[64,512]{1,0:T(8,128)(2,1)S(1)}, bf16[64,512]{1,0:T(8,128)(2,1)S(1)}, u32[]{:S(2)}, u32[]{:S(2)}) collective-permute-start(bf16[64,512]{1,0:T(8,128)(2,1)S(1)} %constant_dynamic-slice_fusion), channel_id=1, source_target_pairs={{0,2},{4,6},{8,10},{12,14},{16,18},{20,22},{24,26},{28,30}} | collective-permute-start | bytes 196616 | tf_op jit(solution)/shard_map/ppermute | solution.py:405
  9.8 1.3 %collective-permute-start = (bf16[64,512]{1,0:T(8,128)(2,1)S(1)}, bf16[64,512]{1,0:T(8,128)(2,1)S(1)}, u32[]{:S(2)}, u32[]{:S(2)}) collective-permute-start(bf16[64,512]{1,0:T(8,128)(2,1)S(1)} %constant_dynamic-slice_fusion), channel_id=1, source_target_pairs={{0,1},{4,5},{8,9},{12,13},{16,17},{20,21},{24,25},{28,29}} | collective-permute-start | bytes 196616 | tf_op jit(solution)/shard_map/ppermute | solution.py:405
  11.1 1.9 %load.1 = (bf16[1024,512]{1,0:T(8,128)(2,1)S(1)}, bf16[2048,512]{1,0:T(8,128)(2,1)S(1)}) custom-call(bf16[1024,512]{1,0:T(8,128)(2,1)} %c_hbm.1, bf16[2048,512]{1,0:T(8,128)(2,1)} %s_hbm.1), custom_call_target="tpu_custom_call" | custom-call | tf_op jit(solution)/shard_map/load/pallas_call | solution.py:235
  13.0 0.0 collective-permute-done.2
  13.0 0.0 collective-permute-done.1
  13.0 0.0 collective-permute-done
  13.0 0.9 %add_select_fusion.refs_0_ = bf16[64,512]{1,0:T(8,128)(2,1)S(1)} fusion(bf16[64,512]{1,0:T(8,128)(2,1)S(1)} %collective-permute-done.2, bf16[64,512]{1,0:T(8,128)(2,1)S(1)} %collective-permute-done, bf16[64,512]{1,0:T(8,128)(2,1)S(1)} %collective-permute-done.1, pred[]{:T(512)S(6)} %eq.3, bf16[1024,512]{1,0:T(8,128)(2,1)} %c_hbm.1, s32[]{:T(128)S(6)} %select_n.12), kind=kLoop, calls=%fused_computation | loop fusion | flops 229376 | bytes 327685 | tf_op jit(solution)/shard_map/jit(_where)/select_n | solution.py:410
  13.9 1.6 %collective-permute-start.9 = (bf16[64,512]{1,0:T(8,128)(2,1)S(1)}, bf16[64,512]{1,0:T(8,128)(2,1)S(1)}, u32[]{:S(2)}, u32[]{:S(2)}) collective-permute-start(bf16[64,512]{1,0:T(8,128)(2,1)S(1)} %add_select_fusion.refs_0_), channel_id=1, source_target_pairs={{0,28},{4,24},{8,20},{12,16},{16,12},{20,8},{24,4},{28,0},{1,29},{... | collective-permute-start | bytes 196616 | tf_op jit(solution)/shard_map/ppermute | solution.py:397
  15.6 0.9 %collective-permute-start.8 = (bf16[64,512]{1,0:T(8,128)(2,1)S(1)}, bf16[64,512]{1,0:T(8,128)(2,1)S(1)}, u32[]{:S(2)}, u32[]{:S(2)}) collective-permute-start(bf16[64,512]{1,0:T(8,128)(2,1)S(1)} %add_select_fusion.refs_0_), channel_id=1, source_target_pairs={{0,24},{4,28},{8,16},{12,20},{16,8},{20,12},{24,0},{28,4},{1,25},{... | collective-permute-start | bytes 196616 | tf_op jit(solution)/shard_map/ppermute | solution.py:397
  16.5 1.4 %collective-permute-start.7 = (bf16[64,512]{1,0:T(8,128)(2,1)S(1)}, bf16[64,512]{1,0:T(8,128)(2,1)S(1)}, u32[]{:S(2)}, u32[]{:S(2)}) collective-permute-start(bf16[64,512]{1,0:T(8,128)(2,1)S(1)} %add_select_fusion.refs_0_), channel_id=1, source_target_pairs={{0,20},{4,16},{8,28},{12,24},{16,4},{20,0},{24,12},{28,8},{1,21},{... | collective-permute-start | bytes 196616 | tf_op jit(solution)/shard_map/ppermute | solution.py:397
  17.9 0.5 collective-permute-start.6
  18.4 0.7 %collective-permute-start.5 = (bf16[64,512]{1,0:T(8,128)(2,1)S(1)}, bf16[64,512]{1,0:T(8,128)(2,1)S(1)}, u32[]{:S(2)}, u32[]{:S(2)}) collective-permute-start(bf16[64,512]{1,0:T(8,128)(2,1)S(1)} %add_select_fusion.refs_0_), channel_id=1, source_target_pairs={{0,12},{4,8},{8,4},{12,0},{16,28},{20,24},{24,20},{28,16},{1,13},{... | collective-permute-start | bytes 196616 | tf_op jit(solution)/shard_map/ppermute | solution.py:397
  19.1 0.1 collective-permute-done.9.refs_7_
  19.2 1.3 %collective-permute-start.4 = (bf16[64,512]{1,0:T(8,128)(2,1)S(1)}, bf16[64,512]{1,0:T(8,128)(2,1)S(1)}, u32[]{:S(2)}, u32[]{:S(2)}) collective-permute-start(bf16[64,512]{1,0:T(8,128)(2,1)S(1)} %add_select_fusion.refs_0_), channel_id=1, source_target_pairs={{0,8},{4,12},{8,0},{12,4},{16,24},{20,28},{24,16},{28,20},{1,9},{5... | collective-permute-start | bytes 196616 | tf_op jit(solution)/shard_map/ppermute | solution.py:397
  20.5 1.0 %collective-permute-done.8.refs_6_ = bf16[64,512]{1,0:T(8,128)(2,1)S(1)} collective-permute-done((bf16[64,512]{1,0:T(8,128)(2,1)S(1)}, bf16[64,512]{1,0:T(8,128)(2,1)S(1)}, u32[]{:S(2)}, u32[]{:S(2)}) %collective-permute-start.8) | collective-permute-done | bytes 65568 | tf_op jit(solution)/shard_map/ppermute | solution.py:397
  21.5 0.1 collective-permute-start.3
  21.6 5.3 %kern_own.1 = (bf16[1024,2048]{1,0:T(8,128)(2,1)S(1)}, f32[2048,128]{1,0:T(8,128)S(1)}, bf16[128,512]{1,0:T(8,128)(2,1)S(1)}) custom-call(s32[1]{0:T(128)} %bitcast.me_ref, bf16[1024,512]{1,0:T(8,128)(2,1)S(1)} %get-tuple-element.35.c_ref, bf16[2048,512]{1,0:T(8,128)(2,1)S(1)} %get-tuple-element.36.s_ref.refs_9_), custom_call_target="tpu_custom_call" | custom-call | tf_op jit(solution)/shard_map/kern_own/pallas_call | solution.py:332
  26.9 0.0 collective-permute-done.7.refs_5_
  26.9 0.0 collective-permute-done.6.refs_4_
  26.9 0.0 collective-permute-done.5.refs_3_
  26.9 0.0 collective-permute-done.4.refs_2_
  26.9 0.0 collective-permute-done.3.refs_1_
  26.9 5.3 %gram.1 = (bf16[512,512]{1,0:T(8,128)(2,1)S(1)}, f32[4,128,512]{2,1,0:T(8,128)}, f32[128,512]{1,0:T(8,128)S(1)}, f32[128,512]{1,0:T(8,128)S(1)}, f32[128,512]{1,0:T(8,128)S(1)}, /*index=5*/f32[128,512]{1,0:T(8,128)S(1)}) custom-call(s32[1]{0:T(128)} %bitcast.me_ref, bf16[64,512]{1,0:T(8,128)(2,1)S(1)} %add_select_fusion.refs_0_, ...), custom_call_target="tpu_custom_call" | custom-call | tf_op jit(solution)/shard_map/gram/pallas_call | solution.py:374
  32.2 0.5 collective-permute-start.10
  32.6 2.3 %kern_center.1 = (f32[4,5,128,128]{3,2,1,0:T(8,128)S(1)}, f32[4,4,128,128]{3,2,1,0:T(8,128)S(1)}) custom-call(s32[1]{0:T(128)} %bitcast.1.off_ref, bf16[512,512]{1,0:T(8,128)(2,1)S(1)} %get-tuple-element.40.panel_ref, bf16[128,512]{1,0:T(8,128)(2,1)S(1)} %get-tuple-element.41.own_ref), custom_call_target="tpu_custom_call" | custom-call | tf_op jit(solution)/shard_map/kern_center/pallas_call | solution.py:120
  34.9 0.2 collective-permute-done.10.other_ref
  35.1 0.1 pair_sum.1
  35.2 0.6 collective-permute-start.11
  35.8 1.2 %collective-permute-start.12 = (f32[128,512]{1,0:T(8,128)S(1)}, f32[128,512]{1,0:T(8,128)S(1)}, u32[]{:S(2)}, u32[]{:S(2)}) collective-permute-start(f32[128,512]{1,0:T(8,128)S(1)} %get-tuple-element.51), channel_id=1, source_target_pairs={{0,16},{4,20},{8,24},{12,28},{16,0},{20,4},{24,8},{28,12},{1,17},{... | collective-permute-start | bytes 786440 | tf_op jit(solution)/shard_map/ppermute | solution.py:397
  37.0 1.8 %collective-permute-start.13 = (f32[128,512]{1,0:T(8,128)S(1)}, f32[128,512]{1,0:T(8,128)S(1)}, u32[]{:S(2)}, u32[]{:S(2)}) collective-permute-start(f32[128,512]{1,0:T(8,128)S(1)} %get-tuple-element.52), channel_id=1, source_target_pairs={{0,24},{4,28},{8,16},{12,20},{16,8},{20,12},{24,0},{28,4},{1,25},{... | collective-permute-start | bytes 786440 | tf_op jit(solution)/shard_map/ppermute | solution.py:397
  38.8 26.2 %chol.1 = (f32[128,512]{1,0:T(8,128)}, f32[512,512]{1,0:T(8,128)}) custom-call(f32[4,5,128,128]{3,2,1,0:T(8,128)S(1)} %get-tuple-element.53.ain_ref, f32[4,4,128,128]{3,2,1,0:T(8,128)S(1)} %get-tuple-element.54.sin_ref), custom_call_target="tpu_custom_call" | custom-call | tf_op jit(solution)/shard_map/chol/pallas_call | solution.py:199
  65.0 0.0 collective-permute-done.11.refs_1_
  65.0 0.0 collective-permute-done.12.refs_2_
  65.0 0.0 collective-permute-done.13.refs_3_
  65.1 0.8 %gram_sum.1 = f32[128,512]{1,0:T(8,128)} custom-call(f32[128,512]{1,0:T(8,128)S(1)} %get-tuple-element.49.refs_0_, f32[128,512]{1,0:T(8,128)S(1)} %collective-permute-done.11.refs_1_, f32[128,512]{1,0:T(8,128)S(1)} %collective-permute-done.12.refs_2_, f32[128,512]{1,0:T(8,128)S(1)} %collective-permute-done.13.refs_3_), custom_call_target="tpu_custom_call" | custom-call | tf_op jit(solution)/shard_map/gram_sum/pallas_call | solution.py:273
Async XLA Ops:
  1.5 11.5 %collective-permute-start.2 = (bf16[64,512]{1,0:T(8,128)(2,1)S(1)}, bf16[64,512]{1,0:T(8,128)(2,1)S(1)}, u32[]{:S(2)}, u32[]{:S(2)}) collective-permute-start(bf16[64,512]{1,0:T(8,128)(2,1)S(1)} %constant_dynamic-slice_fusion), channel_id=1, source_target_pairs={{0,3},{4,7},{8,11},{12,15},{16,19},{20,23},{24,27},{28,31}} | collective-permute-start | bytes 196616 | tf_op jit(solution)/shard_map/ppermute | solution.py:405
  8.5 4.5 %collective-permute-start.1 = (bf16[64,512]{1,0:T(8,128)(2,1)S(1)}, bf16[64,512]{1,0:T(8,128)(2,1)S(1)}, u32[]{:S(2)}, u32[]{:S(2)}) collective-permute-start(bf16[64,512]{1,0:T(8,128)(2,1)S(1)} %constant_dynamic-slice_fusion), channel_id=1, source_target_pairs={{0,2},{4,6},{8,10},{12,14},{16,18},{20,22},{24,26},{28,30}} | collective-permute-start | bytes 196616 | tf_op jit(solution)/shard_map/ppermute | solution.py:405
  9.8 3.3 %collective-permute-start = (bf16[64,512]{1,0:T(8,128)(2,1)S(1)}, bf16[64,512]{1,0:T(8,128)(2,1)S(1)}, u32[]{:S(2)}, u32[]{:S(2)}) collective-permute-start(bf16[64,512]{1,0:T(8,128)(2,1)S(1)} %constant_dynamic-slice_fusion), channel_id=1, source_target_pairs={{0,1},{4,5},{8,9},{12,13},{16,17},{20,21},{24,25},{28,29}} | collective-permute-start | bytes 196616 | tf_op jit(solution)/shard_map/ppermute | solution.py:405
  13.9 5.3 %collective-permute-start.9 = (bf16[64,512]{1,0:T(8,128)(2,1)S(1)}, bf16[64,512]{1,0:T(8,128)(2,1)S(1)}, u32[]{:S(2)}, u32[]{:S(2)}) collective-permute-start(bf16[64,512]{1,0:T(8,128)(2,1)S(1)} %add_select_fusion.refs_0_), channel_id=1, source_target_pairs={{0,28},{4,24},{8,20},{12,16},{16,12},{20,8},{24,4},{28,0},{1,29},{... | collective-permute-start | bytes 196616 | tf_op jit(solution)/shard_map/ppermute | solution.py:397
  15.6 6.0 %collective-permute-start.8 = (bf16[64,512]{1,0:T(8,128)(2,1)S(1)}, bf16[64,512]{1,0:T(8,128)(2,1)S(1)}, u32[]{:S(2)}, u32[]{:S(2)}) collective-permute-start(bf16[64,512]{1,0:T(8,128)(2,1)S(1)} %add_select_fusion.refs_0_), channel_id=1, source_target_pairs={{0,24},{4,28},{8,16},{12,20},{16,8},{20,12},{24,0},{28,4},{1,25},{... | collective-permute-start | bytes 196616 | tf_op jit(solution)/shard_map/ppermute | solution.py:397
  16.5 10.4 %collective-permute-start.7 = (bf16[64,512]{1,0:T(8,128)(2,1)S(1)}, bf16[64,512]{1,0:T(8,128)(2,1)S(1)}, u32[]{:S(2)}, u32[]{:S(2)}) collective-permute-start(bf16[64,512]{1,0:T(8,128)(2,1)S(1)} %add_select_fusion.refs_0_), channel_id=1, source_target_pairs={{0,20},{4,16},{8,28},{12,24},{16,4},{20,0},{24,12},{28,8},{1,21},{... | collective-permute-start | bytes 196616 | tf_op jit(solution)/shard_map/ppermute | solution.py:397
  17.9 9.0 %collective-permute-start.6 = (bf16[64,512]{1,0:T(8,128)(2,1)S(1)}, bf16[64,512]{1,0:T(8,128)(2,1)S(1)}, u32[]{:S(2)}, u32[]{:S(2)}) collective-permute-start(bf16[64,512]{1,0:T(8,128)(2,1)S(1)} %add_select_fusion.refs_0_), channel_id=1, source_target_pairs={{0,16},{4,20},{8,24},{12,28},{16,0},{20,4},{24,8},{28,12},{1,17},{... | collective-permute-start | bytes 196616 | tf_op jit(solution)/shard_map/ppermute | solution.py:397
  18.4 8.5 %collective-permute-start.5 = (bf16[64,512]{1,0:T(8,128)(2,1)S(1)}, bf16[64,512]{1,0:T(8,128)(2,1)S(1)}, u32[]{:S(2)}, u32[]{:S(2)}) collective-permute-start(bf16[64,512]{1,0:T(8,128)(2,1)S(1)} %add_select_fusion.refs_0_), channel_id=1, source_target_pairs={{0,12},{4,8},{8,4},{12,0},{16,28},{20,24},{24,20},{28,16},{1,13},{... | collective-permute-start | bytes 196616 | tf_op jit(solution)/shard_map/ppermute | solution.py:397
  19.2 7.7 %collective-permute-start.4 = (bf16[64,512]{1,0:T(8,128)(2,1)S(1)}, bf16[64,512]{1,0:T(8,128)(2,1)S(1)}, u32[]{:S(2)}, u32[]{:S(2)}) collective-permute-start(bf16[64,512]{1,0:T(8,128)(2,1)S(1)} %add_select_fusion.refs_0_), channel_id=1, source_target_pairs={{0,8},{4,12},{8,0},{12,4},{16,24},{20,28},{24,16},{28,20},{1,9},{5... | collective-permute-start | bytes 196616 | tf_op jit(solution)/shard_map/ppermute | solution.py:397
  21.5 5.4 %collective-permute-start.3 = (bf16[64,512]{1,0:T(8,128)(2,1)S(1)}, bf16[64,512]{1,0:T(8,128)(2,1)S(1)}, u32[]{:S(2)}, u32[]{:S(2)}) collective-permute-start(bf16[64,512]{1,0:T(8,128)(2,1)S(1)} %add_select_fusion.refs_0_), channel_id=1, source_target_pairs={{0,4},{4,0},{8,12},{12,8},{16,20},{20,16},{24,28},{28,24},{1,5},{5... | collective-permute-start | bytes 196616 | tf_op jit(solution)/shard_map/ppermute | solution.py:397
  32.2 2.9 %collective-permute-start.10 = (f32[4,128,512]{2,1,0:T(8,128)}, f32[4,128,512]{2,1,0:T(8,128)S(1)}, u32[]{:S(2)}, u32[]{:S(2)}) collective-permute-start(f32[4,128,512]{2,1,0:T(8,128)} %get-tuple-element.39), channel_id=1, source_target_pairs={{0,4},{4,0},{8,12},{12,8},{16,20},{20,16},{24,28},{28,24},{1,5},{5... | collective-permute-start | bytes 3145736 | tf_op jit(solution)/shard_map/ppermute | solution.py:397
  35.2 29.8 %collective-permute-start.11 = (f32[128,512]{1,0:T(8,128)S(1)}, f32[128,512]{1,0:T(8,128)S(1)}, u32[]{:S(2)}, u32[]{:S(2)}) collective-permute-start(f32[128,512]{1,0:T(8,128)S(1)} %get-tuple-element.50), channel_id=1, source_target_pairs={{0,8},{4,12},{8,0},{12,4},{16,24},{20,28},{24,16},{28,20},{1,9},{5... | collective-permute-start | bytes 786440 | tf_op jit(solution)/shard_map/ppermute | solution.py:397
  35.8 29.2 %collective-permute-start.12 = (f32[128,512]{1,0:T(8,128)S(1)}, f32[128,512]{1,0:T(8,128)S(1)}, u32[]{:S(2)}, u32[]{:S(2)}) collective-permute-start(f32[128,512]{1,0:T(8,128)S(1)} %get-tuple-element.51), channel_id=1, source_target_pairs={{0,16},{4,20},{8,24},{12,28},{16,0},{20,4},{24,8},{28,12},{1,17},{... | collective-permute-start | bytes 786440 | tf_op jit(solution)/shard_map/ppermute | solution.py:397
  37.0 28.1 %collective-permute-start.13 = (f32[128,512]{1,0:T(8,128)S(1)}, f32[128,512]{1,0:T(8,128)S(1)}, u32[]{:S(2)}, u32[]{:S(2)}) collective-permute-start(f32[128,512]{1,0:T(8,128)S(1)} %get-tuple-element.52), channel_id=1, source_target_pairs={{0,24},{4,28},{8,16},{12,20},{16,8},{20,12},{24,0},{28,4},{1,25},{... | collective-permute-start | bytes 786440 | tf_op jit(solution)/shard_map/ppermute | solution.py:397

commit v5 on v4

--- a/solution.py
+++ b/solution.py
@@ -53,8 +53,7 @@
             for r,w,u,m in probs:
                 ub=u[base:e,:]; mb=m[base:e,:]
                 zs.append(mmul(ub.T[e:,:],jnp.concatenate([ub,mb],axis=1)))
-            gaps=B//VB-1
-            for f in fills[b::gaps]: f()
+            for f in fills[b:b+1]: f()
             for (r,w,u,m),z in zip(probs,zs):
                 r[e:,:]=r[e:,:]-z[:,:B]
                 w[e:,:]=w[e:,:]-z[:,B:]
@@ -92,7 +91,7 @@
     for j in range(len(row)):
         v=un[:,j*B:(j+1)*B]
         if j<nb:
-            v=jnp.where(j>K,v,0.0); v=jnp.where(j==K,uk,v)
+            v=uk if isinstance(K,int) and j==K else jnp.where(j==K,uk,jnp.where(j>K,v,0.0))
         u_ref[K,j]=v
         l_ref[j,K]=v.T
 
@@ -123,14 +122,16 @@
         compiler_params=pltpu.CompilerParams(vmem_limit_bytes=16<<20),
         name='kern_center')(off,panel,own)
 
-def body(ain_ref,sin_ref,chol_ref,prec_ref,a_ref,u_ref,l_ref,s_ref,v_ref,h_ref,ms_ref,r0,w0,k0,m0,r1,w1,k1,m1):
+def body(ain_ref,sin_ref,chol_ref,prec_ref,a_ref,u_ref,l_ref,s_ref,v_ref,h_ref,ms_ref,ks_ref,mc_ref,kc_ref,r0,w0,k0,m0,r1,w1,k1,m1):
     nb,nj=ain_ref.shape[:2]; no=nj-nb
     eye=lax.broadcasted_iota(jnp.int32,(B,B),0)==lax.broadcasted_iota(jnp.int32,(B,B),1)
     zero=jnp.zeros((B,B),jnp.float32)
     for j in range(nj):
-        u_ref[nb,j]=zero; l_ref[j,nb]=zero
+        u_ref[nb,j]=zero; l_ref[j,nb]=zero; a_ref[nb,j]=zero
     for j in range(nb):
         v_ref[nb,j]=zero; h_ref[j,nb]=zero
+    for j in range(nb): s_ref[nb,j]=zero
+    for ref in (ms_ref,ks_ref,mc_ref,kc_ref): ref[nb]=zero
     top=None
     for i in range(nb):
         for j in range(nj): a_ref[i,j]=ain_ref[i,j]
@@ -140,17 +141,26 @@
     r0[...]=ain_ref[0,0]; r1[...]=sin_ref[0,0]
     def step(K,low):
         Kp=jnp.where(K==0,nb,K-1)
-        fills=trail(a_ref,u_ref,l_ref,Kp,nb,nj)+trail(s_ref,v_ref,h_ref,Kp,nb,nb)[::-1]
-        factor128([(r0,w0,k0,m0),(r1,w1,k1,m1)],fills)
-        ms_ref[K]=m0[...]
-        put(m0[...],k0[...],[a_ref[K,j] for j in range(nj)],K,nb,u_ref,l_ref)
-        put(m1[...],k1[...],[s_ref[K,j] for j in range(nb)],K,nb,v_ref,h_ref)
+        tl=trail(a_ref,u_ref,l_ref,Kp,nb,nj); tc=trail(s_ref,v_ref,h_ref,Kp,nb,nb)
+        def rows():
+            put(ms_ref[Kp],ks_ref[Kp],[a_ref[Kp,j] for j in range(nj)],Kp,nb,u_ref,l_ref)
+            put(mc_ref[Kp],kc_ref[Kp],[s_ref[Kp,j] for j in range(nb)],Kp,nb,v_ref,h_ref)
+        def run(fs):
+            for f in fs: f()
+        half=len(tl)//2+1
+        factor128([(r0,w0,k0,m0),(r1,w1,k1,m1)],
+            [rows,functools.partial(run,tl[:half]+tc[:half-1]),functools.partial(run,tl[half:]+tc[half-1:])])
         K1=jnp.minimum(K+1,nb-1)
-        r0[...]=a_ref[K1,K1]-mmul(l_ref[K1,K],u_ref[K,K1])
-        r1[...]=s_ref[K1,K1]-mmul(h_ref[K1,K],v_ref[K,K1])
+        x0=mmul(m0[...],a_ref[K,K1]); x1=mmul(m1[...],s_ref[K,K1])
+        r0[...]=a_ref[K1,K1]-mmul(x0.T,x0)
+        r1[...]=s_ref[K1,K1]-mmul(x1.T,x1)
+        ms_ref[K]=m0[...]; ks_ref[K]=k0[...]; mc_ref[K]=m1[...]; kc_ref[K]=k1[...]
         x=k1[...]
         return jnp.minimum(low,jnp.where(eye,x*x,1e30))
     low=lax.fori_loop(0,nb,step,jnp.full((B,B),1e30,jnp.float32))
+    last=nb-1
+    put(ms_ref[last],ks_ref[last],[a_ref[last,j] for j in range(nj)],last,nb,u_ref,l_ref)
+    put(mc_ref[last],kc_ref[last],[s_ref[last,j] for j in range(nb)],last,nb,v_ref,h_ref)
     for i in range(no):
         for t in range(nb):
             chol_ref[i*B:(i+1)*B,t*B:(t+1)*B]=l_ref[nb+i,t]
@@ -181,7 +191,8 @@
         r1[...]=s_ref[0,0]
         def again(K,carry):
             Kp=jnp.where(K==0,nb,K-1)
-            factor128([(r1,w1,k1,m1)],trail(s_ref,v_ref,h_ref,Kp,nb,nb))
+            for f in trail(s_ref,v_ref,h_ref,Kp,nb,nb): f()
+            factor128([(r1,w1,k1,m1)])
             put(m1[...],k1[...],[s_ref[K,j] for j in range(nb)],K,nb,v_ref,h_ref)
             K1=jnp.minimum(K+1,nb-1)
             r1[...]=s_ref[K1,K1]-mmul(h_ref[K1,K],v_ref[K,K1])
@@ -199,7 +210,7 @@
     return pl.pallas_call(body,
         out_shape=(jax.ShapeDtypeStruct((no*B,nb*B),f32),jax.ShapeDtypeStruct((nb*B,nb*B),f32)),
         in_specs=[vm,vm],out_specs=(vm,vm),
-        scratch_shapes=[V(nb,nj),V(nb+1,nj),V(nj,nb+1),V(nb,nb),V(nb+1,nb),V(nb,nb+1),V(nb)]+[V()]*8,
+        scratch_shapes=[V(nb+1,nj),V(nb+1,nj),V(nj,nb+1),V(nb+1,nb),V(nb+1,nb),V(nb,nb+1)]+[V(nb+1)]*4+[V()]*8,
         compiler_params=pltpu.CompilerParams(vmem_limit_bytes=24<<20),
         name='chol')(a,s)
 

time: 66.1 us -> 64.7 us (0.979)
  Pallas kernels: 41.8 us -> 40.4 us
    pallas_call x1, Pallas kernels: 26.2 us -> 24.9 us  [factor_kernel(): pl.pallas_call(body, out_shape=(jax.ShapeDtypeStruct((no * B, nb * B), f3...]
  transfers between devices with their start and end apart: 14 -> 14, of which waited for: 3 -> 3; matrix products, arithmetic and copies ran while one was open for 0% -> 0% of each run, Pallas kernels for 54% -> 53%
where the time goes in v5:
time: 64.7 us; the launch traced here: 64.4 us
  Pallas kernels  40.4 us (62%)
  starting transfers between devices  20.1 us (31%)
  waiting for transfers between devices  1.42 us (2%)
  other arithmetic  0.87 us (1%)
  local copies, waits for them, and re-layouts  0.85 us (1%)
  between operations  0.76 us (1%)
    pallas_call x1, Pallas kernels, factor_kernel(): pl.pallas_call(body, out_shape=(jax.ShapeDtypeStruct((no * B, nb * B), f3...  24.9 us
    ppermute x11, starting transfers between devices, swap(): return lax.ppermute(x, axis, [(i, i ^ d) for i in range(n)])  10.5 us
    ppermute x3, starting transfers between devices, panel_pieces(): got = [lax.ppermute(chunk, 'ctr', [(0, d)]) for d in range(1, ctrs)]  9.56 us
    pallas_call x1, Pallas kernels, own_kernel(): pl.pallas_call(functools.partial(own_body, row_dev=row_dev), in_specs=[pl...  5.3 us
    pallas_call x1, Pallas kernels, gram_kernel(): pl.pallas_call(functools.partial(gram_body, samps=samps, tile=tile), in_s...  5.26 us
    pallas_call x1, Pallas kernels, init_kernel(): pl.pallas_call(functools.partial(init_body, own=ro), out_shape=(V(nb, nb...  2.27 us
    pallas_call x1, Pallas kernels, load_kernel(): pl.pallas_call(functools.partial(load_body, parts=parts), in_specs=[outsi...  1.89 us
    ppermute x11, waiting for transfers between devices, swap(): return lax.ppermute(x, axis, [(i, i ^ d) for i in range(n)])  1.37 us
  transfers between devices with their start and end apart: 14, of which 3 were waited for; matrix products, arithmetic and copies ran while one was open for 0% of the time, Pallas kernels for 53%

profile of v5, /device:TPU:0, one launch (start us, length us, event | category | flops | bytes accessed | tf_op | source)
XLA Modules:
  0.0 64.4 jit_solution(6770486952968505711)
XLA Ops:
  0.6 0.8 %constant_dynamic-slice_fusion = bf16[64,512]{1,0:T(8,128)(2,1)S(1)} fusion(bf16[1024,512]{1,0:T(8,128)(2,1)} %c_hbm.1, s32[]{:T(128)S(6)} %select_n.12), kind=kLoop, calls=%fused_computation.1 | loop fusion | bytes 131076 | tf_op jit(solution)/shard_map/dynamic_slice | solution.py:415
  1.5 7.0 %collective-permute-start.2 = (bf16[64,512]{1,0:T(8,128)(2,1)S(1)}, bf16[64,512]{1,0:T(8,128)(2,1)S(1)}, u32[]{:S(2)}, u32[]{:S(2)}) collective-permute-start(bf16[64,512]{1,0:T(8,128)(2,1)S(1)} %constant_dynamic-slice_fusion), channel_id=1, source_target_pairs={{0,3},{4,7},{8,11},{12,15},{16,19},{20,23},{24,27},{28,31}} | collective-permute-start | bytes 196616 | tf_op jit(solution)/shard_map/ppermute | solution.py:416
  8.5 1.3 %collective-permute-start.1 = (bf16[64,512]{1,0:T(8,128)(2,1)S(1)}, bf16[64,512]{1,0:T(8,128)(2,1)S(1)}, u32[]{:S(2)}, u32[]{:S(2)}) collective-permute-start(bf16[64,512]{1,0:T(8,128)(2,1)S(1)} %constant_dynamic-slice_fusion), channel_id=1, source_target_pairs={{0,2},{4,6},{8,10},{12,14},{16,18},{20,22},{24,26},{28,30}} | collective-permute-start | bytes 196616 | tf_op jit(solution)/shard_map/ppermute | solution.py:416
  9.8 1.3 %collective-permute-start = (bf16[64,512]{1,0:T(8,128)(2,1)S(1)}, bf16[64,512]{1,0:T(8,128)(2,1)S(1)}, u32[]{:S(2)}, u32[]{:S(2)}) collective-permute-start(bf16[64,512]{1,0:T(8,128)(2,1)S(1)} %constant_dynamic-slice_fusion), channel_id=1, source_target_pairs={{0,1},{4,5},{8,9},{12,13},{16,17},{20,21},{24,25},{28,29}} | collective-permute-start | bytes 196616 | tf_op jit(solution)/shard_map/ppermute | solution.py:416
  11.1 1.9 %load.1 = (bf16[1024,512]{1,0:T(8,128)(2,1)S(1)}, bf16[2048,512]{1,0:T(8,128)(2,1)S(1)}) custom-call(bf16[1024,512]{1,0:T(8,128)(2,1)} %c_hbm.1, bf16[2048,512]{1,0:T(8,128)(2,1)} %s_hbm.1), custom_call_target="tpu_custom_call" | custom-call | tf_op jit(solution)/shard_map/load/pallas_call | solution.py:246
  13.0 0.0 collective-permute-done.2
  13.0 0.0 collective-permute-done.1
  13.0 0.0 collective-permute-done
  13.0 0.9 %add_select_fusion.refs_0_ = bf16[64,512]{1,0:T(8,128)(2,1)S(1)} fusion(bf16[64,512]{1,0:T(8,128)(2,1)S(1)} %collective-permute-done.2, bf16[64,512]{1,0:T(8,128)(2,1)S(1)} %collective-permute-done, bf16[64,512]{1,0:T(8,128)(2,1)S(1)} %collective-permute-done.1, pred[]{:T(512)S(6)} %eq.3, bf16[1024,512]{1,0:T(8,128)(2,1)} %c_hbm.1, s32[]{:T(128)S(6)} %select_n.12), kind=kLoop, calls=%fused_computation | loop fusion | flops 229376 | bytes 327685 | tf_op jit(solution)/shard_map/jit(_where)/select_n | solution.py:421
  13.9 1.6 %collective-permute-start.9 = (bf16[64,512]{1,0:T(8,128)(2,1)S(1)}, bf16[64,512]{1,0:T(8,128)(2,1)S(1)}, u32[]{:S(2)}, u32[]{:S(2)}) collective-permute-start(bf16[64,512]{1,0:T(8,128)(2,1)S(1)} %add_select_fusion.refs_0_), channel_id=1, source_target_pairs={{0,28},{4,24},{8,20},{12,16},{16,12},{20,8},{24,4},{28,0},{1,29},{... | collective-permute-start | bytes 196616 | tf_op jit(solution)/shard_map/ppermute | solution.py:408
  15.6 0.9 %collective-permute-start.8 = (bf16[64,512]{1,0:T(8,128)(2,1)S(1)}, bf16[64,512]{1,0:T(8,128)(2,1)S(1)}, u32[]{:S(2)}, u32[]{:S(2)}) collective-permute-start(bf16[64,512]{1,0:T(8,128)(2,1)S(1)} %add_select_fusion.refs_0_), channel_id=1, source_target_pairs={{0,24},{4,28},{8,16},{12,20},{16,8},{20,12},{24,0},{28,4},{1,25},{... | collective-permute-start | bytes 196616 | tf_op jit(solution)/shard_map/ppermute | solution.py:408
  16.5 1.4 %collective-permute-start.7 = (bf16[64,512]{1,0:T(8,128)(2,1)S(1)}, bf16[64,512]{1,0:T(8,128)(2,1)S(1)}, u32[]{:S(2)}, u32[]{:S(2)}) collective-permute-start(bf16[64,512]{1,0:T(8,128)(2,1)S(1)} %add_select_fusion.refs_0_), channel_id=1, source_target_pairs={{0,20},{4,16},{8,28},{12,24},{16,4},{20,0},{24,12},{28,8},{1,21},{... | collective-permute-start | bytes 196616 | tf_op jit(solution)/shard_map/ppermute | solution.py:408
  17.9 0.5 collective-permute-start.6
  18.4 0.7 %collective-permute-start.5 = (bf16[64,512]{1,0:T(8,128)(2,1)S(1)}, bf16[64,512]{1,0:T(8,128)(2,1)S(1)}, u32[]{:S(2)}, u32[]{:S(2)}) collective-permute-start(bf16[64,512]{1,0:T(8,128)(2,1)S(1)} %add_select_fusion.refs_0_), channel_id=1, source_target_pairs={{0,12},{4,8},{8,4},{12,0},{16,28},{20,24},{24,20},{28,16},{1,13},{... | collective-permute-start | bytes 196616 | tf_op jit(solution)/shard_map/ppermute | solution.py:408
  19.1 0.1 collective-permute-done.9.refs_7_
  19.2 1.3 %collective-permute-start.4 = (bf16[64,512]{1,0:T(8,128)(2,1)S(1)}, bf16[64,512]{1,0:T(8,128)(2,1)S(1)}, u32[]{:S(2)}, u32[]{:S(2)}) collective-permute-start(bf16[64,512]{1,0:T(8,128)(2,1)S(1)} %add_select_fusion.refs_0_), channel_id=1, source_target_pairs={{0,8},{4,12},{8,0},{12,4},{16,24},{20,28},{24,16},{28,20},{1,9},{5... | collective-permute-start | bytes 196616 | tf_op jit(solution)/shard_map/ppermute | solution.py:408
  20.5 1.0 %collective-permute-done.8.refs_6_ = bf16[64,512]{1,0:T(8,128)(2,1)S(1)} collective-permute-done((bf16[64,512]{1,0:T(8,128)(2,1)S(1)}, bf16[64,512]{1,0:T(8,128)(2,1)S(1)}, u32[]{:S(2)}, u32[]{:S(2)}) %collective-permute-start.8) | collective-permute-done | bytes 65568 | tf_op jit(solution)/shard_map/ppermute | solution.py:408
  21.5 0.1 collective-permute-start.3
  21.6 5.3 %kern_own.1 = (bf16[1024,2048]{1,0:T(8,128)(2,1)S(1)}, f32[2048,128]{1,0:T(8,128)S(1)}, bf16[128,512]{1,0:T(8,128)(2,1)S(1)}) custom-call(s32[1]{0:T(128)} %bitcast.me_ref, bf16[1024,512]{1,0:T(8,128)(2,1)S(1)} %get-tuple-element.35.c_ref, bf16[2048,512]{1,0:T(8,128)(2,1)S(1)} %get-tuple-element.36.s_ref.refs_9_), custom_call_target="tpu_custom_call" | custom-call | tf_op jit(solution)/shard_map/kern_own/pallas_call | solution.py:343
  26.9 0.0 collective-permute-done.7.refs_5_
  26.9 0.0 collective-permute-done.6.refs_4_
  26.9 0.0 collective-permute-done.5.refs_3_
  26.9 0.0 collective-permute-done.4.refs_2_
  26.9 0.0 collective-permute-done.3.refs_1_
  26.9 5.3 %gram.1 = (bf16[512,512]{1,0:T(8,128)(2,1)S(1)}, f32[4,128,512]{2,1,0:T(8,128)}, f32[128,512]{1,0:T(8,128)S(1)}, f32[128,512]{1,0:T(8,128)S(1)}, f32[128,512]{1,0:T(8,128)S(1)}, /*index=5*/f32[128,512]{1,0:T(8,128)S(1)}) custom-call(s32[1]{0:T(128)} %bitcast.me_ref, bf16[64,512]{1,0:T(8,128)(2,1)S(1)} %add_select_fusion.refs_0_, ...), custom_call_target="tpu_custom_call" | custom-call | tf_op jit(solution)/shard_map/gram/pallas_call | solution.py:385
  32.2 0.5 collective-permute-start.10
  32.6 2.3 %kern_center.1 = (f32[4,5,128,128]{3,2,1,0:T(8,128)S(1)}, f32[4,4,128,128]{3,2,1,0:T(8,128)S(1)}) custom-call(s32[1]{0:T(128)} %bitcast.1.off_ref, bf16[512,512]{1,0:T(8,128)(2,1)S(1)} %get-tuple-element.40.panel_ref, bf16[128,512]{1,0:T(8,128)(2,1)S(1)} %get-tuple-element.41.own_ref), custom_call_target="tpu_custom_call" | custom-call | tf_op jit(solution)/shard_map/kern_center/pallas_call | solution.py:119
  34.9 0.2 collective-permute-done.10.other_ref
  35.1 0.1 pair_sum.1
  35.2 0.6 collective-permute-start.11
  35.8 1.2 %collective-permute-start.12 = (f32[128,512]{1,0:T(8,128)S(1)}, f32[128,512]{1,0:T(8,128)S(1)}, u32[]{:S(2)}, u32[]{:S(2)}) collective-permute-start(f32[128,512]{1,0:T(8,128)S(1)} %get-tuple-element.51), channel_id=1, source_target_pairs={{0,16},{4,20},{8,24},{12,28},{16,0},{20,4},{24,8},{28,12},{1,17},{... | collective-permute-start | bytes 786440 | tf_op jit(solution)/shard_map/ppermute | solution.py:408
  37.0 1.8 %collective-permute-start.13 = (f32[128,512]{1,0:T(8,128)S(1)}, f32[128,512]{1,0:T(8,128)S(1)}, u32[]{:S(2)}, u32[]{:S(2)}) collective-permute-start(f32[128,512]{1,0:T(8,128)S(1)} %get-tuple-element.52), channel_id=1, source_target_pairs={{0,24},{4,28},{8,16},{12,20},{16,8},{20,12},{24,0},{28,4},{1,25},{... | collective-permute-start | bytes 786440 | tf_op jit(solution)/shard_map/ppermute | solution.py:408
  38.8 24.9 %chol.1 = (f32[128,512]{1,0:T(8,128)}, f32[512,512]{1,0:T(8,128)}) custom-call(f32[4,5,128,128]{3,2,1,0:T(8,128)S(1)} %get-tuple-element.53.ain_ref, f32[4,4,128,128]{3,2,1,0:T(8,128)S(1)} %get-tuple-element.54.sin_ref), custom_call_target="tpu_custom_call" | custom-call | tf_op jit(solution)/shard_map/chol/pallas_call | solution.py:210
  63.7 0.0 collective-permute-done.11.refs_1_
  63.7 0.0 collective-permute-done.12.refs_2_
  63.7 0.0 collective-permute-done.13.refs_3_
  63.7 0.8 %gram_sum.1 = f32[128,512]{1,0:T(8,128)} custom-call(f32[128,512]{1,0:T(8,128)S(1)} %get-tuple-element.49.refs_0_, f32[128,512]{1,0:T(8,128)S(1)} %collective-permute-done.11.refs_1_, f32[128,512]{1,0:T(8,128)S(1)} %collective-permute-done.12.refs_2_, f32[128,512]{1,0:T(8,128)S(1)} %collective-permute-done.13.refs_3_), custom_call_target="tpu_custom_call" | custom-call | tf_op jit(solution)/shard_map/gram_sum/pallas_call | solution.py:284
Async XLA Ops:
  1.5 11.5 %collective-permute-start.2 = (bf16[64,512]{1,0:T(8,128)(2,1)S(1)}, bf16[64,512]{1,0:T(8,128)(2,1)S(1)}, u32[]{:S(2)}, u32[]{:S(2)}) collective-permute-start(bf16[64,512]{1,0:T(8,128)(2,1)S(1)} %constant_dynamic-slice_fusion), channel_id=1, source_target_pairs={{0,3},{4,7},{8,11},{12,15},{16,19},{20,23},{24,27},{28,31}} | collective-permute-start | bytes 196616 | tf_op jit(solution)/shard_map/ppermute | solution.py:416
  8.5 4.5 %collective-permute-start.1 = (bf16[64,512]{1,0:T(8,128)(2,1)S(1)}, bf16[64,512]{1,0:T(8,128)(2,1)S(1)}, u32[]{:S(2)}, u32[]{:S(2)}) collective-permute-start(bf16[64,512]{1,0:T(8,128)(2,1)S(1)} %constant_dynamic-slice_fusion), channel_id=1, source_target_pairs={{0,2},{4,6},{8,10},{12,14},{16,18},{20,22},{24,26},{28,30}} | collective-permute-start | bytes 196616 | tf_op jit(solution)/shard_map/ppermute | solution.py:416
  9.8 3.3 %collective-permute-start = (bf16[64,512]{1,0:T(8,128)(2,1)S(1)}, bf16[64,512]{1,0:T(8,128)(2,1)S(1)}, u32[]{:S(2)}, u32[]{:S(2)}) collective-permute-start(bf16[64,512]{1,0:T(8,128)(2,1)S(1)} %constant_dynamic-slice_fusion), channel_id=1, source_target_pairs={{0,1},{4,5},{8,9},{12,13},{16,17},{20,21},{24,25},{28,29}} | collective-permute-start | bytes 196616 | tf_op jit(solution)/shard_map/ppermute | solution.py:416
  13.9 5.3 %collective-permute-start.9 = (bf16[64,512]{1,0:T(8,128)(2,1)S(1)}, bf16[64,512]{1,0:T(8,128)(2,1)S(1)}, u32[]{:S(2)}, u32[]{:S(2)}) collective-permute-start(bf16[64,512]{1,0:T(8,128)(2,1)S(1)} %add_select_fusion.refs_0_), channel_id=1, source_target_pairs={{0,28},{4,24},{8,20},{12,16},{16,12},{20,8},{24,4},{28,0},{1,29},{... | collective-permute-start | bytes 196616 | tf_op jit(solution)/shard_map/ppermute | solution.py:408
  15.6 6.0 %collective-permute-start.8 = (bf16[64,512]{1,0:T(8,128)(2,1)S(1)}, bf16[64,512]{1,0:T(8,128)(2,1)S(1)}, u32[]{:S(2)}, u32[]{:S(2)}) collective-permute-start(bf16[64,512]{1,0:T(8,128)(2,1)S(1)} %add_select_fusion.refs_0_), channel_id=1, source_target_pairs={{0,24},{4,28},{8,16},{12,20},{16,8},{20,12},{24,0},{28,4},{1,25},{... | collective-permute-start | bytes 196616 | tf_op jit(solution)/shard_map/ppermute | solution.py:408
  16.5 10.4 %collective-permute-start.7 = (bf16[64,512]{1,0:T(8,128)(2,1)S(1)}, bf16[64,512]{1,0:T(8,128)(2,1)S(1)}, u32[]{:S(2)}, u32[]{:S(2)}) collective-permute-start(bf16[64,512]{1,0:T(8,128)(2,1)S(1)} %add_select_fusion.refs_0_), channel_id=1, source_target_pairs={{0,20},{4,16},{8,28},{12,24},{16,4},{20,0},{24,12},{28,8},{1,21},{... | collective-permute-start | bytes 196616 | tf_op jit(solution)/shard_map/ppermute | solution.py:408
  17.9 9.0 %collective-permute-start.6 = (bf16[64,512]{1,0:T(8,128)(2,1)S(1)}, bf16[64,512]{1,0:T(8,128)(2,1)S(1)}, u32[]{:S(2)}, u32[]{:S(2)}) collective-permute-start(bf16[64,512]{1,0:T(8,128)(2,1)S(1)} %add_select_fusion.refs_0_), channel_id=1, source_target_pairs={{0,16},{4,20},{8,24},{12,28},{16,0},{20,4},{24,8},{28,12},{1,17},{... | collective-permute-start | bytes 196616 | tf_op jit(solution)/shard_map/ppermute | solution.py:408
  18.4 8.5 %collective-permute-start.5 = (bf16[64,512]{1,0:T(8,128)(2,1)S(1)}, bf16[64,512]{1,0:T(8,128)(2,1)S(1)}, u32[]{:S(2)}, u32[]{:S(2)}) collective-permute-start(bf16[64,512]{1,0:T(8,128)(2,1)S(1)} %add_select_fusion.refs_0_), channel_id=1, source_target_pairs={{0,12},{4,8},{8,4},{12,0},{16,28},{20,24},{24,20},{28,16},{1,13},{... | collective-permute-start | bytes 196616 | tf_op jit(solution)/shard_map/ppermute | solution.py:408
  19.2 7.7 %collective-permute-start.4 = (bf16[64,512]{1,0:T(8,128)(2,1)S(1)}, bf16[64,512]{1,0:T(8,128)(2,1)S(1)}, u32[]{:S(2)}, u32[]{:S(2)}) collective-permute-start(bf16[64,512]{1,0:T(8,128)(2,1)S(1)} %add_select_fusion.refs_0_), channel_id=1, source_target_pairs={{0,8},{4,12},{8,0},{12,4},{16,24},{20,28},{24,16},{28,20},{1,9},{5... | collective-permute-start | bytes 196616 | tf_op jit(solution)/shard_map/ppermute | solution.py:408
  21.5 5.4 %collective-permute-start.3 = (bf16[64,512]{1,0:T(8,128)(2,1)S(1)}, bf16[64,512]{1,0:T(8,128)(2,1)S(1)}, u32[]{:S(2)}, u32[]{:S(2)}) collective-permute-start(bf16[64,512]{1,0:T(8,128)(2,1)S(1)} %add_select_fusion.refs_0_), channel_id=1, source_target_pairs={{0,4},{4,0},{8,12},{12,8},{16,20},{20,16},{24,28},{28,24},{1,5},{5... | collective-permute-start | bytes 196616 | tf_op jit(solution)/shard_map/ppermute | solution.py:408
  32.2 2.9 %collective-permute-start.10 = (f32[4,128,512]{2,1,0:T(8,128)}, f32[4,128,512]{2,1,0:T(8,128)S(1)}, u32[]{:S(2)}, u32[]{:S(2)}) collective-permute-start(f32[4,128,512]{2,1,0:T(8,128)} %get-tuple-element.39), channel_id=1, source_target_pairs={{0,4},{4,0},{8,12},{12,8},{16,20},{20,16},{24,28},{28,24},{1,5},{5... | collective-permute-start | bytes 3145736 | tf_op jit(solution)/shard_map/ppermute | solution.py:408
  35.2 28.4 %collective-permute-start.11 = (f32[128,512]{1,0:T(8,128)S(1)}, f32[128,512]{1,0:T(8,128)S(1)}, u32[]{:S(2)}, u32[]{:S(2)}) collective-permute-start(f32[128,512]{1,0:T(8,128)S(1)} %get-tuple-element.50), channel_id=1, source_target_pairs={{0,8},{4,12},{8,0},{12,4},{16,24},{20,28},{24,16},{28,20},{1,9},{5... | collective-permute-start | bytes 786440 | tf_op jit(solution)/shard_map/ppermute | solution.py:408
  35.8 27.8 %collective-permute-start.12 = (f32[128,512]{1,0:T(8,128)S(1)}, f32[128,512]{1,0:T(8,128)S(1)}, u32[]{:S(2)}, u32[]{:S(2)}) collective-permute-start(f32[128,512]{1,0:T(8,128)S(1)} %get-tuple-element.51), channel_id=1, source_target_pairs={{0,16},{4,20},{8,24},{12,28},{16,0},{20,4},{24,8},{28,12},{1,17},{... | collective-permute-start | bytes 786440 | tf_op jit(solution)/shard_map/ppermute | solution.py:408
  37.0 26.7 %collective-permute-start.13 = (f32[128,512]{1,0:T(8,128)S(1)}, f32[128,512]{1,0:T(8,128)S(1)}, u32[]{:S(2)}, u32[]{:S(2)}) collective-permute-start(f32[128,512]{1,0:T(8,128)S(1)} %get-tuple-element.52), channel_id=1, source_target_pairs={{0,24},{4,28},{8,16},{12,20},{16,8},{20,12},{24,0},{28,4},{1,25},{... | collective-permute-start | bytes 786440 | tf_op jit(solution)/shard_map/ppermute | solution.py:408

commit v6 on v5

--- a/solution.py
+++ b/solution.py
@@ -308,10 +308,8 @@
 
 
 def col_norms(x, scale):
-    hi, lo = square_parts(x)
-    one = jnp.ones((x.shape[1], B), jnp.bfloat16)
-    dot = lambda a: jnp.dot(a, one, preferred_element_type=jnp.float32)
-    return (dot(hi) + dot(lo)) * scale
+    total = jnp.sum(jnp.square(x.astype(jnp.float32)), axis=1, keepdims=True) * scale
+    return jnp.broadcast_to(total, (x.shape[0], B))
 
 
 def kern_tile(x, y, xcol, yrow):

time: 64.7 us -> 63.9 us (0.988)
  Pallas kernels: 40.4 us -> 39.7 us
    pallas_call x1, Pallas kernels: 5.3 us -> 4.51 us  [own_kernel(): pl.pallas_call(functools.partial(own_body, row_dev=row_dev), in_specs=[pl...]
where the time goes in v6:
time: 63.9 us; the launch traced here: 63.6 us
  Pallas kernels  39.7 us (62%)
  starting transfers between devices  20.1 us (31%)
  waiting for transfers between devices  1.42 us (2%)
  other arithmetic  0.87 us (1%)
  local copies, waits for them, and re-layouts  0.85 us (1%)
  between operations  0.76 us (1%)
    pallas_call x1, Pallas kernels, factor_kernel(): pl.pallas_call(body, out_shape=(jax.ShapeDtypeStruct((no * B, nb * B), f3...  24.9 us
    ppermute x11, starting transfers between devices, swap(): return lax.ppermute(x, axis, [(i, i ^ d) for i in range(n)])  10.5 us
    ppermute x3, starting transfers between devices, panel_pieces(): got = [lax.ppermute(chunk, 'ctr', [(0, d)]) for d in range(1, ctrs)]  9.56 us
    pallas_call x1, Pallas kernels, gram_kernel(): pl.pallas_call(functools.partial(gram_body, samps=samps, tile=tile), in_s...  5.25 us
    pallas_call x1, Pallas kernels, own_kernel(): pl.pallas_call(functools.partial(own_body, row_dev=row_dev), in_specs=[pl...  4.51 us
    pallas_call x1, Pallas kernels, init_kernel(): pl.pallas_call(functools.partial(init_body, own=ro), out_shape=(V(nb, nb...  2.27 us
    pallas_call x1, Pallas kernels, load_kernel(): pl.pallas_call(functools.partial(load_body, parts=parts), in_specs=[outsi...  1.89 us
    ppermute x11, waiting for transfers between devices, swap(): return lax.ppermute(x, axis, [(i, i ^ d) for i in range(n)])  1.37 us
  transfers between devices with their start and end apart: 14, of which 3 were waited for; matrix products, arithmetic and copies ran while one was open for 0% of the time, Pallas kernels for 53%

profile of v6, /device:TPU:0, one launch (start us, length us, event | category | flops | bytes accessed | tf_op | source)
XLA Modules:
  0.0 63.6 jit_solution(3429803859078705943)
XLA Ops:
  0.6 0.8 %constant_dynamic-slice_fusion = bf16[64,512]{1,0:T(8,128)(2,1)S(1)} fusion(bf16[1024,512]{1,0:T(8,128)(2,1)} %c_hbm.1, s32[]{:T(128)S(6)} %select_n.12), kind=kLoop, calls=%fused_computation.1 | loop fusion | bytes 131076 | tf_op jit(solution)/shard_map/dynamic_slice | solution.py:413
  1.5 7.0 %collective-permute-start.2 = (bf16[64,512]{1,0:T(8,128)(2,1)S(1)}, bf16[64,512]{1,0:T(8,128)(2,1)S(1)}, u32[]{:S(2)}, u32[]{:S(2)}) collective-permute-start(bf16[64,512]{1,0:T(8,128)(2,1)S(1)} %constant_dynamic-slice_fusion), channel_id=1, source_target_pairs={{0,3},{4,7},{8,11},{12,15},{16,19},{20,23},{24,27},{28,31}} | collective-permute-start | bytes 196616 | tf_op jit(solution)/shard_map/ppermute | solution.py:414
  8.5 1.3 %collective-permute-start.1 = (bf16[64,512]{1,0:T(8,128)(2,1)S(1)}, bf16[64,512]{1,0:T(8,128)(2,1)S(1)}, u32[]{:S(2)}, u32[]{:S(2)}) collective-permute-start(bf16[64,512]{1,0:T(8,128)(2,1)S(1)} %constant_dynamic-slice_fusion), channel_id=1, source_target_pairs={{0,2},{4,6},{8,10},{12,14},{16,18},{20,22},{24,26},{28,30}} | collective-permute-start | bytes 196616 | tf_op jit(solution)/shard_map/ppermute | solution.py:414
  9.8 1.3 %collective-permute-start = (bf16[64,512]{1,0:T(8,128)(2,1)S(1)}, bf16[64,512]{1,0:T(8,128)(2,1)S(1)}, u32[]{:S(2)}, u32[]{:S(2)}) collective-permute-start(bf16[64,512]{1,0:T(8,128)(2,1)S(1)} %constant_dynamic-slice_fusion), channel_id=1, source_target_pairs={{0,1},{4,5},{8,9},{12,13},{16,17},{20,21},{24,25},{28,29}} | collective-permute-start | bytes 196616 | tf_op jit(solution)/shard_map/ppermute | solution.py:414
  11.1 1.9 %load.1 = (bf16[1024,512]{1,0:T(8,128)(2,1)S(1)}, bf16[2048,512]{1,0:T(8,128)(2,1)S(1)}) custom-call(bf16[1024,512]{1,0:T(8,128)(2,1)} %c_hbm.1, bf16[2048,512]{1,0:T(8,128)(2,1)} %s_hbm.1), custom_call_target="tpu_custom_call" | custom-call | tf_op jit(solution)/shard_map/load/pallas_call | solution.py:246
  13.0 0.0 collective-permute-done.2
  13.0 0.0 collective-permute-done.1
  13.0 0.0 collective-permute-done
  13.0 0.9 %add_select_fusion.refs_0_ = bf16[64,512]{1,0:T(8,128)(2,1)S(1)} fusion(bf16[64,512]{1,0:T(8,128)(2,1)S(1)} %collective-permute-done.2, bf16[64,512]{1,0:T(8,128)(2,1)S(1)} %collective-permute-done, bf16[64,512]{1,0:T(8,128)(2,1)S(1)} %collective-permute-done.1, pred[]{:T(512)S(6)} %eq.3, bf16[1024,512]{1,0:T(8,128)(2,1)} %c_hbm.1, s32[]{:T(128)S(6)} %select_n.12), kind=kLoop, calls=%fused_computation | loop fusion | flops 229376 | bytes 327685 | tf_op jit(solution)/shard_map/jit(_where)/select_n | solution.py:419
  13.9 1.6 %collective-permute-start.9 = (bf16[64,512]{1,0:T(8,128)(2,1)S(1)}, bf16[64,512]{1,0:T(8,128)(2,1)S(1)}, u32[]{:S(2)}, u32[]{:S(2)}) collective-permute-start(bf16[64,512]{1,0:T(8,128)(2,1)S(1)} %add_select_fusion.refs_0_), channel_id=1, source_target_pairs={{0,28},{4,24},{8,20},{12,16},{16,12},{20,8},{24,4},{28,0},{1,29},{... | collective-permute-start | bytes 196616 | tf_op jit(solution)/shard_map/ppermute | solution.py:406
  15.6 0.9 %collective-permute-start.8 = (bf16[64,512]{1,0:T(8,128)(2,1)S(1)}, bf16[64,512]{1,0:T(8,128)(2,1)S(1)}, u32[]{:S(2)}, u32[]{:S(2)}) collective-permute-start(bf16[64,512]{1,0:T(8,128)(2,1)S(1)} %add_select_fusion.refs_0_), channel_id=1, source_target_pairs={{0,24},{4,28},{8,16},{12,20},{16,8},{20,12},{24,0},{28,4},{1,25},{... | collective-permute-start | bytes 196616 | tf_op jit(solution)/shard_map/ppermute | solution.py:406
  16.5 1.4 %collective-permute-start.7 = (bf16[64,512]{1,0:T(8,128)(2,1)S(1)}, bf16[64,512]{1,0:T(8,128)(2,1)S(1)}, u32[]{:S(2)}, u32[]{:S(2)}) collective-permute-start(bf16[64,512]{1,0:T(8,128)(2,1)S(1)} %add_select_fusion.refs_0_), channel_id=1, source_target_pairs={{0,20},{4,16},{8,28},{12,24},{16,4},{20,0},{24,12},{28,8},{1,21},{... | collective-permute-start | bytes 196616 | tf_op jit(solution)/shard_map/ppermute | solution.py:406
  17.9 0.5 collective-permute-start.6
  18.4 0.7 %collective-permute-start.5 = (bf16[64,512]{1,0:T(8,128)(2,1)S(1)}, bf16[64,512]{1,0:T(8,128)(2,1)S(1)}, u32[]{:S(2)}, u32[]{:S(2)}) collective-permute-start(bf16[64,512]{1,0:T(8,128)(2,1)S(1)} %add_select_fusion.refs_0_), channel_id=1, source_target_pairs={{0,12},{4,8},{8,4},{12,0},{16,28},{20,24},{24,20},{28,16},{1,13},{... | collective-permute-start | bytes 196616 | tf_op jit(solution)/shard_map/ppermute | solution.py:406
  19.1 0.1 collective-permute-done.9.refs_7_
  19.2 1.3 %collective-permute-start.4 = (bf16[64,512]{1,0:T(8,128)(2,1)S(1)}, bf16[64,512]{1,0:T(8,128)(2,1)S(1)}, u32[]{:S(2)}, u32[]{:S(2)}) collective-permute-start(bf16[64,512]{1,0:T(8,128)(2,1)S(1)} %add_select_fusion.refs_0_), channel_id=1, source_target_pairs={{0,8},{4,12},{8,0},{12,4},{16,24},{20,28},{24,16},{28,20},{1,9},{5... | collective-permute-start | bytes 196616 | tf_op jit(solution)/shard_map/ppermute | solution.py:406
  20.5 1.0 %collective-permute-done.8.refs_6_ = bf16[64,512]{1,0:T(8,128)(2,1)S(1)} collective-permute-done((bf16[64,512]{1,0:T(8,128)(2,1)S(1)}, bf16[64,512]{1,0:T(8,128)(2,1)S(1)}, u32[]{:S(2)}, u32[]{:S(2)}) %collective-permute-start.8) | collective-permute-done | bytes 65568 | tf_op jit(solution)/shard_map/ppermute | solution.py:406
  21.5 0.1 collective-permute-start.3
  21.6 4.5 %kern_own.1 = (bf16[1024,2048]{1,0:T(8,128)(2,1)S(1)}, f32[2048,128]{1,0:T(8,128)S(1)}, bf16[128,512]{1,0:T(8,128)(2,1)S(1)}) custom-call(s32[1]{0:T(128)} %bitcast.me_ref, bf16[1024,512]{1,0:T(8,128)(2,1)S(1)} %get-tuple-element.35.c_ref, bf16[2048,512]{1,0:T(8,128)(2,1)S(1)} %get-tuple-element.36.s_ref.refs_9_), custom_call_target="tpu_custom_call" | custom-call | tf_op jit(solution)/shard_map/kern_own/pallas_call | solution.py:341
  26.1 0.0 collective-permute-done.7.refs_5_
  26.1 0.0 collective-permute-done.6.refs_4_
  26.1 0.0 collective-permute-done.5.refs_3_
  26.1 0.0 collective-permute-done.4.refs_2_
  26.1 0.0 collective-permute-done.3.refs_1_
  26.1 5.3 %gram.1 = (bf16[512,512]{1,0:T(8,128)(2,1)S(1)}, f32[4,128,512]{2,1,0:T(8,128)}, f32[128,512]{1,0:T(8,128)S(1)}, f32[128,512]{1,0:T(8,128)S(1)}, f32[128,512]{1,0:T(8,128)S(1)}, /*index=5*/f32[128,512]{1,0:T(8,128)S(1)}) custom-call(s32[1]{0:T(128)} %bitcast.me_ref, bf16[64,512]{1,0:T(8,128)(2,1)S(1)} %add_select_fusion.refs_0_, ...), custom_call_target="tpu_custom_call" | custom-call | tf_op jit(solution)/shard_map/gram/pallas_call | solution.py:383
  31.4 0.5 collective-permute-start.10
  31.8 2.3 %kern_center.1 = (f32[4,5,128,128]{3,2,1,0:T(8,128)S(1)}, f32[4,4,128,128]{3,2,1,0:T(8,128)S(1)}) custom-call(s32[1]{0:T(128)} %bitcast.1.off_ref, bf16[512,512]{1,0:T(8,128)(2,1)S(1)} %get-tuple-element.40.panel_ref, bf16[128,512]{1,0:T(8,128)(2,1)S(1)} %get-tuple-element.41.own_ref), custom_call_target="tpu_custom_call" | custom-call | tf_op jit(solution)/shard_map/kern_center/pallas_call | solution.py:119
  34.1 0.2 collective-permute-done.10.other_ref
  34.3 0.1 pair_sum.1
  34.5 0.6 collective-permute-start.11
  35.1 1.2 %collective-permute-start.12 = (f32[128,512]{1,0:T(8,128)S(1)}, f32[128,512]{1,0:T(8,128)S(1)}, u32[]{:S(2)}, u32[]{:S(2)}) collective-permute-start(f32[128,512]{1,0:T(8,128)S(1)} %get-tuple-element.51), channel_id=1, source_target_pairs={{0,16},{4,20},{8,24},{12,28},{16,0},{20,4},{24,8},{28,12},{1,17},{... | collective-permute-start | bytes 786440 | tf_op jit(solution)/shard_map/ppermute | solution.py:406
  36.2 1.8 %collective-permute-start.13 = (f32[128,512]{1,0:T(8,128)S(1)}, f32[128,512]{1,0:T(8,128)S(1)}, u32[]{:S(2)}, u32[]{:S(2)}) collective-permute-start(f32[128,512]{1,0:T(8,128)S(1)} %get-tuple-element.52), channel_id=1, source_target_pairs={{0,24},{4,28},{8,16},{12,20},{16,8},{20,12},{24,0},{28,4},{1,25},{... | collective-permute-start | bytes 786440 | tf_op jit(solution)/shard_map/ppermute | solution.py:406
  38.0 24.9 %chol.1 = (f32[128,512]{1,0:T(8,128)}, f32[512,512]{1,0:T(8,128)}) custom-call(f32[4,5,128,128]{3,2,1,0:T(8,128)S(1)} %get-tuple-element.53.ain_ref, f32[4,4,128,128]{3,2,1,0:T(8,128)S(1)} %get-tuple-element.54.sin_ref), custom_call_target="tpu_custom_call" | custom-call | tf_op jit(solution)/shard_map/chol/pallas_call | solution.py:210
  62.9 0.0 collective-permute-done.11.refs_1_
  62.9 0.0 collective-permute-done.12.refs_2_
  62.9 0.0 collective-permute-done.13.refs_3_
  62.9 0.8 %gram_sum.1 = f32[128,512]{1,0:T(8,128)} custom-call(f32[128,512]{1,0:T(8,128)S(1)} %get-tuple-element.49.refs_0_, f32[128,512]{1,0:T(8,128)S(1)} %collective-permute-done.11.refs_1_, f32[128,512]{1,0:T(8,128)S(1)} %collective-permute-done.12.refs_2_, f32[128,512]{1,0:T(8,128)S(1)} %collective-permute-done.13.refs_3_), custom_call_target="tpu_custom_call" | custom-call | tf_op jit(solution)/shard_map/gram_sum/pallas_call | solution.py:284
Async XLA Ops:
  1.5 11.5 %collective-permute-start.2 = (bf16[64,512]{1,0:T(8,128)(2,1)S(1)}, bf16[64,512]{1,0:T(8,128)(2,1)S(1)}, u32[]{:S(2)}, u32[]{:S(2)}) collective-permute-start(bf16[64,512]{1,0:T(8,128)(2,1)S(1)} %constant_dynamic-slice_fusion), channel_id=1, source_target_pairs={{0,3},{4,7},{8,11},{12,15},{16,19},{20,23},{24,27},{28,31}} | collective-permute-start | bytes 196616 | tf_op jit(solution)/shard_map/ppermute | solution.py:414
  8.5 4.5 %collective-permute-start.1 = (bf16[64,512]{1,0:T(8,128)(2,1)S(1)}, bf16[64,512]{1,0:T(8,128)(2,1)S(1)}, u32[]{:S(2)}, u32[]{:S(2)}) collective-permute-start(bf16[64,512]{1,0:T(8,128)(2,1)S(1)} %constant_dynamic-slice_fusion), channel_id=1, source_target_pairs={{0,2},{4,6},{8,10},{12,14},{16,18},{20,22},{24,26},{28,30}} | collective-permute-start | bytes 196616 | tf_op jit(solution)/shard_map/ppermute | solution.py:414
  9.8 3.3 %collective-permute-start = (bf16[64,512]{1,0:T(8,128)(2,1)S(1)}, bf16[64,512]{1,0:T(8,128)(2,1)S(1)}, u32[]{:S(2)}, u32[]{:S(2)}) collective-permute-start(bf16[64,512]{1,0:T(8,128)(2,1)S(1)} %constant_dynamic-slice_fusion), channel_id=1, source_target_pairs={{0,1},{4,5},{8,9},{12,13},{16,17},{20,21},{24,25},{28,29}} | collective-permute-start | bytes 196616 | tf_op jit(solution)/shard_map/ppermute | solution.py:414
  13.9 5.3 %collective-permute-start.9 = (bf16[64,512]{1,0:T(8,128)(2,1)S(1)}, bf16[64,512]{1,0:T(8,128)(2,1)S(1)}, u32[]{:S(2)}, u32[]{:S(2)}) collective-permute-start(bf16[64,512]{1,0:T(8,128)(2,1)S(1)} %add_select_fusion.refs_0_), channel_id=1, source_target_pairs={{0,28},{4,24},{8,20},{12,16},{16,12},{20,8},{24,4},{28,0},{1,29},{... | collective-permute-start | bytes 196616 | tf_op jit(solution)/shard_map/ppermute | solution.py:406
  15.6 6.0 %collective-permute-start.8 = (bf16[64,512]{1,0:T(8,128)(2,1)S(1)}, bf16[64,512]{1,0:T(8,128)(2,1)S(1)}, u32[]{:S(2)}, u32[]{:S(2)}) collective-permute-start(bf16[64,512]{1,0:T(8,128)(2,1)S(1)} %add_select_fusion.refs_0_), channel_id=1, source_target_pairs={{0,24},{4,28},{8,16},{12,20},{16,8},{20,12},{24,0},{28,4},{1,25},{... | collective-permute-start | bytes 196616 | tf_op jit(solution)/shard_map/ppermute | solution.py:406
  16.5 9.6 %collective-permute-start.7 = (bf16[64,512]{1,0:T(8,128)(2,1)S(1)}, bf16[64,512]{1,0:T(8,128)(2,1)S(1)}, u32[]{:S(2)}, u32[]{:S(2)}) collective-permute-start(bf16[64,512]{1,0:T(8,128)(2,1)S(1)} %add_select_fusion.refs_0_), channel_id=1, source_target_pairs={{0,20},{4,16},{8,28},{12,24},{16,4},{20,0},{24,12},{28,8},{1,21},{... | collective-permute-start | bytes 196616 | tf_op jit(solution)/shard_map/ppermute | solution.py:406
  17.9 8.2 %collective-permute-start.6 = (bf16[64,512]{1,0:T(8,128)(2,1)S(1)}, bf16[64,512]{1,0:T(8,128)(2,1)S(1)}, u32[]{:S(2)}, u32[]{:S(2)}) collective-permute-start(bf16[64,512]{1,0:T(8,128)(2,1)S(1)} %add_select_fusion.refs_0_), channel_id=1, source_target_pairs={{0,16},{4,20},{8,24},{12,28},{16,0},{20,4},{24,8},{28,12},{1,17},{... | collective-permute-start | bytes 196616 | tf_op jit(solution)/shard_map/ppermute | solution.py:406
  18.4 7.7 %collective-permute-start.5 = (bf16[64,512]{1,0:T(8,128)(2,1)S(1)}, bf16[64,512]{1,0:T(8,128)(2,1)S(1)}, u32[]{:S(2)}, u32[]{:S(2)}) collective-permute-start(bf16[64,512]{1,0:T(8,128)(2,1)S(1)} %add_select_fusion.refs_0_), channel_id=1, source_target_pairs={{0,12},{4,8},{8,4},{12,0},{16,28},{20,24},{24,20},{28,16},{1,13},{... | collective-permute-start | bytes 196616 | tf_op jit(solution)/shard_map/ppermute | solution.py:406
  19.2 7.0 %collective-permute-start.4 = (bf16[64,512]{1,0:T(8,128)(2,1)S(1)}, bf16[64,512]{1,0:T(8,128)(2,1)S(1)}, u32[]{:S(2)}, u32[]{:S(2)}) collective-permute-start(bf16[64,512]{1,0:T(8,128)(2,1)S(1)} %add_select_fusion.refs_0_), channel_id=1, source_target_pairs={{0,8},{4,12},{8,0},{12,4},{16,24},{20,28},{24,16},{28,20},{1,9},{5... | collective-permute-start | bytes 196616 | tf_op jit(solution)/shard_map/ppermute | solution.py:406
  21.5 4.6 %collective-permute-start.3 = (bf16[64,512]{1,0:T(8,128)(2,1)S(1)}, bf16[64,512]{1,0:T(8,128)(2,1)S(1)}, u32[]{:S(2)}, u32[]{:S(2)}) collective-permute-start(bf16[64,512]{1,0:T(8,128)(2,1)S(1)} %add_select_fusion.refs_0_), channel_id=1, source_target_pairs={{0,4},{4,0},{8,12},{12,8},{16,20},{20,16},{24,28},{28,24},{1,5},{5... | collective-permute-start | bytes 196616 | tf_op jit(solution)/shard_map/ppermute | solution.py:406
  31.4 2.9 %collective-permute-start.10 = (f32[4,128,512]{2,1,0:T(8,128)}, f32[4,128,512]{2,1,0:T(8,128)S(1)}, u32[]{:S(2)}, u32[]{:S(2)}) collective-permute-start(f32[4,128,512]{2,1,0:T(8,128)} %get-tuple-element.39), channel_id=1, source_target_pairs={{0,4},{4,0},{8,12},{12,8},{16,20},{20,16},{24,28},{28,24},{1,5},{5... | collective-permute-start | bytes 3145736 | tf_op jit(solution)/shard_map/ppermute | solution.py:406
  34.5 28.4 %collective-permute-start.11 = (f32[128,512]{1,0:T(8,128)S(1)}, f32[128,512]{1,0:T(8,128)S(1)}, u32[]{:S(2)}, u32[]{:S(2)}) collective-permute-start(f32[128,512]{1,0:T(8,128)S(1)} %get-tuple-element.50), channel_id=1, source_target_pairs={{0,8},{4,12},{8,0},{12,4},{16,24},{20,28},{24,16},{28,20},{1,9},{5... | collective-permute-start | bytes 786440 | tf_op jit(solution)/shard_map/ppermute | solution.py:406
  35.1 27.8 %collective-permute-start.12 = (f32[128,512]{1,0:T(8,128)S(1)}, f32[128,512]{1,0:T(8,128)S(1)}, u32[]{:S(2)}, u32[]{:S(2)}) collective-permute-start(f32[128,512]{1,0:T(8,128)S(1)} %get-tuple-element.51), channel_id=1, source_target_pairs={{0,16},{4,20},{8,24},{12,28},{16,0},{20,4},{24,8},{28,12},{1,17},{... | collective-permute-start | bytes 786440 | tf_op jit(solution)/shard_map/ppermute | solution.py:406
  36.2 26.7 %collective-permute-start.13 = (f32[128,512]{1,0:T(8,128)S(1)}, f32[128,512]{1,0:T(8,128)S(1)}, u32[]{:S(2)}, u32[]{:S(2)}) collective-permute-start(f32[128,512]{1,0:T(8,128)S(1)} %get-tuple-element.52), channel_id=1, source_target_pairs={{0,24},{4,28},{8,16},{12,20},{16,8},{20,12},{24,0},{28,4},{1,25},{... | collective-permute-start | bytes 786440 | tf_op jit(solution)/shard_map/ppermute | solution.py:406

commit v7 on v6

--- a/solution.py
+++ b/solution.py
@@ -142,14 +142,15 @@
     def step(K,low):
         Kp=jnp.where(K==0,nb,K-1)
         tl=trail(a_ref,u_ref,l_ref,Kp,nb,nj); tc=trail(s_ref,v_ref,h_ref,Kp,nb,nb)
-        def rows():
+        def row0():
             put(ms_ref[Kp],ks_ref[Kp],[a_ref[Kp,j] for j in range(nj)],Kp,nb,u_ref,l_ref)
+        def row1():
             put(mc_ref[Kp],kc_ref[Kp],[s_ref[Kp,j] for j in range(nb)],Kp,nb,v_ref,h_ref)
         def run(fs):
             for f in fs: f()
         half=len(tl)//2+1
         factor128([(r0,w0,k0,m0),(r1,w1,k1,m1)],
-            [rows,functools.partial(run,tl[:half]+tc[:half-1]),functools.partial(run,tl[half:]+tc[half-1:])])
+            [row0,functools.partial(run,[row1]+tl[:half]),functools.partial(run,tl[half:]+tc)])
         K1=jnp.minimum(K+1,nb-1)
         x0=mmul(m0[...],a_ref[K,K1]); x1=mmul(m1[...],s_ref[K,K1])
         r0[...]=a_ref[K1,K1]-mmul(x0.T,x0)

time: 63.9 us -> 63.8 us (level)
  no operation moved by 1% of the time
where the time goes in v7:
time: 63.8 us; the launch traced here: 63.6 us
  Pallas kernels  39.6 us (62%)
  starting transfers between devices  20.1 us (32%)
  waiting for transfers between devices  1.42 us (2%)
  other arithmetic  0.87 us (1%)
  local copies, waits for them, and re-layouts  0.85 us (1%)
  between operations  0.76 us (1%)
    pallas_call x1, Pallas kernels, factor_kernel(): pl.pallas_call(body, out_shape=(jax.ShapeDtypeStruct((no * B, nb * B), f3...  24.8 us
    ppermute x11, starting transfers between devices, swap(): return lax.ppermute(x, axis, [(i, i ^ d) for i in range(n)])  10.5 us
    ppermute x3, starting transfers between devices, panel_pieces(): got = [lax.ppermute(chunk, 'ctr', [(0, d)]) for d in range(1, ctrs)]  9.56 us
    pallas_call x1, Pallas kernels, gram_kernel(): pl.pallas_call(functools.partial(gram_body, samps=samps, tile=tile), in_s...  5.25 us
    pallas_call x1, Pallas kernels, own_kernel(): pl.pallas_call(functools.partial(own_body, row_dev=row_dev), in_specs=[pl...  4.51 us
    pallas_call x1, Pallas kernels, init_kernel(): pl.pallas_call(functools.partial(init_body, own=ro), out_shape=(V(nb, nb...  2.27 us
    pallas_call x1, Pallas kernels, load_kernel(): pl.pallas_call(functools.partial(load_body, parts=parts), in_specs=[outsi...  1.89 us
    ppermute x11, waiting for transfers between devices, swap(): return lax.ppermute(x, axis, [(i, i ^ d) for i in range(n)])  1.37 us
  transfers between devices with their start and end apart: 14, of which 3 were waited for; matrix products, arithmetic and copies ran while one was open for 0% of the time, Pallas kernels for 53%

profile of v7, /device:TPU:0, one launch (start us, length us, event | category | flops | bytes accessed | tf_op | source)
XLA Modules:
  0.0 63.6 jit_solution(10292631101400994133)
XLA Ops:
  0.6 0.8 %constant_dynamic-slice_fusion = bf16[64,512]{1,0:T(8,128)(2,1)S(1)} fusion(bf16[1024,512]{1,0:T(8,128)(2,1)} %c_hbm.1, s32[]{:T(128)S(6)} %select_n.12), kind=kLoop, calls=%fused_computation.1 | loop fusion | bytes 131076 | tf_op jit(solution)/shard_map/dynamic_slice | solution.py:414
  1.5 7.0 %collective-permute-start.2 = (bf16[64,512]{1,0:T(8,128)(2,1)S(1)}, bf16[64,512]{1,0:T(8,128)(2,1)S(1)}, u32[]{:S(2)}, u32[]{:S(2)}) collective-permute-start(bf16[64,512]{1,0:T(8,128)(2,1)S(1)} %constant_dynamic-slice_fusion), channel_id=1, source_target_pairs={{0,3},{4,7},{8,11},{12,15},{16,19},{20,23},{24,27},{28,31}} | collective-permute-start | bytes 196616 | tf_op jit(solution)/shard_map/ppermute | solution.py:415
  8.5 1.3 %collective-permute-start.1 = (bf16[64,512]{1,0:T(8,128)(2,1)S(1)}, bf16[64,512]{1,0:T(8,128)(2,1)S(1)}, u32[]{:S(2)}, u32[]{:S(2)}) collective-permute-start(bf16[64,512]{1,0:T(8,128)(2,1)S(1)} %constant_dynamic-slice_fusion), channel_id=1, source_target_pairs={{0,2},{4,6},{8,10},{12,14},{16,18},{20,22},{24,26},{28,30}} | collective-permute-start | bytes 196616 | tf_op jit(solution)/shard_map/ppermute | solution.py:415
  9.8 1.3 %collective-permute-start = (bf16[64,512]{1,0:T(8,128)(2,1)S(1)}, bf16[64,512]{1,0:T(8,128)(2,1)S(1)}, u32[]{:S(2)}, u32[]{:S(2)}) collective-permute-start(bf16[64,512]{1,0:T(8,128)(2,1)S(1)} %constant_dynamic-slice_fusion), channel_id=1, source_target_pairs={{0,1},{4,5},{8,9},{12,13},{16,17},{20,21},{24,25},{28,29}} | collective-permute-start | bytes 196616 | tf_op jit(solution)/shard_map/ppermute | solution.py:415
  11.1 1.9 %load.1 = (bf16[1024,512]{1,0:T(8,128)(2,1)S(1)}, bf16[2048,512]{1,0:T(8,128)(2,1)S(1)}) custom-call(bf16[1024,512]{1,0:T(8,128)(2,1)} %c_hbm.1, bf16[2048,512]{1,0:T(8,128)(2,1)} %s_hbm.1), custom_call_target="tpu_custom_call" | custom-call | tf_op jit(solution)/shard_map/load/pallas_call | solution.py:247
  13.0 0.0 collective-permute-done.2
  13.0 0.0 collective-permute-done.1
  13.0 0.0 collective-permute-done
  13.0 0.9 %add_select_fusion.refs_0_ = bf16[64,512]{1,0:T(8,128)(2,1)S(1)} fusion(bf16[64,512]{1,0:T(8,128)(2,1)S(1)} %collective-permute-done.2, bf16[64,512]{1,0:T(8,128)(2,1)S(1)} %collective-permute-done, bf16[64,512]{1,0:T(8,128)(2,1)S(1)} %collective-permute-done.1, pred[]{:T(512)S(6)} %eq.3, bf16[1024,512]{1,0:T(8,128)(2,1)} %c_hbm.1, s32[]{:T(128)S(6)} %select_n.12), kind=kLoop, calls=%fused_computation | loop fusion | flops 229376 | bytes 327685 | tf_op jit(solution)/shard_map/jit(_where)/select_n | solution.py:420
  13.9 1.6 %collective-permute-start.9 = (bf16[64,512]{1,0:T(8,128)(2,1)S(1)}, bf16[64,512]{1,0:T(8,128)(2,1)S(1)}, u32[]{:S(2)}, u32[]{:S(2)}) collective-permute-start(bf16[64,512]{1,0:T(8,128)(2,1)S(1)} %add_select_fusion.refs_0_), channel_id=1, source_target_pairs={{0,28},{4,24},{8,20},{12,16},{16,12},{20,8},{24,4},{28,0},{1,29},{... | collective-permute-start | bytes 196616 | tf_op jit(solution)/shard_map/ppermute | solution.py:407
  15.6 0.9 %collective-permute-start.8 = (bf16[64,512]{1,0:T(8,128)(2,1)S(1)}, bf16[64,512]{1,0:T(8,128)(2,1)S(1)}, u32[]{:S(2)}, u32[]{:S(2)}) collective-permute-start(bf16[64,512]{1,0:T(8,128)(2,1)S(1)} %add_select_fusion.refs_0_), channel_id=1, source_target_pairs={{0,24},{4,28},{8,16},{12,20},{16,8},{20,12},{24,0},{28,4},{1,25},{... | collective-permute-start | bytes 196616 | tf_op jit(solution)/shard_map/ppermute | solution.py:407
  16.5 1.4 %collective-permute-start.7 = (bf16[64,512]{1,0:T(8,128)(2,1)S(1)}, bf16[64,512]{1,0:T(8,128)(2,1)S(1)}, u32[]{:S(2)}, u32[]{:S(2)}) collective-permute-start(bf16[64,512]{1,0:T(8,128)(2,1)S(1)} %add_select_fusion.refs_0_), channel_id=1, source_target_pairs={{0,20},{4,16},{8,28},{12,24},{16,4},{20,0},{24,12},{28,8},{1,21},{... | collective-permute-start | bytes 196616 | tf_op jit(solution)/shard_map/ppermute | solution.py:407
  17.9 0.5 collective-permute-start.6
  18.4 0.7 %collective-permute-start.5 = (bf16[64,512]{1,0:T(8,128)(2,1)S(1)}, bf16[64,512]{1,0:T(8,128)(2,1)S(1)}, u32[]{:S(2)}, u32[]{:S(2)}) collective-permute-start(bf16[64,512]{1,0:T(8,128)(2,1)S(1)} %add_select_fusion.refs_0_), channel_id=1, source_target_pairs={{0,12},{4,8},{8,4},{12,0},{16,28},{20,24},{24,20},{28,16},{1,13},{... | collective-permute-start | bytes 196616 | tf_op jit(solution)/shard_map/ppermute | solution.py:407
  19.1 0.1 collective-permute-done.9.refs_7_
  19.2 1.3 %collective-permute-start.4 = (bf16[64,512]{1,0:T(8,128)(2,1)S(1)}, bf16[64,512]{1,0:T(8,128)(2,1)S(1)}, u32[]{:S(2)}, u32[]{:S(2)}) collective-permute-start(bf16[64,512]{1,0:T(8,128)(2,1)S(1)} %add_select_fusion.refs_0_), channel_id=1, source_target_pairs={{0,8},{4,12},{8,0},{12,4},{16,24},{20,28},{24,16},{28,20},{1,9},{5... | collective-permute-start | bytes 196616 | tf_op jit(solution)/shard_map/ppermute | solution.py:407
  20.5 1.0 %collective-permute-done.8.refs_6_ = bf16[64,512]{1,0:T(8,128)(2,1)S(1)} collective-permute-done((bf16[64,512]{1,0:T(8,128)(2,1)S(1)}, bf16[64,512]{1,0:T(8,128)(2,1)S(1)}, u32[]{:S(2)}, u32[]{:S(2)}) %collective-permute-start.8) | collective-permute-done | bytes 65568 | tf_op jit(solution)/shard_map/ppermute | solution.py:407
  21.5 0.1 collective-permute-start.3
  21.6 4.5 %kern_own.1 = (bf16[1024,2048]{1,0:T(8,128)(2,1)S(1)}, f32[2048,128]{1,0:T(8,128)S(1)}, bf16[128,512]{1,0:T(8,128)(2,1)S(1)}) custom-call(s32[1]{0:T(128)} %bitcast.me_ref, bf16[1024,512]{1,0:T(8,128)(2,1)S(1)} %get-tuple-element.35.c_ref, bf16[2048,512]{1,0:T(8,128)(2,1)S(1)} %get-tuple-element.36.s_ref.refs_9_), custom_call_target="tpu_custom_call" | custom-call | tf_op jit(solution)/shard_map/kern_own/pallas_call | solution.py:342
  26.1 0.0 collective-permute-done.7.refs_5_
  26.1 0.0 collective-permute-done.6.refs_4_
  26.1 0.0 collective-permute-done.5.refs_3_
  26.1 0.0 collective-permute-done.4.refs_2_
  26.1 0.0 collective-permute-done.3.refs_1_
  26.1 5.3 %gram.1 = (bf16[512,512]{1,0:T(8,128)(2,1)S(1)}, f32[4,128,512]{2,1,0:T(8,128)}, f32[128,512]{1,0:T(8,128)S(1)}, f32[128,512]{1,0:T(8,128)S(1)}, f32[128,512]{1,0:T(8,128)S(1)}, /*index=5*/f32[128,512]{1,0:T(8,128)S(1)}) custom-call(s32[1]{0:T(128)} %bitcast.me_ref, bf16[64,512]{1,0:T(8,128)(2,1)S(1)} %add_select_fusion.refs_0_, ...), custom_call_target="tpu_custom_call" | custom-call | tf_op jit(solution)/shard_map/gram/pallas_call | solution.py:384
  31.4 0.5 collective-permute-start.10
  31.8 2.3 %kern_center.1 = (f32[4,5,128,128]{3,2,1,0:T(8,128)S(1)}, f32[4,4,128,128]{3,2,1,0:T(8,128)S(1)}) custom-call(s32[1]{0:T(128)} %bitcast.1.off_ref, bf16[512,512]{1,0:T(8,128)(2,1)S(1)} %get-tuple-element.40.panel_ref, bf16[128,512]{1,0:T(8,128)(2,1)S(1)} %get-tuple-element.41.own_ref), custom_call_target="tpu_custom_call" | custom-call | tf_op jit(solution)/shard_map/kern_center/pallas_call | solution.py:119
  34.1 0.2 collective-permute-done.10.other_ref
  34.3 0.1 pair_sum.1
  34.5 0.6 collective-permute-start.11
  35.1 1.2 %collective-permute-start.12 = (f32[128,512]{1,0:T(8,128)S(1)}, f32[128,512]{1,0:T(8,128)S(1)}, u32[]{:S(2)}, u32[]{:S(2)}) collective-permute-start(f32[128,512]{1,0:T(8,128)S(1)} %get-tuple-element.51), channel_id=1, source_target_pairs={{0,16},{4,20},{8,24},{12,28},{16,0},{20,4},{24,8},{28,12},{1,17},{... | collective-permute-start | bytes 786440 | tf_op jit(solution)/shard_map/ppermute | solution.py:407
  36.2 1.8 %collective-permute-start.13 = (f32[128,512]{1,0:T(8,128)S(1)}, f32[128,512]{1,0:T(8,128)S(1)}, u32[]{:S(2)}, u32[]{:S(2)}) collective-permute-start(f32[128,512]{1,0:T(8,128)S(1)} %get-tuple-element.52), channel_id=1, source_target_pairs={{0,24},{4,28},{8,16},{12,20},{16,8},{20,12},{24,0},{28,4},{1,25},{... | collective-permute-start | bytes 786440 | tf_op jit(solution)/shard_map/ppermute | solution.py:407
  38.0 24.8 %chol.1 = (f32[128,512]{1,0:T(8,128)}, f32[512,512]{1,0:T(8,128)}) custom-call(f32[4,5,128,128]{3,2,1,0:T(8,128)S(1)} %get-tuple-element.53.ain_ref, f32[4,4,128,128]{3,2,1,0:T(8,128)S(1)} %get-tuple-element.54.sin_ref), custom_call_target="tpu_custom_call" | custom-call | tf_op jit(solution)/shard_map/chol/pallas_call | solution.py:211
  62.8 0.0 collective-permute-done.11.refs_1_
  62.8 0.0 collective-permute-done.12.refs_2_
  62.8 0.0 collective-permute-done.13.refs_3_
  62.8 0.8 %gram_sum.1 = f32[128,512]{1,0:T(8,128)} custom-call(f32[128,512]{1,0:T(8,128)S(1)} %get-tuple-element.49.refs_0_, f32[128,512]{1,0:T(8,128)S(1)} %collective-permute-done.11.refs_1_, f32[128,512]{1,0:T(8,128)S(1)} %collective-permute-done.12.refs_2_, f32[128,512]{1,0:T(8,128)S(1)} %collective-permute-done.13.refs_3_), custom_call_target="tpu_custom_call" | custom-call | tf_op jit(solution)/shard_map/gram_sum/pallas_call | solution.py:285
Async XLA Ops:
  1.5 11.5 %collective-permute-start.2 = (bf16[64,512]{1,0:T(8,128)(2,1)S(1)}, bf16[64,512]{1,0:T(8,128)(2,1)S(1)}, u32[]{:S(2)}, u32[]{:S(2)}) collective-permute-start(bf16[64,512]{1,0:T(8,128)(2,1)S(1)} %constant_dynamic-slice_fusion), channel_id=1, source_target_pairs={{0,3},{4,7},{8,11},{12,15},{16,19},{20,23},{24,27},{28,31}} | collective-permute-start | bytes 196616 | tf_op jit(solution)/shard_map/ppermute | solution.py:415
  8.5 4.5 %collective-permute-start.1 = (bf16[64,512]{1,0:T(8,128)(2,1)S(1)}, bf16[64,512]{1,0:T(8,128)(2,1)S(1)}, u32[]{:S(2)}, u32[]{:S(2)}) collective-permute-start(bf16[64,512]{1,0:T(8,128)(2,1)S(1)} %constant_dynamic-slice_fusion), channel_id=1, source_target_pairs={{0,2},{4,6},{8,10},{12,14},{16,18},{20,22},{24,26},{28,30}} | collective-permute-start | bytes 196616 | tf_op jit(solution)/shard_map/ppermute | solution.py:415
  9.8 3.3 %collective-permute-start = (bf16[64,512]{1,0:T(8,128)(2,1)S(1)}, bf16[64,512]{1,0:T(8,128)(2,1)S(1)}, u32[]{:S(2)}, u32[]{:S(2)}) collective-permute-start(bf16[64,512]{1,0:T(8,128)(2,1)S(1)} %constant_dynamic-slice_fusion), channel_id=1, source_target_pairs={{0,1},{4,5},{8,9},{12,13},{16,17},{20,21},{24,25},{28,29}} | collective-permute-start | bytes 196616 | tf_op jit(solution)/shard_map/ppermute | solution.py:415
  13.9 5.3 %collective-permute-start.9 = (bf16[64,512]{1,0:T(8,128)(2,1)S(1)}, bf16[64,512]{1,0:T(8,128)(2,1)S(1)}, u32[]{:S(2)}, u32[]{:S(2)}) collective-permute-start(bf16[64,512]{1,0:T(8,128)(2,1)S(1)} %add_select_fusion.refs_0_), channel_id=1, source_target_pairs={{0,28},{4,24},{8,20},{12,16},{16,12},{20,8},{24,4},{28,0},{1,29},{... | collective-permute-start | bytes 196616 | tf_op jit(solution)/shard_map/ppermute | solution.py:407
  15.6 6.0 %collective-permute-start.8 = (bf16[64,512]{1,0:T(8,128)(2,1)S(1)}, bf16[64,512]{1,0:T(8,128)(2,1)S(1)}, u32[]{:S(2)}, u32[]{:S(2)}) collective-permute-start(bf16[64,512]{1,0:T(8,128)(2,1)S(1)} %add_select_fusion.refs_0_), channel_id=1, source_target_pairs={{0,24},{4,28},{8,16},{12,20},{16,8},{20,12},{24,0},{28,4},{1,25},{... | collective-permute-start | bytes 196616 | tf_op jit(solution)/shard_map/ppermute | solution.py:407
  16.5 9.6 %collective-permute-start.7 = (bf16[64,512]{1,0:T(8,128)(2,1)S(1)}, bf16[64,512]{1,0:T(8,128)(2,1)S(1)}, u32[]{:S(2)}, u32[]{:S(2)}) collective-permute-start(bf16[64,512]{1,0:T(8,128)(2,1)S(1)} %add_select_fusion.refs_0_), channel_id=1, source_target_pairs={{0,20},{4,16},{8,28},{12,24},{16,4},{20,0},{24,12},{28,8},{1,21},{... | collective-permute-start | bytes 196616 | tf_op jit(solution)/shard_map/ppermute | solution.py:407
  17.9 8.2 %collective-permute-start.6 = (bf16[64,512]{1,0:T(8,128)(2,1)S(1)}, bf16[64,512]{1,0:T(8,128)(2,1)S(1)}, u32[]{:S(2)}, u32[]{:S(2)}) collective-permute-start(bf16[64,512]{1,0:T(8,128)(2,1)S(1)} %add_select_fusion.refs_0_), channel_id=1, source_target_pairs={{0,16},{4,20},{8,24},{12,28},{16,0},{20,4},{24,8},{28,12},{1,17},{... | collective-permute-start | bytes 196616 | tf_op jit(solution)/shard_map/ppermute | solution.py:407
  18.4 7.7 %collective-permute-start.5 = (bf16[64,512]{1,0:T(8,128)(2,1)S(1)}, bf16[64,512]{1,0:T(8,128)(2,1)S(1)}, u32[]{:S(2)}, u32[]{:S(2)}) collective-permute-start(bf16[64,512]{1,0:T(8,128)(2,1)S(1)} %add_select_fusion.refs_0_), channel_id=1, source_target_pairs={{0,12},{4,8},{8,4},{12,0},{16,28},{20,24},{24,20},{28,16},{1,13},{... | collective-permute-start | bytes 196616 | tf_op jit(solution)/shard_map/ppermute | solution.py:407
  19.2 7.0 %collective-permute-start.4 = (bf16[64,512]{1,0:T(8,128)(2,1)S(1)}, bf16[64,512]{1,0:T(8,128)(2,1)S(1)}, u32[]{:S(2)}, u32[]{:S(2)}) collective-permute-start(bf16[64,512]{1,0:T(8,128)(2,1)S(1)} %add_select_fusion.refs_0_), channel_id=1, source_target_pairs={{0,8},{4,12},{8,0},{12,4},{16,24},{20,28},{24,16},{28,20},{1,9},{5... | collective-permute-start | bytes 196616 | tf_op jit(solution)/shard_map/ppermute | solution.py:407
  21.5 4.6 %collective-permute-start.3 = (bf16[64,512]{1,0:T(8,128)(2,1)S(1)}, bf16[64,512]{1,0:T(8,128)(2,1)S(1)}, u32[]{:S(2)}, u32[]{:S(2)}) collective-permute-start(bf16[64,512]{1,0:T(8,128)(2,1)S(1)} %add_select_fusion.refs_0_), channel_id=1, source_target_pairs={{0,4},{4,0},{8,12},{12,8},{16,20},{20,16},{24,28},{28,24},{1,5},{5... | collective-permute-start | bytes 196616 | tf_op jit(solution)/shard_map/ppermute | solution.py:407
  31.4 2.9 %collective-permute-start.10 = (f32[4,128,512]{2,1,0:T(8,128)}, f32[4,128,512]{2,1,0:T(8,128)S(1)}, u32[]{:S(2)}, u32[]{:S(2)}) collective-permute-start(f32[4,128,512]{2,1,0:T(8,128)} %get-tuple-element.39), channel_id=1, source_target_pairs={{0,4},{4,0},{8,12},{12,8},{16,20},{20,16},{24,28},{28,24},{1,5},{5... | collective-permute-start | bytes 3145736 | tf_op jit(solution)/shard_map/ppermute | solution.py:407
  34.5 28.3 %collective-permute-start.11 = (f32[128,512]{1,0:T(8,128)S(1)}, f32[128,512]{1,0:T(8,128)S(1)}, u32[]{:S(2)}, u32[]{:S(2)}) collective-permute-start(f32[128,512]{1,0:T(8,128)S(1)} %get-tuple-element.50), channel_id=1, source_target_pairs={{0,8},{4,12},{8,0},{12,4},{16,24},{20,28},{24,16},{28,20},{1,9},{5... | collective-permute-start | bytes 786440 | tf_op jit(solution)/shard_map/ppermute | solution.py:407
  35.1 27.7 %collective-permute-start.12 = (f32[128,512]{1,0:T(8,128)S(1)}, f32[128,512]{1,0:T(8,128)S(1)}, u32[]{:S(2)}, u32[]{:S(2)}) collective-permute-start(f32[128,512]{1,0:T(8,128)S(1)} %get-tuple-element.51), channel_id=1, source_target_pairs={{0,16},{4,20},{8,24},{12,28},{16,0},{20,4},{24,8},{28,12},{1,17},{... | collective-permute-start | bytes 786440 | tf_op jit(solution)/shard_map/ppermute | solution.py:407
  36.2 26.6 %collective-permute-start.13 = (f32[128,512]{1,0:T(8,128)S(1)}, f32[128,512]{1,0:T(8,128)S(1)}, u32[]{:S(2)}, u32[]{:S(2)}) collective-permute-start(f32[128,512]{1,0:T(8,128)S(1)} %get-tuple-element.52), channel_id=1, source_target_pairs={{0,24},{4,28},{8,16},{12,20},{16,8},{20,12},{24,0},{28,4},{1,25},{... | collective-permute-start | bytes 786440 | tf_op jit(solution)/shard_map/ppermute | solution.py:407
